TPU v7x, 512 devices: a whole 4x4x16 slice. The times are simulated.
512 devices in a mesh: mem: 128 (over x, z, core), rep: 4 (over y).
Axes of the slice: x: 4, y: 4, z: 16, core: 2. Of those that a mesh axis runs over, the one named last changes fastest.
Arguments:
- states: bfloat16 [2048, 384], P('rep'), may hold values from -6 to 6
- batch_index: int32 [2, 2048], P(None, 'rep'), may hold values from 0 to 511
- obs_pick: int32 [2, 128], replicated, may hold values from 0 to 383
- norm_gain: float32 [384], replicated, may hold values from 0.5 to 1.5
- w_in: bfloat16 [384, 1024], replicated, may hold values from -0.3125 to 0.3125
- b_in: float32 [1024], replicated, may hold values from -0.5 to 0.5
- member_params: bfloat16 [128, 393216], P('mem', 'rep'), may hold values from -6 to 6
- observed: bfloat16 [2, 2048, 128], P(None, 'rep'), may hold values from -6 to 6
- perturbation: bfloat16 [128, 2, 2048, 128], P('mem', None, 'rep'), may hold values from -6 to 6
- inv_sigma: float32 [2, 2048, 128], P(None, 'rep'), may hold values from 0.5 to 4
Outputs:
- updated_params: bfloat16 [128, 393216], P('mem', 'rep')
Inputs may be any that keep to these rules, and one draw needn't show every extreme that they name: `batch_index`: row number of a start state inside the block of 512 given states that belongs to its block of 512 batch rows. `obs_pick`: observed feature numbers; a number may repeat.
All inputs are finite; a program needn't handle non-finite values.
Results may differ from a plain program's by a relative error of at most 0.0056.
Values may be sent and summed in bfloat16 or wider, within the bound.
No kernel may reach another device: no remote copies, remote signals or barrier semaphores. Data moves between devices by JAX's collectives and lax.ppermute only.
A program may use at most 64 MiB of HBM per device.

v0:
```python
import jax
import jax.numpy as jnp
from jax import lax
from jax.sharding import PartitionSpec as P

EPS = 1e-06
DT = 0.5


def hidden_layer(state, norm_gain, w_in, b_in):
    normed = (
        state * lax.rsqrt(jnp.mean(state * state, axis=-1, keepdims=True) + EPS) * norm_gain
    ).astype(jnp.bfloat16)
    return jax.nn.gelu(jnp.dot(normed, w_in, preferred_element_type=jnp.float32) + b_in).astype(
        jnp.bfloat16
    )


def member_sums(pieces):
    weighted, misfit_w = pieces
    count = weighted.shape[0]
    gram_list = []
    innov_list = []
    for item_index in range(weighted.shape[1]):
        flat = weighted[:, item_index].reshape(count, -1).astype(jnp.float32)
        anomaly = (flat - jnp.mean(flat, axis=0)).astype(jnp.bfloat16)
        misfit_flat = misfit_w[:, item_index].reshape(count, -1)
        gram_list.append(
            lax.dot_general(
                anomaly, anomaly, (((1,), (1,)), ((), ())), preferred_element_type=jnp.float32
            )
        )
        innov_list.append(
            lax.dot_general(
                anomaly, misfit_flat, (((1,), (1,)), ((), ())), preferred_element_type=jnp.float32
            )
        )
    return (jnp.stack(gram_list, axis=0), jnp.stack(innov_list, axis=0))


def solve_columns(system, right_side):
    lower_factor = jnp.linalg.cholesky(system)
    halfway = lax.linalg.triangular_solve(lower_factor, right_side, left_side=True, lower=True)
    return lax.linalg.triangular_solve(
        lower_factor, halfway, left_side=True, lower=True, transpose_a=True
    )


def on_device(
    states,
    batch_index,
    obs_pick,
    norm_gain,
    w_in,
    b_in,
    member_params,
    observed,
    perturbation,
    inv_sigma,
):
    local_members = member_params.shape[0]
    width = w_in.shape[1]
    features = w_in.shape[0]
    step_count = batch_index.shape[0]
    picked = obs_pick.shape[1]
    whole_params = lax.all_gather(member_params, "rep", axis=1, tiled=True)
    weights = whole_params.reshape(local_members, width, features)
    step_scale = DT * width ** (-0.5)
    start_state = jnp.take(states, batch_index, axis=0).astype(jnp.float32)
    shared = hidden_layer(start_state, norm_gain, w_in, b_in)
    current = start_state[None] + step_scale * jnp.einsum(
        "kbh,jhs->jkbs", shared, weights, preferred_element_type=jnp.float32
    )
    layer = hidden_layer(current, norm_gain, w_in, b_in)
    current = current + step_scale * jnp.einsum(
        "jkbh,jhs->jkbs", layer, weights, preferred_element_type=jnp.float32
    )
    feature_ids = lax.broadcasted_iota(jnp.int32, (step_count, features, picked), 1)
    selector = (feature_ids == obs_pick[:, None, :]).astype(jnp.float32)
    predicted = jnp.einsum("jkbs,ksf->jkbf", current, selector, precision=lax.Precision.HIGHEST)
    weighted = (predicted * inv_sigma).astype(jnp.bfloat16)
    misfit_w = (
        observed.astype(jnp.float32) * inv_sigma
        + perturbation.astype(jnp.float32)
        - predicted * inv_sigma
    ).astype(jnp.bfloat16)
    misfit_local = jnp.sum(jnp.square(misfit_w.astype(jnp.float32)))
    gram_items, innov_items = member_sums(
        (
            lax.all_to_all(weighted, "mem", split_axis=2, concat_axis=0, tiled=True),
            lax.all_to_all(misfit_w, "mem", split_axis=2, concat_axis=0, tiled=True),
        )
    )
    gram_matrix = jnp.sum(gram_items, axis=0)
    innovation = jnp.sum(innov_items, axis=0)
    members = gram_matrix.shape[0]
    entries = members * step_count * batch_index.shape[1] * lax.axis_size("rep") * picked
    identity = jnp.eye(members, dtype=jnp.float32)
    gram_matrix, innovation, misfit_total = lax.psum(
        (gram_matrix, innovation, misfit_local), ("mem", "rep")
    )
    system = gram_matrix + (1.0 + misfit_total / entries) * (members - 1) * identity
    coefficients = solve_columns(system, innovation)
    param_block = lax.all_to_all(member_params, "mem", split_axis=1, concat_axis=0, tiled=True)
    params_f = param_block.astype(jnp.float32)
    spread = params_f - jnp.mean(params_f, axis=0)
    change = jnp.einsum("kj,kp->jp", coefficients, spread, precision=lax.Precision.HIGHEST)
    renewed = (params_f + change).astype(jnp.bfloat16)
    return lax.all_to_all(renewed, "mem", split_axis=0, concat_axis=1, tiled=True)


def solution(mesh):
    placed = (
        P("rep", None),
        P(None, "rep"),
        P(),
        P(),
        P(),
        P(),
        P("mem", "rep"),
        P(None, "rep", None),
        P("mem", None, "rep", None),
        P(None, "rep", None),
    )
    return jax.shard_map(
        on_device, mesh=mesh, in_specs=placed, out_specs=P("mem", "rep"), check_vma=False
    )
```

profile of v0, /device:TPU:1, one launch (start us, length us, event | category | flops | bytes accessed | tf_op | source)
XLA Modules:
  0.0 754.6 jit_solution(18304707724078509563)
XLA Ops:
  7.1 2.8 reduce.16
  9.9 0.7 reshape.213
  10.6 20.8 %all-to-all-start = ((bf16[128,2,384]{2,1,0:T(2,128)(2,1)}), bf16[128,2,384]{2,1,0:T(2,128)(2,1)}, u32[]{:S(2)}, u32[]{:S(2)}) async-start(bf16[128,2,384]{2,1,0:T(2,128)(2,1)} %reshape.213), calls=%async_computation | async-start | bytes 393216 | tf_op jit(solution)/shard_map/all_to_all | solution.py:104
  32.8 16.5 %all_gather.3 = bf16[1,393216]{1,0:T(2,128)(2,1)S(1)} all-gather(bf16[1,98304]{1,0:T(2,128)(2,1)S(1)} %copy-done.2), channel_id=1, replica_groups=mesh['mem'=128,'rep'=4] {'rep'}, dimensions={1}, use_global_device_ids=true | all-gather | bytes 983040 | tf_op jit(solution)/shard_map/all_gather | solution.py:66
  49.3 16.3 %reduce.14 = bf16[393216]{0:T(1024)(128)(2,1)S(1)} reduce(bf16[1,393216]{1,0:T(2,128)(2,1)S(1)} %all_gather.3, bf16[]{:T(256)} %constant.98), dimensions={0}, to_apply=%all_gather.3.reduce_sub_computation | reduce | bytes 1572866 | tf_op jit(solution)/shard_map/all_gather | solution.py:66
  65.6 1.2 reshape.185
  66.9 1.3 reshape.205
  68.1 4.1 gather_fusion
  72.7 1.2 copy.38
  73.9 4.1 multiply_reduce_fusion
  78.1 1.2 copy.43
  79.5 1.8 copy.52
  81.3 5.2 fusion.25
  86.5 3.7 multiply_reduce_fusion.1
  90.2 1.8 copy.44
  92.0 18.6 %all-to-all-start.1 = ((bf16[1,2,512,128]{3,1,0,2:T(2,128)(2,1)}), bf16[1,2,512,128]{3,1,0,2:T(2,128)(2,1)S(1)}, u32[]{:S(2)}, u32[]{:S(2)}) async-start(bf16[1,2,512,128]{3,1,0,2:T(2,128)(2,1)} %copy.44), calls=%async_computation.1 | async-start | bytes 524288 | tf_op jit(solution)/shard_map/all_to_all | solution.py:90
  110.6 0.9 copy.54
  111.5 21.6 %all-to-all-done.1 = bf16[1,2,512,128]{3,1,0,2:T(2,128)(2,1)S(1)} async-done(((bf16[1,2,512,128]{3,1,0,2:T(2,128)(2,1)}), bf16[1,2,512,128]{3,1,0,2:T(2,128)(2,1)S(1)}, u32[]{:S(2)}, u32[]{:S(2)}) %all-to-all-start.1) | async-done | bytes 262176 | tf_op jit(solution)/shard_map/all_to_all | solution.py:90
  133.1 7.3 all-to-all-start.2
  140.5 105.6 %psum.22 = f32[]{:T(128)} all-reduce(f32[]{:T(128)} %get-tuple-element.9), channel_id=1, replica_groups=mesh['mem'=128,'rep'=4] {'mem','rep'}, use_global_device_ids=true, to_apply=%region_6.7 | all-reduce | flops 1 | bytes 8 | tf_op jit(solution)/shard_map/psum | solution.py:99
  246.6 1.6 reshape.214
  249.0 0.8 fusion.31
  249.8 0.8 fusion.32
  250.7 443.4 %all-reduce.3.cloned.1.call-done = (f32[128,128]{1,0:T(8,128)}, f32[128,128]{1,0:T(8,128)}) async-done(((f32[128,128]{1,0:T(8,128)}, f32[128,128]{1,0:T(8,128)}), (f32[128,128]{1,0:T(8,128)}, f32[128,128]{1,0:T(8,128)})) %all-reduce.3.cloned.1.call-update) | async-done | bytes 131088 | tf_op jit(solution)/shard_map/psum | solution.py:99
  694.1 0.9 select_add_fusion
  695.0 0.9 fusion.74
  695.9 11.7 %cholesky.16 = f32[128,128]{1,0:T(8,128)S(1)} custom-call(f32[128,128]{1,0:T(8,128)S(1)} %fusion.74), custom_call_target="Cholesky" | custom-call | tf_op jit(solution)/shard_map/jit(cholesky)/cholesky | solution.py:42
  708.9 9.8 %custom-call.8 = f32[1,128,128]{1,2,0:T(8,128)S(1)} custom-call(f32[1,128,128]{2,1,0:T(8,128)S(1)} %fusion.69), custom_call_target="InvertDiagBlocksLowerTriangular" | custom-call | tf_op jit(solution)/shard_map/triangular_solve | solution.py:44
  718.7 1.1 fusion.72
  720.6 0.8 reduce.17
  721.4 25.5 %all_to_all.65 = bf16[128,2,384]{2,1,0:T(2,128)(2,1)S(1)} all-to-all(bf16[128,2,384]{2,1,0:T(2,128)(2,1)S(1)} %reshape.215), channel_id=1, replica_groups=mesh['mem'=128,'rep'=4] {'mem'}, dimensions={0} | all-to-all | bytes 393216 | tf_op jit(solution)/shard_map/all_to_all | solution.py:109
  746.9 0.9 reshape.216
  (43 shorter events, 5.6 us)
Async XLA Ops:
  6.5 67.4 %copy-start = (bf16[384,1024]{1,0:T(8,128)(2,1)S(1)}, bf16[384,1024]{1,0:T(8,128)(2,1)}, u32[]{:S(2)}) copy-start(bf16[384,1024]{1,0:T(8,128)(2,1)} %param.14) | copy-start | bytes 2359300
  6.5 26.3 %copy-start.2 = (bf16[1,98304]{1,0:T(2,128)(2,1)S(1)}, bf16[1,98304]{1,0:T(2,128)(2,1)}, u32[]{:S(2)}) copy-start(bf16[1,98304]{1,0:T(2,128)(2,1)} %param.16) | copy-start | bytes 589828
  10.6 81.4 %all-to-all-start = ((bf16[128,2,384]{2,1,0:T(2,128)(2,1)}), bf16[128,2,384]{2,1,0:T(2,128)(2,1)}, u32[]{:S(2)}, u32[]{:S(2)}) async-start(bf16[128,2,384]{2,1,0:T(2,128)(2,1)} %reshape.213), calls=%async_computation | async-start | bytes 393216 | tf_op jit(solution)/shard_map/all_to_all | solution.py:104
  65.6 2.5 copy-start.1
  72.2 1.7 copy-start.5
  72.2 1.7 copy-start.6
  73.9 5.4 copy-start.3
  81.3 5.2 copy-start.4
  92.0 41.1 %all-to-all-start.1 = ((bf16[1,2,512,128]{3,1,0,2:T(2,128)(2,1)}), bf16[1,2,512,128]{3,1,0,2:T(2,128)(2,1)S(1)}, u32[]{:S(2)}, u32[]{:S(2)}) async-start(bf16[1,2,512,128]{3,1,0,2:T(2,128)(2,1)} %copy.44), calls=%async_computation.1 | async-start | bytes 524288 | tf_op jit(solution)/shard_map/all_to_all | solution.py:90
  133.1 115.6 %all-to-all-start.2 = ((bf16[1,2,512,128]{3,1,0,2:T(2,128)(2,1)}), bf16[1,2,512,128]{3,1,0,2:T(2,128)(2,1)S(1)}, u32[]{:S(2)}, u32[]{:S(2)}) async-start(bf16[1,2,512,128]{3,1,0,2:T(2,128)(2,1)} %copy.54), calls=%async_computation.2 | async-start | bytes 524288 | tf_op jit(solution)/shard_map/all_to_all | solution.py:91
  140.4 553.6 %all-reduce.3.cloned.1.call-start = ((), (), s32[]{:S(2)}) async-start(), calls=%async_computation.4 | async-start | bytes 262144 | tf_op jit(solution)/shard_map/psum | solution.py:99
Sparse Core Ops, SparseCore 0:
  250.8 443.2 all-reduce.2
where the time goes:
time: 756 us; the launch traced here: 755 us
  waiting for transfers between devices  465 us (62%)
  blocking collectives  148 us (20%)
  starting transfers between devices  46.7 us (6%)
  other arithmetic  46.5 us (6%)
  local copies, waits for them, and re-layouts  17.6 us (2%)
  matrix products  16.9 us (2%)
  between operations  14.3 us (2%)
    psum x1, waiting for transfers between devices, on_device(): lax.psum((gram_matrix, innovation, misfit_local), ('mem', 'rep'))  443 us
    psum x1, blocking collectives, on_device(): lax.psum((gram_matrix, innovation, misfit_local), ('mem', 'rep'))  106 us
    all_to_all x1, blocking collectives, on_device(): lax.all_to_all(renewed, 'mem', split_axis=0, concat_axis=1, tiled=True)  25.5 us
    all_to_all x1, waiting for transfers between devices, on_device(): lax.all_to_all(weighted, 'mem', split_axis=2, concat_axis=0, tiled=True)  21.6 us
    all_to_all x1, starting transfers between devices, on_device(): lax.all_to_all(member_params, 'mem', split_axis=1, concat_axis=0, tiled=T...  20.8 us
    all_to_all x1, starting transfers between devices, on_device(): lax.all_to_all(weighted, 'mem', split_axis=2, concat_axis=0, tiled=True)  18.6 us
    all_gather x1, blocking collectives, on_device(): whole_params = lax.all_gather(member_params, 'rep', axis=1, tiled=True)  16.5 us
    all_gather x1, other arithmetic, on_device(): whole_params = lax.all_gather(member_params, 'rep', axis=1, tiled=True)  16.3 us
  transfers between devices with their start and end apart: 4, of which 2 were waited for; matrix products, arithmetic and copies ran while one was open for 6% of the time, Pallas kernels for 0%

commit v1 on v0

v1 whole, which is shorter than its diff:
```python
import jax
import jax.numpy as jnp
from jax import lax
from jax.sharding import Mesh
from jax.sharding import PartitionSpec as P

EPS = 1e-06
DT = 0.5
MEM = ("x", "z", "c")
NEAR = ("x", "c", "r")
HIGHEST = lax.Precision.HIGHEST


def hidden_layer(state, norm_gain, w_in, b_in):
    normed = (
        state * lax.rsqrt(jnp.mean(state * state, axis=-1, keepdims=True) + EPS) * norm_gain
    ).astype(jnp.bfloat16)
    return jax.nn.gelu(jnp.dot(normed, w_in, preferred_element_type=jnp.float32) + b_in).astype(
        jnp.bfloat16
    )


def solve_columns(system, right_side):
    lower_factor = jnp.linalg.cholesky(system)
    halfway = lax.linalg.triangular_solve(lower_factor, right_side, left_side=True, lower=True)
    return lax.linalg.triangular_solve(
        lower_factor, halfway, left_side=True, lower=True, transpose_a=True
    )


def exchange(value, axes):
    return lax.all_to_all(value, axes, split_axis=0, concat_axis=0, tiled=True)


def spread_to(value, axes):
    count = lax.axis_size(axes)
    return exchange(jnp.broadcast_to(value[None], (count,) + value.shape), axes)


def total_of(partial):
    near = lax.axis_size(NEAR)
    piece = jnp.sum(exchange(partial.reshape(near, -1, partial.shape[1]), NEAR), axis=0)
    piece = jnp.sum(spread_to(piece, "z"), axis=0)
    return spread_to(piece, NEAR).reshape(partial.shape)


def on_device(
    states,
    batch_index,
    obs_pick,
    norm_gain,
    w_in,
    b_in,
    member_params,
    observed,
    perturbation,
    inv_sigma,
):
    members = lax.axis_size(MEM)
    width = w_in.shape[1]
    features = w_in.shape[0]
    step_count, rows = batch_index.shape
    picked = obs_pick.shape[1]
    own = member_params.reshape(-1, features)
    weights = lax.all_gather(own, "r", axis=0, tiled=True)
    noise = exchange(perturbation.reshape(members, -1, picked), MEM)
    param_block = exchange(own.reshape(members, -1, features), MEM)
    step_scale = DT * width ** (-0.5)
    current = states.astype(jnp.float32)
    for _ in range(2):
        layer = hidden_layer(current, norm_gain, w_in, b_in)
        current = current + step_scale * jnp.dot(layer, weights, preferred_element_type=jnp.float32)
    feature_ids = lax.broadcasted_iota(jnp.int32, (step_count, features, picked), 1)
    selector = (feature_ids == obs_pick[:, None, :]).astype(jnp.float32)
    state_ids = lax.broadcasted_iota(jnp.int32, (step_count, rows, states.shape[0]), 2)
    row_selector = (state_ids == batch_index[:, :, None]).astype(jnp.float32)
    narrowed = jnp.einsum("bs,ksf->kbf", current, selector, precision=HIGHEST)
    predicted = jnp.einsum("kib,kbf->kif", row_selector, narrowed, precision=HIGHEST)
    scaled = predicted * inv_sigma
    aim = observed.astype(jnp.float32) * inv_sigma
    weighted = scaled.astype(jnp.bfloat16)
    misfit_w = (aim + perturbation[0].astype(jnp.float32) - scaled).astype(jnp.bfloat16)
    misfit_local = jnp.sum(jnp.square(misfit_w.astype(jnp.float32)))
    entries = members * step_count * rows * lax.axis_size("r") * picked
    gathered = exchange(weighted.reshape(members, -1, picked), MEM).astype(jnp.float32)
    depth = gathered.shape[1]
    place = lax.axis_index(MEM) * depth
    aim_here = lax.dynamic_slice_in_dim(aim.reshape(-1, picked), place, depth, 0)
    anomaly = (gathered - jnp.mean(gathered, axis=0)).astype(jnp.bfloat16)
    misfit_here = (aim_here + noise.astype(jnp.float32) - gathered).astype(jnp.bfloat16)
    both = jnp.concatenate([anomaly, misfit_here], axis=0)
    partial = lax.dot_general(
        both, anomaly, (((1, 2), (1, 2)), ((), ())), preferred_element_type=jnp.float32
    )
    unit = lax.broadcasted_iota(jnp.int32, partial.shape, 0) == lax.broadcasted_iota(
        jnp.int32, partial.shape, 1
    )
    partial = partial + jnp.where(unit, misfit_local * ((members - 1) / entries), 0.0)
    total = total_of(partial)
    system = total[:members] + (members - 1.0) * jnp.eye(members, dtype=jnp.float32)
    coefficients = solve_columns(system, total[members:].T)
    centred = coefficients - jnp.mean(coefficients, axis=0)
    params_f = param_block.astype(jnp.float32)
    change = jnp.einsum("kj,kap->jap", centred, params_f, precision=HIGHEST)
    renewed = (params_f + change).astype(jnp.bfloat16)
    return exchange(renewed, MEM).reshape(member_params.shape)


def solution(mesh):
    fine = Mesh(mesh.devices.reshape(4, 16, 2, 4), ("x", "z", "c", "r"))
    placed = (
        P("r", None),
        P(None, "r"),
        P(),
        P(),
        P(),
        P(),
        P(MEM, "r"),
        P(None, "r", None),
        P(MEM, None, "r", None),
        P(None, "r", None),
    )
    return jax.shard_map(
        on_device, mesh=fine, in_specs=placed, out_specs=P(MEM, "r"), check_vma=False
    )
```

time: 756 us -> 208 us (0.28)
  waiting for transfers between devices: 465 us -> 28.8 us
  starting transfers between devices: 46.7 us -> 18.7 us
  blocking collectives: 148 us -> 122 us
  other arithmetic: 46.5 us -> 25.5 us
  local copies, waits for them, and re-layouts: 17.6 us -> 3.73 us
  between operations: 14.3 us -> 0.9 us
  matrix products: 16.9 us -> 7.92 us
    psum x1 -> x0, waiting for transfers between devices: 443 us -> none  [on_device(): lax.psum((gram_matrix, innovation, misfit_local), ('mem', 'rep'))]
    psum x1 -> x0, blocking collectives: 106 us -> none  [on_device(): lax.psum((gram_matrix, innovation, misfit_local), ('mem', 'rep'))]
    all_to_all x1 -> x4, blocking collectives: 25.5 us -> 110 us  [exchange(): return lax.all_to_all(value, axes, split_axis=0, concat_axis=0, tiled=True)]
    all_to_all x3, starting transfers between devices: 46.7 us -> 18.7 us  [exchange(): return lax.all_to_all(value, axes, split_axis=0, concat_axis=0, tiled=True)]
    all_gather x1 -> x0, other arithmetic: 16.3 us -> none  [on_device(): whole_params = lax.all_gather(member_params, 'rep', axis=1, tiled=True)]
    dot_general x8 -> x6, matrix products: 15.6 us -> 7.41 us  [the longest x2 3.38 us: on_device(): jnp.dot(layer, weights, preferred_element_type=jnp.float32)]
  transfers between devices with their start and end apart: 4 -> 3, of which waited for: 2 -> 2; matrix products, arithmetic and copies ran while one was open for 6% -> 12% of each run, Pallas kernels for 0% -> 0%
where the time goes in v1:
time: 208 us
  blocking collectives  122 us (59%)
  waiting for transfers between devices  28.8 us (14%)
  other arithmetic  25.5 us (12%)
  starting transfers between devices  18.7 us (9%)
  matrix products  7.92 us (4%)
  local copies, waits for them, and re-layouts  3.73 us (2%)
    all_to_all x4, blocking collectives, exchange(): return lax.all_to_all(value, axes, split_axis=0, concat_axis=0, tiled=True)  110 us
    all_to_all x3, waiting for transfers between devices, exchange(): return lax.all_to_all(value, axes, split_axis=0, concat_axis=0, tiled=True)  28.8 us
    all_to_all x3, starting transfers between devices, exchange(): return lax.all_to_all(value, axes, split_axis=0, concat_axis=0, tiled=True)  18.7 us
    another operation x3, other arithmetic, solve_columns(): lower_factor = jnp.linalg.cholesky(system)  12.5 us
    all_gather x1, blocking collectives, on_device(): weights = lax.all_gather(own, 'r', axis=0, tiled=True)  12.2 us
    another operation x2, other arithmetic, solve_columns(): lax.linalg.triangular_solve(lower_factor, halfway, left_side=True, lower=...  10.5 us
  transfers between devices with their start and end apart: 3, of which 2 were waited for; matrix products, arithmetic and copies ran while one was open for 12% of the time, Pallas kernels for 0%

profile of v1, /device:TPU:1, one launch (start us, length us, event | category | flops | bytes accessed | tf_op | source)
XLA Modules:
  0.0 207.8 jit_solution(9530216531847236784)
XLA Ops:
  0.0 2.1 %reduce.6 = bf16[98304]{0:T(1024)(128)(2,1)S(1)} reduce(bf16[1,98304]{1,0:T(2,128)(2,1)} %param.16, bf16[]{:T(256)} %constant.99), dimensions={0}, to_apply=%param.16.reduce_sub_computation | reduce | bytes 393218 | tf_op args[6]
  2.3 12.2 %all_gather.3 = bf16[1024,384]{1,0:T(8,128)(2,1)S(1)} all-gather(bf16[256,384]{1,0:T(8,128)(2,1)S(1)} %reshape.63), channel_id=1, replica_groups=mesh['x'=4,'z'=16,'c'=2,'r'=4] {'r'}, dimensions={0}, use_global_device_ids=true | all-gather | bytes 983040 | tf_op jit(solution)/shard_map/all_gather | solution.py:65
  14.5 0.2 copy.33
  14.7 0.1 fusion.30
  14.8 0.4 copy-done.6
  15.2 1.7 multiply_reduce_fusion
  16.9 1.7 fusion.19
  18.7 0.7 fusion.50
  19.3 0.3 copy-done.1
  19.7 2.7 %multiply_reduce_fusion.1 = (f32[]{:T(128)}, f32[2,512,128]{2,1,0:T(8,128)S(1)}, bf16[2,512,128]{2,1,0:T(8,128)(2,1)S(1)}) fusion(bf16[1,2,512,128]{3,2,1,0:T(8,128)(2,1)} %param.18, f32[2,512,128]{2,1,0:T(8,128)S(1)} %copy-done.1, bf16[2,512,128]{2,1,0:T(8,128)(2,1)S(1)} %copy-done.3, f32[2,128,512]{2,1,0:T(8,128)S(1)} %fusion.50, s32[2,512]{1,0:T(2,128)S(1)} %copy-done.4), kind=kOutput, calls=%fused_computation.55 | convolution fusion | flops 807272448 | bytes 2363396 | tf_op jit(solution)/shard_map/kib,kbf->kif/dot_general | solution.py:78
  22.4 44.3 %all_to_all.35 = bf16[128,8,128]{2,1,0:T(8,128)(2,1)S(1)} all-to-all(bf16[128,8,128]{2,1,0:T(8,128)(2,1)S(1)} %bitcast.49), channel_id=1, replica_groups=mesh['x'=4,'z'=16,'c'=2,'r'=4] {'x','z','c'}, dimensions={0} | all-to-all | bytes 524288 | tf_op jit(solution)/shard_map/all_to_all | solution.py:32
  66.7 7.3 %all-to-all-start.2 = ((bf16[128,8,128]{2,1,0:T(8,128)(2,1)}), bf16[128,8,128]{2,1,0:T(8,128)(2,1)S(1)}, u32[]{:S(2)}, u32[]{:S(2)}) async-start(bf16[128,8,128]{2,1,0:T(8,128)(2,1)} %bitcast.3), calls=%async_computation.2 | async-start | bytes 524288 | tf_op jit(solution)/shard_map/all_to_all | solution.py:32
  74.8 21.9 %all-to-all-done.2 = bf16[128,8,128]{2,1,0:T(8,128)(2,1)S(1)} async-done(((bf16[128,8,128]{2,1,0:T(8,128)(2,1)}), bf16[128,8,128]{2,1,0:T(8,128)(2,1)S(1)}, u32[]{:S(2)}, u32[]{:S(2)}) %all-to-all-start.2) | async-done | bytes 262176 | tf_op jit(solution)/shard_map/all_to_all | solution.py:32
  96.6 0.1 fusion.36
  96.8 0.3 fusion.23
  97.1 15.5 %all_to_all.36 = f32[32,8,128]{2,1,0:T(8,128)S(1)} all-to-all(f32[32,8,128]{2,1,0:T(8,128)S(1)} %fusion.23), channel_id=1, replica_groups=mesh['x'=4,'z'=16,'c'=2,'r'=4] {'x','c','r'}, dimensions={0} | all-to-all | bytes 262144 | tf_op jit(solution)/shard_map/all_to_all | solution.py:32
  112.6 14.2 %all_to_all.37 = f32[16,8,128]{2,1,0:T(8,128)S(1)} all-to-all(f32[16,8,128]{2,1,0:T(8,128)S(1)} %broadcast_in_dim.15), channel_id=1, replica_groups=mesh['x'=4,'z'=16,'c'=2,'r'=4] {'z'}, dimensions={0} | all-to-all | bytes 131072 | tf_op jit(solution)/shard_map/all_to_all | solution.py:32
  126.9 0.6 broadcast_in_dim.16
  127.5 5.7 %all-to-all-start.5 = ((f32[32,8,128]{2,1,0:T(8,128)}), f32[32,8,128]{2,1,0:T(8,128)S(1)}, u32[]{:S(2)}, u32[]{:S(2)}) async-start(f32[32,8,128]{2,1,0:T(8,128)} %broadcast_in_dim.16), calls=%async_computation.5 | async-start | bytes 262144 | tf_op jit(solution)/shard_map/all_to_all | solution.py:32
  133.3 0.8 reshape_reshape.3
  134.1 6.9 %all-to-all-done.5 = f32[32,8,128]{2,1,0:T(8,128)S(1)} async-done(((f32[32,8,128]{2,1,0:T(8,128)}), f32[32,8,128]{2,1,0:T(8,128)S(1)}, u32[]{:S(2)}, u32[]{:S(2)}) %all-to-all-start.5) | async-done | bytes 131104 | tf_op jit(solution)/shard_map/all_to_all | solution.py:32
  140.9 5.7 %all-to-all-start = ((bf16[128,2,384]{2,1,0:T(2,128)(2,1)}), bf16[128,2,384]{2,1,0:T(2,128)(2,1)S(1)}, u32[]{:S(2)}, u32[]{:S(2)}) async-start(bf16[128,2,384]{2,1,0:T(2,128)(2,1)} %reshape_reshape.3), calls=%async_computation | async-start | bytes 393216 | tf_op jit(solution)/shard_map/all_to_all | solution.py:32
  146.8 11.7 %cholesky.16 = f32[128,128]{1,0:T(8,128)S(1)} custom-call(f32[128,128]{1,0:T(8,128)S(1)} %fusion.60), custom_call_target="Cholesky" | custom-call | tf_op jit(solution)/shard_map/jit(cholesky)/cholesky | solution.py:24
  158.5 0.7 compare_reduce_fusion
  159.2 0.7 fusion.53
  159.9 9.8 %custom-call.8 = f32[1,128,128]{1,2,0:T(8,128)S(1)} custom-call(f32[1,128,128]{2,1,0:T(8,128)S(1)} %fusion.53), custom_call_target="InvertDiagBlocksLowerTriangular" | custom-call | tf_op jit(solution)/shard_map/triangular_solve | solution.py:26
  169.8 0.3 fusion.54
  170.0 0.2 fusion.74
  170.3 0.4 fusion.21
  170.7 0.2 copy.41
  170.9 36.0 %all_to_all.38 = bf16[128,2,384]{2,1,0:T(2,128)(2,1)S(1)} all-to-all(bf16[128,2,384]{2,1,0:T(2,128)(2,1)S(1)} %copy.41), channel_id=1, replica_groups=mesh['x'=4,'z'=16,'c'=2,'r'=4] {'x','z','c'}, dimensions={0} | all-to-all | bytes 393216 | tf_op jit(solution)/shard_map/all_to_all | solution.py:32
  206.9 0.9 reshape.68
  (29 shorter events, 0.5 us)
Async XLA Ops:
  0.0 14.8 %copy-start = (bf16[384,1024]{1,0:T(8,128)(2,1)S(1)}, bf16[384,1024]{1,0:T(8,128)(2,1)}, u32[]{:S(2)}) copy-start(bf16[384,1024]{1,0:T(8,128)(2,1)} %param.14) | copy-start | bytes 2359300
  2.2 12.3 %copy-start.2 = (bf16[512,384]{1,0:T(8,128)(2,1)S(1)}, bf16[512,384]{1,0:T(8,128)(2,1)}, u32[]{:S(2)}) copy-start(bf16[512,384]{1,0:T(8,128)(2,1)} %param.10) | copy-start | bytes 1179652
  14.5 0.7 copy-start.6
  14.5 0.7 copy-start.7
  16.9 1.7 copy-start.5
  18.6 1.0 copy-start.1
  18.6 1.1 copy-start.3
  18.6 1.1 copy-start.4
  66.7 29.9 %all-to-all-start.2 = ((bf16[128,8,128]{2,1,0:T(8,128)(2,1)}), bf16[128,8,128]{2,1,0:T(8,128)(2,1)S(1)}, u32[]{:S(2)}, u32[]{:S(2)}) async-start(bf16[128,8,128]{2,1,0:T(8,128)(2,1)} %bitcast.3), calls=%async_computation.2 | async-start | bytes 524288 | tf_op jit(solution)/shard_map/all_to_all | solution.py:32
  127.5 13.4 %all-to-all-start.5 = ((f32[32,8,128]{2,1,0:T(8,128)}), f32[32,8,128]{2,1,0:T(8,128)S(1)}, u32[]{:S(2)}, u32[]{:S(2)}) async-start(f32[32,8,128]{2,1,0:T(8,128)} %broadcast_in_dim.16), calls=%async_computation.5 | async-start | bytes 262144 | tf_op jit(solution)/shard_map/all_to_all | solution.py:32
  140.9 29.3 %all-to-all-start = ((bf16[128,2,384]{2,1,0:T(2,128)(2,1)}), bf16[128,2,384]{2,1,0:T(2,128)(2,1)S(1)}, u32[]{:S(2)}, u32[]{:S(2)}) async-start(bf16[128,2,384]{2,1,0:T(2,128)(2,1)} %reshape_reshape.3), calls=%async_computation | async-start | bytes 393216 | tf_op jit(solution)/shard_map/all_to_all | solution.py:32

commit v2 on v1

--- a/solution.py
+++ b/solution.py
@@ -1,6 +1,8 @@
 import jax
 import jax.numpy as jnp
 from jax import lax
+from jax.experimental import pallas as pl
+from jax.experimental.pallas import tpu as pltpu
 from jax.sharding import Mesh
 from jax.sharding import PartitionSpec as P
 
@@ -8,6 +10,7 @@
 DT = 0.5
 MEM = ("x", "z", "c")
 NEAR = ("x", "c", "r")
+BLOCK = 8
 HIGHEST = lax.Precision.HIGHEST
 
 
@@ -20,12 +23,65 @@
     )
 
 
-def solve_columns(system, right_side):
-    lower_factor = jnp.linalg.cholesky(system)
-    halfway = lax.linalg.triangular_solve(lower_factor, right_side, left_side=True, lower=True)
-    return lax.linalg.triangular_solve(
-        lower_factor, halfway, left_side=True, lower=True, transpose_a=True
-    )
+def eliminate(left, right):
+    wide = lambda v: jnp.broadcast_to(v, left[0].shape)
+    cols = [[wide(tile[:, q : q + 1]) for q in range(BLOCK)] for tile in left]
+    pivots = [[wide(cols[0][q][p : p + 1]) for q in range(BLOCK)] for p in range(BLOCK)]
+    top = [wide(left[0][p : p + 1]) for p in range(BLOCK)]
+    side = [wide(right[0][p : p + 1]) for p in range(BLOCK)]
+    for p in range(BLOCK):
+        inverse = 1.0 / pivots[p][p]
+        for c in range(p + 1, BLOCK):
+            pivots[p][c] = pivots[p][c] * inverse
+        top[p] = top[p] * inverse
+        side[p] = side[p] * inverse
+        for q in range(BLOCK):
+            if q != p:
+                factor = pivots[q][p]
+                for c in range(p + 1, BLOCK):
+                    pivots[q][c] = pivots[q][c] - factor * pivots[p][c]
+                top[q] = top[q] - factor * top[p]
+                side[q] = side[q] - factor * side[p]
+    row = lax.broadcasted_iota(jnp.int32, left[0].shape, 0)
+    last_left, last_right = top[0], side[0]
+    for p in range(1, BLOCK):
+        last_left = jnp.where(row == p, top[p], last_left)
+        last_right = jnp.where(row == p, side[p], last_right)
+    next_left, next_right = [], []
+    for t in range(1, len(left)):
+        a, b = left[t], right[t]
+        for q in range(BLOCK):
+            a = a - cols[t][q] * top[q]
+            b = b - cols[t][q] * side[q]
+        next_left.append(a)
+        next_right.append(b)
+    next_left.append(last_left)
+    next_right.append(last_right)
+    turn = left[0].shape[1] - BLOCK
+    return [pltpu.roll(a, turn, 1) for a in next_left], next_right
+
+
+def solve_kernel(total_ref, out_ref):
+    n = out_ref.shape[0]
+    row = lax.broadcasted_iota(jnp.int32, (n, n), 0)
+    column = lax.broadcasted_iota(jnp.int32, (n, n), 1)
+    system = total_ref[:n] + jnp.where(row == column, n - 1.0, 0.0)
+    right_side = total_ref[n:].T
+    left = [system[t : t + BLOCK] for t in range(0, n, BLOCK)]
+    right = [right_side[t : t + BLOCK] for t in range(0, n, BLOCK)]
+    _, solved = lax.fori_loop(0, n // BLOCK, lambda _, lr: eliminate(*lr), (left, right))
+    solved = jnp.concatenate(solved, axis=0)
+    out_ref[...] = solved - jnp.mean(solved, axis=0, keepdims=True)
+
+
+def centred_coefficients(total):
+    n = total.shape[1]
+    return pl.pallas_call(
+        solve_kernel,
+        out_shape=jax.ShapeDtypeStruct((n, n), jnp.float32),
+        cost_estimate=pl.CostEstimate(flops=40000000, bytes_accessed=200000, transcendentals=0),
+        compiler_params=pltpu.CompilerParams(vmem_limit_bytes=4 * 1024 * 1024),
+    )(total)
 
 
 def exchange(value, axes):
@@ -67,7 +123,9 @@
     param_block = exchange(own.reshape(members, -1, features), MEM)
     step_scale = DT * width ** (-0.5)
     current = states.astype(jnp.float32)
-    for _ in range(2):
+    for turn in range(2):
+        if turn:
+            current, noise = lax.optimization_barrier((current, noise))
         layer = hidden_layer(current, norm_gain, w_in, b_in)
         current = current + step_scale * jnp.dot(layer, weights, preferred_element_type=jnp.float32)
     feature_ids = lax.broadcasted_iota(jnp.int32, (step_count, features, picked), 1)
@@ -97,9 +155,7 @@
     )
     partial = partial + jnp.where(unit, misfit_local * ((members - 1) / entries), 0.0)
     total = total_of(partial)
-    system = total[:members] + (members - 1.0) * jnp.eye(members, dtype=jnp.float32)
-    coefficients = solve_columns(system, total[members:].T)
-    centred = coefficients - jnp.mean(coefficients, axis=0)
+    centred = centred_coefficients(total)
     params_f = param_block.astype(jnp.float32)
     change = jnp.einsum("kj,kap->jap", centred, params_f, precision=HIGHEST)
     renewed = (params_f + change).astype(jnp.bfloat16)

time: 208 us -> 181 us (0.87)
  blocking collectives: 122 us -> 68.7 us
  starting transfers between devices: 18.7 us -> 42.6 us
  other arithmetic: 25.5 us -> 1.68 us
  waiting for transfers between devices: 28.8 us -> 47.1 us
  Pallas kernels: 0 us -> 8.32 us
    all_to_all x4 -> x3, blocking collectives: 110 us -> 55.9 us  [exchange(): return lax.all_to_all(value, axes, split_axis=0, concat_axis=0, tiled=True)]
    all_to_all x3 -> x4, starting transfers between devices: 18.7 us -> 42.6 us  [exchange(): return lax.all_to_all(value, axes, split_axis=0, concat_axis=0, tiled=True)]
    another operation x5 -> x0, other arithmetic: 23 us -> none  [the longest x3 12.5 us: solve_columns(): lower_factor = jnp.linalg.cholesky(system)]
    all_to_all x3 -> x4, waiting for transfers between devices: 28.8 us -> 47.1 us  [exchange(): return lax.all_to_all(value, axes, split_axis=0, concat_axis=0, tiled=True)]
    pallas_call x0 -> x1, Pallas kernels: none -> 8.32 us  [centred_coefficients(): pl.pallas_call(solve_kernel, out_shape=jax.ShapeDtypeStruct((n, n), jnp.f...]
  transfers between devices with their start and end apart: 3 -> 4, of which waited for: 2 -> 4; matrix products, arithmetic and copies ran while one was open for 12% -> 2% of each run, Pallas kernels for 0% -> 5%
where the time goes in v2:
time: 181 us; the launch traced here: 180 us
  blocking collectives  68.7 us (38%)
  waiting for transfers between devices  47.1 us (26%)
  starting transfers between devices  42.6 us (24%)
  Pallas kernels  8.32 us (5%)
  matrix products  7.95 us (4%)
  local copies, waits for them, and re-layouts  3.18 us (2%)
    all_to_all x3, blocking collectives, exchange(): return lax.all_to_all(value, axes, split_axis=0, concat_axis=0, tiled=True)  55.9 us
    all_to_all x4, waiting for transfers between devices, exchange(): return lax.all_to_all(value, axes, split_axis=0, concat_axis=0, tiled=True)  47.1 us
    all_to_all x4, starting transfers between devices, exchange(): return lax.all_to_all(value, axes, split_axis=0, concat_axis=0, tiled=True)  42.6 us
    all_gather x1, blocking collectives, on_device(): weights = lax.all_gather(own, 'r', axis=0, tiled=True)  12.8 us
    pallas_call x1, Pallas kernels, centred_coefficients(): pl.pallas_call(solve_kernel, out_shape=jax.ShapeDtypeStruct((n, n), jnp.f...  8.32 us
    dot_general x2, matrix products, on_device(): jnp.dot(layer, weights, preferred_element_type=jnp.float32)  4.2 us
  transfers between devices with their start and end apart: 4, of which 4 were waited for; matrix products, arithmetic and copies ran while one was open for 2% of the time, Pallas kernels for 5%

profile of v2, /device:TPU:1, one launch (start us, length us, event | category | flops | bytes accessed | tf_op | source)
XLA Modules:
  0.0 180.4 jit_solution(15319833800089987840)
XLA Ops:
  0.0 20.5 %all-to-all-start.1 = ((bf16[128,8,128]{2,1,0:T(8,128)(2,1)}), bf16[128,8,128]{2,1,0:T(8,128)(2,1)S(1)}, u32[]{:S(2)}, u32[]{:S(2)}) async-start(bf16[128,8,128]{2,1,0:T(8,128)(2,1)} %bitcast.28), calls=%async_computation.1 | async-start | bytes 524288 | tf_op jit(solution)/shard_map/all_to_all | solution.py:88
  20.6 1.2 reduce
  21.7 0.1 reshape.49
  21.9 0.0 copy-start.10
  21.9 0.2 fusion.30
  22.0 12.8 %all_gather.3 = bf16[1024,384]{1,0:T(8,128)(2,1)S(1)} all-gather(bf16[256,384]{1,0:T(8,128)(2,1)S(1)} %reshape.49), channel_id=1, replica_groups=mesh['x'=4,'z'=16,'c'=2,'r'=4] {'r'}, dimensions={0}, use_global_device_ids=true | all-gather | bytes 983040 | tf_op jit(solution)/shard_map/all_gather | solution.py:121
  34.9 1.5 fusion.17
  36.4 6.6 %all-to-all-done.1 = bf16[128,8,128]{2,1,0:T(8,128)(2,1)S(1)} async-done(((bf16[128,8,128]{2,1,0:T(8,128)(2,1)}), bf16[128,8,128]{2,1,0:T(8,128)(2,1)S(1)}, u32[]{:S(2)}, u32[]{:S(2)}) %all-to-all-start.1) | async-done | bytes 262176 | tf_op jit(solution)/shard_map/all_to_all | solution.py:88
  43.1 0.1 multiply_reduce_fusion
  43.2 2.7 %fusion.19 = f32[512,384,1]{1,0,2:T(8,128)S(1)} fusion(f32[512,384]{1,0:T(8,128)S(1)} %fusion.17, bf16[1024,384]{1,0:T(8,128)(2,1)} %copy-done.2, bf16[384,1024]{1,0:T(8,128)(2,1)S(1)} %copy-done, f32[1024]{0:T(1024)S(1)} %copy-done.9, f32[512]{0:T(512)S(1)} %add_rsqrt_fusion, f32[384]{0:T(512)S(1)} %copy-done.10), kind=kOutput, calls=%fused_computation.24 | convolution fusion | flops 811532288 | bytes 3153408 | tf_op jit(solution)/shard_map/dot_general | solution.py:130
  46.0 0.7 fusion.50
  46.6 0.2 copy-done.1
  46.9 0.2 copy-done.3
  47.1 0.1 copy-done.6
  47.1 2.4 %multiply_reduce_fusion.1 = (f32[]{:T(128)}, f32[2,512,128]{2,1,0:T(8,128)S(1)}, bf16[2,512,128]{2,1,0:T(8,128)(2,1)}) fusion(bf16[1,2,512,128]{3,2,1,0:T(8,128)(2,1)S(1)} %copy-done.1, f32[2,512,128]{2,1,0:T(8,128)S(1)} %copy-done.3, bf16[2,512,128]{2,1,0:T(8,128)(2,1)S(1)} %copy-done.6, f32[2,128,512]{2,1,0:T(8,128)S(1)} %fusion.50, ...), kind=kOutput, calls=%fused_computation.55 | convolution fusion | flops 807272448 | bytes 2363396 | tf_op jit(solution)/shard_map/kib,kbf->kif/dot_general | solution.py:136
  49.5 10.8 %all-to-all-start.2 = ((bf16[128,8,128]{2,1,0:T(8,128)(2,1)}), bf16[128,8,128]{2,1,0:T(8,128)(2,1)S(1)}, u32[]{:S(2)}, u32[]{:S(2)}) async-start(bf16[128,8,128]{2,1,0:T(8,128)(2,1)} %bitcast.2), calls=%async_computation.2 | async-start | bytes 524288 | tf_op jit(solution)/shard_map/all_to_all | solution.py:88
  61.0 21.9 %all-to-all-done.2 = bf16[128,8,128]{2,1,0:T(8,128)(2,1)S(1)} async-done(((bf16[128,8,128]{2,1,0:T(8,128)(2,1)}), bf16[128,8,128]{2,1,0:T(8,128)(2,1)S(1)}, u32[]{:S(2)}, u32[]{:S(2)}) %all-to-all-start.2) | async-done | bytes 262176 | tf_op jit(solution)/shard_map/all_to_all | solution.py:88
  82.9 0.1 fusion.36
  83.0 0.3 fusion.23
  83.3 15.2 %all_to_all.35 = f32[32,8,128]{2,1,0:T(8,128)S(1)} all-to-all(f32[32,8,128]{2,1,0:T(8,128)S(1)} %fusion.23), channel_id=1, replica_groups=mesh['x'=4,'z'=16,'c'=2,'r'=4] {'x','c','r'}, dimensions={0} | all-to-all | bytes 262144 | tf_op jit(solution)/shard_map/all_to_all | solution.py:88
  98.6 14.2 %all_to_all.36 = f32[16,8,128]{2,1,0:T(8,128)S(1)} all-to-all(f32[16,8,128]{2,1,0:T(8,128)S(1)} %broadcast_in_dim.14), channel_id=1, replica_groups=mesh['x'=4,'z'=16,'c'=2,'r'=4] {'z'}, dimensions={0} | all-to-all | bytes 131072 | tf_op jit(solution)/shard_map/all_to_all | solution.py:88
  112.9 0.7 broadcast_in_dim.15
  113.5 5.5 %all-to-all-start.5 = ((f32[32,8,128]{2,1,0:T(8,128)}), f32[32,8,128]{2,1,0:T(8,128)S(1)}, u32[]{:S(2)}, u32[]{:S(2)}) async-start(f32[32,8,128]{2,1,0:T(8,128)} %broadcast_in_dim.15), calls=%async_computation.5 | async-start | bytes 262144 | tf_op jit(solution)/shard_map/all_to_all | solution.py:88
  119.1 0.8 reshape_reshape.3
  119.9 6.9 %all-to-all-done.5 = f32[32,8,128]{2,1,0:T(8,128)S(1)} async-done(((f32[32,8,128]{2,1,0:T(8,128)}), f32[32,8,128]{2,1,0:T(8,128)S(1)}, u32[]{:S(2)}, u32[]{:S(2)}) %all-to-all-start.5) | async-done | bytes 131104 | tf_op jit(solution)/shard_map/all_to_all | solution.py:88
  126.7 5.7 %all-to-all-start = ((bf16[128,2,384]{2,1,0:T(2,128)(2,1)}), bf16[128,2,384]{2,1,0:T(2,128)(2,1)S(1)}, u32[]{:S(2)}, u32[]{:S(2)}) async-start(bf16[128,2,384]{2,1,0:T(2,128)(2,1)} %reshape_reshape.3), calls=%async_computation | async-start | bytes 393216 | tf_op jit(solution)/shard_map/all_to_all | solution.py:88
  132.4 8.3 %shard_map.100 = f32[128,128]{1,0:T(8,128)S(1)} custom-call(f32[256,128]{1,0:T(8,128)S(1)} %bitcast.27), custom_call_target="tpu_custom_call" | custom-call | flops 40000000 | bytes 200000 | tf_op jit(solution)/shard_map/pallas_call | solution.py:79
  140.7 11.7 %all-to-all-done = bf16[128,2,384]{2,1,0:T(2,128)(2,1)S(1)} async-done(((bf16[128,2,384]{2,1,0:T(2,128)(2,1)}), bf16[128,2,384]{2,1,0:T(2,128)(2,1)S(1)}, u32[]{:S(2)}, u32[]{:S(2)}) %all-to-all-start) | async-done | bytes 196640 | tf_op jit(solution)/shard_map/all_to_all | solution.py:88
  152.5 0.4 fusion.21
  152.9 0.2 copy.29
  153.1 26.4 %all_to_all.37 = bf16[128,2,384]{2,1,0:T(2,128)(2,1)S(1)} all-to-all(bf16[128,2,384]{2,1,0:T(2,128)(2,1)S(1)} %copy.29), channel_id=1, replica_groups=mesh['x'=4,'z'=16,'c'=2,'r'=4] {'x','z','c'}, dimensions={0} | all-to-all | bytes 393216 | tf_op jit(solution)/shard_map/all_to_all | solution.py:88
  179.5 0.9 reshape.55
  (26 shorter events, 0.2 us)
Async XLA Ops:
  0.0 34.9 %copy-start = (bf16[384,1024]{1,0:T(8,128)(2,1)S(1)}, bf16[384,1024]{1,0:T(8,128)(2,1)}, u32[]{:S(2)}) copy-start(bf16[384,1024]{1,0:T(8,128)(2,1)} %param.14) | copy-start | bytes 2359300
  0.0 20.6 %copy-start.5 = (bf16[1,98304]{1,0:T(2,128)(2,1)S(1)}, bf16[1,98304]{1,0:T(2,128)(2,1)}, u32[]{:S(2)}) copy-start(bf16[1,98304]{1,0:T(2,128)(2,1)} %param.16) | copy-start | bytes 589828
  0.0 21.8 %copy-start.4 = (bf16[512,384]{1,0:T(8,128)(2,1)S(1)}, bf16[512,384]{1,0:T(8,128)(2,1)}, u32[]{:S(2)}) copy-start(bf16[512,384]{1,0:T(8,128)(2,1)} %param.10) | copy-start | bytes 1179652
  0.0 43.0 %all-to-all-start.1 = ((bf16[128,8,128]{2,1,0:T(8,128)(2,1)}), bf16[128,8,128]{2,1,0:T(8,128)(2,1)S(1)}, u32[]{:S(2)}, u32[]{:S(2)}) async-start(bf16[128,8,128]{2,1,0:T(8,128)(2,1)} %bitcast.28), calls=%async_computation.1 | async-start | bytes 524288 | tf_op jit(solution)/shard_map/all_to_all | solution.py:88
  21.9 13.0 %copy-start.9 = (f32[1024]{0:T(1024)S(1)}, f32[1024]{0:T(1024)}, u32[]{:S(2)}) copy-start(f32[1024]{0:T(1024)} %param.15) | copy-start | bytes 12292
  21.9 13.0 %copy-start.10 = (f32[384]{0:T(512)S(1)}, f32[384]{0:T(512)}, u32[]{:S(2)}) copy-start(f32[384]{0:T(512)} %param.13) | copy-start | bytes 4612
  34.9 1.5 copy-start.2
  43.2 2.7 %copy-start.8 = (s32[2,128]{1,0:T(2,128)S(1)}, s32[2,128]{1,0:T(2,128)}, u32[]{:S(2)}) copy-start(s32[2,128]{1,0:T(2,128)} %param.12) | copy-start | bytes 3076
  45.9 1.0 copy-start.1
  45.9 1.1 copy-start.3
  45.9 1.2 copy-start.6
  46.0 1.2 copy-start.7
  49.5 33.3 %all-to-all-start.2 = ((bf16[128,8,128]{2,1,0:T(8,128)(2,1)}), bf16[128,8,128]{2,1,0:T(8,128)(2,1)S(1)}, u32[]{:S(2)}, u32[]{:S(2)}) async-start(bf16[128,8,128]{2,1,0:T(8,128)(2,1)} %bitcast.2), calls=%async_computation.2 | async-start | bytes 524288 | tf_op jit(solution)/shard_map/all_to_all | solution.py:88
  113.5 13.2 %all-to-all-start.5 = ((f32[32,8,128]{2,1,0:T(8,128)}), f32[32,8,128]{2,1,0:T(8,128)S(1)}, u32[]{:S(2)}, u32[]{:S(2)}) async-start(f32[32,8,128]{2,1,0:T(8,128)} %broadcast_in_dim.15), calls=%async_computation.5 | async-start | bytes 262144 | tf_op jit(solution)/shard_map/all_to_all | solution.py:88
  126.7 25.7 %all-to-all-start = ((bf16[128,2,384]{2,1,0:T(2,128)(2,1)}), bf16[128,2,384]{2,1,0:T(2,128)(2,1)S(1)}, u32[]{:S(2)}, u32[]{:S(2)}) async-start(bf16[128,2,384]{2,1,0:T(2,128)(2,1)} %reshape_reshape.3), calls=%async_computation | async-start | bytes 393216 | tf_op jit(solution)/shard_map/all_to_all | solution.py:88

commit v3 on v2

--- a/solution.py
+++ b/solution.py
@@ -8,7 +8,9 @@
 
 EPS = 1e-06
 DT = 0.5
-MEM = ("x", "z", "c")
+MEM = ("z", "x", "c")
+PAIR = ("x", "c")
+OWNERS = ("x", "z", "c")
 NEAR = ("x", "c", "r")
 BLOCK = 8
 HIGHEST = lax.Precision.HIGHEST
@@ -61,27 +63,38 @@
     return [pltpu.roll(a, turn, 1) for a in next_left], next_right
 
 
-def solve_kernel(total_ref, out_ref):
-    n = out_ref.shape[0]
+def solve_kernel(first_ref, total_ref, out_ref):
+    n = total_ref.shape[1]
+    few = out_ref.shape[0] // 3
     row = lax.broadcasted_iota(jnp.int32, (n, n), 0)
     column = lax.broadcasted_iota(jnp.int32, (n, n), 1)
     system = total_ref[:n] + jnp.where(row == column, n - 1.0, 0.0)
-    right_side = total_ref[n:].T
+    first = pl.multiple_of(n + first_ref[0] * few, few)
+    right_side = jnp.concatenate([total_ref[pl.ds(first, few), :]] * (n // few), axis=0).T
     left = [system[t : t + BLOCK] for t in range(0, n, BLOCK)]
     right = [right_side[t : t + BLOCK] for t in range(0, n, BLOCK)]
     _, solved = lax.fori_loop(0, n // BLOCK, lambda _, lr: eliminate(*lr), (left, right))
     solved = jnp.concatenate(solved, axis=0)
-    out_ref[...] = solved - jnp.mean(solved, axis=0, keepdims=True)
+    rest = (solved - jnp.mean(solved, axis=0, keepdims=True)).T[:few]
+    for part in range(3):
+        head = rest.astype(jnp.bfloat16).astype(jnp.float32)
+        out_ref[part * few : (part + 1) * few] = head
+        rest = rest - head
 
 
-def centred_coefficients(total):
+def centred_coefficients(total, first, few):
     n = total.shape[1]
     return pl.pallas_call(
         solve_kernel,
-        out_shape=jax.ShapeDtypeStruct((n, n), jnp.float32),
+        out_shape=jax.ShapeDtypeStruct((3 * few, n), jnp.float32),
+        in_specs=[
+            pl.BlockSpec(memory_space=pltpu.SMEM),
+            pl.BlockSpec(memory_space=pltpu.VMEM),
+        ],
+        out_specs=pl.BlockSpec(memory_space=pltpu.VMEM),
         cost_estimate=pl.CostEstimate(flops=40000000, bytes_accessed=200000, transcendentals=0),
         compiler_params=pltpu.CompilerParams(vmem_limit_bytes=4 * 1024 * 1024),
-    )(total)
+    )(first, total)
 
 
 def exchange(value, axes):
@@ -119,8 +132,11 @@
     picked = obs_pick.shape[1]
     own = member_params.reshape(-1, features)
     weights = lax.all_gather(own, "r", axis=0, tiled=True)
+    few = lax.axis_size(PAIR)
+    piece = exchange(member_params.reshape(few, -1), PAIR)
+    perturbation, piece = lax.optimization_barrier((perturbation, piece))
     noise = exchange(perturbation.reshape(members, -1, picked), MEM)
-    param_block = exchange(own.reshape(members, -1, features), MEM)
+    everyone = lax.all_gather(piece, "z", axis=0, tiled=True)
     step_scale = DT * width ** (-0.5)
     current = states.astype(jnp.float32)
     for turn in range(2):
@@ -155,11 +171,11 @@
     )
     partial = partial + jnp.where(unit, misfit_local * ((members - 1) / entries), 0.0)
     total = total_of(partial)
-    centred = centred_coefficients(total)
-    params_f = param_block.astype(jnp.float32)
-    change = jnp.einsum("kj,kap->jap", centred, params_f, precision=HIGHEST)
-    renewed = (params_f + change).astype(jnp.bfloat16)
-    return exchange(renewed, MEM).reshape(member_params.shape)
+    parts = centred_coefficients(total, lax.axis_index("z").reshape(1), few)
+    change = jnp.dot(parts.astype(jnp.bfloat16), everyone, preferred_element_type=jnp.float32)
+    change = jnp.sum(change.reshape(3, few, -1), axis=0)
+    renewed = (piece.astype(jnp.float32) + change).astype(jnp.bfloat16)
+    return exchange(renewed, PAIR).reshape(member_params.shape)
 
 
 def solution(mesh):
@@ -171,11 +187,11 @@
         P(),
         P(),
         P(),
-        P(MEM, "r"),
+        P(OWNERS, "r"),
         P(None, "r", None),
-        P(MEM, None, "r", None),
+        P(OWNERS, None, "r", None),
         P(None, "r", None),
     )
     return jax.shard_map(
-        on_device, mesh=fine, in_specs=placed, out_specs=P(MEM, "r"), check_vma=False
+        on_device, mesh=fine, in_specs=placed, out_specs=P(OWNERS, "r"), check_vma=False
     )

time: 181 us -> 176 us (0.972)
  starting transfers between devices: 42.6 us -> 23.4 us
  waiting for transfers between devices: 47.1 us -> 30.8 us
  between operations: 0.82 us -> 14.2 us
  blocking collectives: 68.7 us -> 80.3 us
  other arithmetic: 1.68 us -> 5.27 us
  matrix products: 7.95 us -> 10.1 us
    all_to_all x4 -> x2, starting transfers between devices: 42.6 us -> 23.4 us  [exchange(): return lax.all_to_all(value, axes, split_axis=0, concat_axis=0, tiled=True)]
    all_to_all x4 -> x2, waiting for transfers between devices: 47.1 us -> 30.8 us  [exchange(): return lax.all_to_all(value, axes, split_axis=0, concat_axis=0, tiled=True)]
    all_to_all x3 -> x5, blocking collectives: 55.9 us -> 67.4 us  [exchange(): return lax.all_to_all(value, axes, split_axis=0, concat_axis=0, tiled=True)]
    all_to_all x0 -> x3, other arithmetic: none -> 3.59 us  [exchange(): return lax.all_to_all(value, axes, split_axis=0, concat_axis=0, tiled=True)]
    dot_general x1, matrix products: 0.37 us -> 2.46 us  [on_device(): jnp.dot(parts.astype(jnp.bfloat16), everyone, preferred_element_type=jnp....]
  transfers between devices with their start and end apart: 4 -> 3, of which waited for: 4 -> 2; matrix products, arithmetic and copies ran while one was open for 2% -> 5% of each run, Pallas kernels for 5% -> 5%
where the time goes in v3:
time: 176 us; the launch traced here: 175 us
  blocking collectives  80.3 us (46%)
  waiting for transfers between devices  30.8 us (18%)
  starting transfers between devices  23.4 us (13%)
  between operations  14.2 us (8%)
  matrix products  10.1 us (6%)
  Pallas kernels  8.38 us (5%)
  other arithmetic  5.27 us (3%)
  local copies, waits for them, and re-layouts  3.02 us (2%)
    all_to_all x5, blocking collectives, exchange(): return lax.all_to_all(value, axes, split_axis=0, concat_axis=0, tiled=True)  67.4 us
    all_to_all x2, waiting for transfers between devices, exchange(): return lax.all_to_all(value, axes, split_axis=0, concat_axis=0, tiled=True)  30.8 us
    all_to_all x2, starting transfers between devices, exchange(): return lax.all_to_all(value, axes, split_axis=0, concat_axis=0, tiled=True)  23.4 us
    all_gather x1, blocking collectives, on_device(): weights = lax.all_gather(own, 'r', axis=0, tiled=True)  12.9 us
    pallas_call x1, Pallas kernels, centred_coefficients(): pl.pallas_call(solve_kernel, out_shape=jax.ShapeDtypeStruct((3 * few, n),...  8.38 us
    dot_general x1, matrix products, on_device(): jnp.einsum('kib,kbf->kif', row_selector, narrowed, precision=HIGHEST)  3.63 us
    all_to_all x3, other arithmetic, exchange(): return lax.all_to_all(value, axes, split_axis=0, concat_axis=0, tiled=True)  3.59 us
  transfers between devices with their start and end apart: 3, of which 2 were waited for; matrix products, arithmetic and copies ran while one was open for 5% of the time, Pallas kernels for 5%

profile of v3, /device:TPU:1, one launch (start us, length us, event | category | flops | bytes accessed | tf_op | source)
XLA Modules:
  0.0 175.5 jit_solution(2766835682138556224)
XLA Ops:
  6.5 0.6 broadcast.97
  7.1 2.8 %reduce.1 = bf16[8,12288]{1,0:T(8,128)(2,1)S(1)} reduce(bf16[8,1,12288]{2,1,0:T(2,128)(2,1)} %bitcast.40, bf16[]{:T(256)} %broadcast.97), dimensions={1}, to_apply=%bitcast.reduce_sub_computation | reduce | bytes 393218 | tf_op jit(solution)/shard_map/all_to_all | solution.py:101
  9.9 0.1 reshape.75
  10.1 15.2 %all_to_all.46 = bf16[8,2,6144]{2,1,0:T(2,128)(2,1)S(1)} all-to-all(bf16[8,2,6144]{2,1,0:T(2,128)(2,1)S(1)} %reshape.75), channel_id=1, replica_groups=mesh['x'=4,'z'=16,'c'=2,'r'=4] {'x','c'}, dimensions={0} | all-to-all | bytes 393216 | tf_op jit(solution)/shard_map/all_to_all | solution.py:101
  25.2 0.2 reshape.76
  25.4 0.9 copy.29
  26.3 0.0 all-gather.2.cloned.1.call-update
  26.4 1.2 reduce
  27.5 0.1 reshape.63
  27.6 14.3 %all-to-all-start.1 = ((bf16[128,8,128]{2,1,0:T(8,128)(2,1)}), bf16[128,8,128]{2,1,0:T(8,128)(2,1)S(1)}, u32[]{:S(2)}, u32[]{:S(2)}) async-start(bf16[128,8,128]{2,1,0:T(8,128)(2,1)} %bitcast.2), calls=%async_computation.1 | async-start | bytes 524288 | tf_op jit(solution)/shard_map/all_to_all | solution.py:101
  42.0 0.2 fusion.30
  42.1 12.9 %all_gather.6 = bf16[1024,384]{1,0:T(8,128)(2,1)S(1)} all-gather(bf16[256,384]{1,0:T(8,128)(2,1)S(1)} %reshape.63), channel_id=1, replica_groups=mesh['x'=4,'z'=16,'c'=2,'r'=4] {'r'}, dimensions={0}, use_global_device_ids=true | all-gather | bytes 983040 | tf_op jit(solution)/shard_map/all_gather | solution.py:134
  55.1 1.5 fusion.18
  56.6 8.2 %all-to-all-done.1 = bf16[128,8,128]{2,1,0:T(8,128)(2,1)S(1)} async-done(((bf16[128,8,128]{2,1,0:T(8,128)(2,1)}), bf16[128,8,128]{2,1,0:T(8,128)(2,1)S(1)}, u32[]{:S(2)}, u32[]{:S(2)}) %all-to-all-start.1) | async-done | bytes 262176 | tf_op jit(solution)/shard_map/all_to_all | solution.py:101
  64.8 0.1 multiply_reduce_fusion
  65.0 0.0 copy-start.5
  65.0 1.5 fusion.20
  66.6 0.7 fusion.50
  67.3 3.6 %multiply_reduce_fusion.1 = (f32[]{:T(128)}, f32[2,512,128]{2,1,0:T(8,128)S(1)}, bf16[2,512,128]{2,1,0:T(8,128)(2,1)}) fusion(bf16[1,2,512,128]{3,2,1,0:T(8,128)(2,1)} %param.18, f32[2,512,128]{2,1,0:T(8,128)} %param.19, bf16[2,512,128]{2,1,0:T(8,128)(2,1)} %param.17, f32[2,128,512]{2,1,0:T(8,128)S(1)} %fusion.50, s32[2,512]{1,0:T(2,128)S(1)} %copy-done.4), kind=kOutput, calls=%fused_computation.55 | convolution fusion | flops 807272448 | bytes 2363396 | tf_op jit(solution)/shard_map/kib,kbf->kif/dot_general | solution.py:152
  70.9 9.1 %all-to-all-start.2 = ((bf16[128,8,128]{2,1,0:T(8,128)(2,1)}), bf16[128,8,128]{2,1,0:T(8,128)(2,1)S(1)}, u32[]{:S(2)}, u32[]{:S(2)}) async-start(bf16[128,8,128]{2,1,0:T(8,128)(2,1)} %bitcast.4), calls=%async_computation.2 | async-start | bytes 524288 | tf_op jit(solution)/shard_map/all_to_all | solution.py:101
  80.6 22.6 %all-to-all-done.2 = bf16[128,8,128]{2,1,0:T(8,128)(2,1)S(1)} async-done(((bf16[128,8,128]{2,1,0:T(8,128)(2,1)}), bf16[128,8,128]{2,1,0:T(8,128)(2,1)S(1)}, u32[]{:S(2)}, u32[]{:S(2)}) %all-to-all-start.2) | async-done | bytes 262176 | tf_op jit(solution)/shard_map/all_to_all | solution.py:101
  103.2 0.1 fusion.36
  103.3 0.3 fusion.23
  103.7 16.5 %all_to_all.47 = f32[32,8,128]{2,1,0:T(8,128)S(1)} all-to-all(f32[32,8,128]{2,1,0:T(8,128)S(1)} %fusion.23), channel_id=1, replica_groups=mesh['x'=4,'z'=16,'c'=2,'r'=4] {'x','c','r'}, dimensions={0} | all-to-all | bytes 262144 | tf_op jit(solution)/shard_map/all_to_all | solution.py:101
  120.2 14.2 %all_to_all.48 = f32[16,8,128]{2,1,0:T(8,128)S(1)} all-to-all(f32[16,8,128]{2,1,0:T(8,128)S(1)} %broadcast_in_dim.14), channel_id=1, replica_groups=mesh['x'=4,'z'=16,'c'=2,'r'=4] {'z'}, dimensions={0} | all-to-all | bytes 131072 | tf_op jit(solution)/shard_map/all_to_all | solution.py:101
  134.5 12.7 %all_to_all.49 = f32[32,8,128]{2,1,0:T(8,128)S(1)} all-to-all(f32[32,8,128]{2,1,0:T(8,128)S(1)} %broadcast_in_dim.15), channel_id=1, replica_groups=mesh['x'=4,'z'=16,'c'=2,'r'=4] {'x','c','r'}, dimensions={0} | all-to-all | bytes 262144 | tf_op jit(solution)/shard_map/all_to_all | solution.py:101
  147.2 8.4 %shard_map.100 = f32[24,128]{1,0:T(8,128)S(1)} custom-call(s32[1]{0:T(128)} %bitcast.1.first_ref, f32[256,128]{1,0:T(8,128)S(1)} %bitcast.37), custom_call_target="tpu_custom_call" | custom-call | flops 40000000 | bytes 200000 | tf_op jit(solution)/shard_map/pallas_call | solution.py:87
  155.5 2.5 %fusion.17 = f32[8,12288]{1,0:T(8,128)S(1)} fusion(bf16[128,12288]{1,0:T(8,128)(2,1)} %all-gather.2.cloned.1.call-done, f32[24,128]{1,0:T(8,128)S(1)} %shard_map.100), kind=kOutput, calls=%fused_computation.21 | convolution fusion | flops 75697152 | bytes 3551232 | tf_op jit(solution)/shard_map/dot_general | solution.py:175
  158.1 0.7 reduce.2
  158.8 0.1 reshape.77
  158.9 8.8 %all_to_all.50 = bf16[8,2,6144]{2,1,0:T(2,128)(2,1)S(1)} all-to-all(bf16[8,2,6144]{2,1,0:T(2,128)(2,1)S(1)} %reshape.77), channel_id=1, replica_groups=mesh['x'=4,'z'=16,'c'=2,'r'=4] {'x','c'}, dimensions={0} | all-to-all | bytes 393216 | tf_op jit(solution)/shard_map/all_to_all | solution.py:101
  167.7 0.9 reshape.78
  (27 shorter events, 0.2 us)
Async XLA Ops:
  6.5 48.6 %copy-start = (bf16[384,1024]{1,0:T(8,128)(2,1)S(1)}, bf16[384,1024]{1,0:T(8,128)(2,1)}, u32[]{:S(2)}) copy-start(bf16[384,1024]{1,0:T(8,128)(2,1)} %param.14) | copy-start | bytes 2359300
  6.5 19.8 %copy-start.2 = (bf16[1,98304]{1,0:T(2,128)(2,1)S(1)}, bf16[1,98304]{1,0:T(2,128)(2,1)}, u32[]{:S(2)}) copy-start(bf16[1,98304]{1,0:T(2,128)(2,1)} %param.16) | copy-start | bytes 589828
  6.5 149.0 %all-gather.2.cloned.1.call-start = ((), (), s32[]{:S(2)}) async-start(), calls=%async_computation.7 | async-start | bytes 3342336 | tf_op jit(solution)/shard_map/all_gather | solution.py:139
  7.1 34.9 %copy-start.3 = (bf16[512,384]{1,0:T(8,128)(2,1)S(1)}, bf16[512,384]{1,0:T(8,128)(2,1)}, u32[]{:S(2)}) copy-start(bf16[512,384]{1,0:T(8,128)(2,1)} %param.10) | copy-start | bytes 1179652
  25.2 29.9 %copy-start.6 = (f32[1024]{0:T(1024)S(1)}, f32[1024]{0:T(1024)}, u32[]{:S(2)}) copy-start(f32[1024]{0:T(1024)} %param.15) | copy-start | bytes 12292
  25.2 29.9 %copy-start.7 = (f32[384]{0:T(512)S(1)}, f32[384]{0:T(512)}, u32[]{:S(2)}) copy-start(f32[384]{0:T(512)} %param.13) | copy-start | bytes 4612
  27.6 37.2 %all-to-all-start.1 = ((bf16[128,8,128]{2,1,0:T(8,128)(2,1)}), bf16[128,8,128]{2,1,0:T(8,128)(2,1)S(1)}, u32[]{:S(2)}, u32[]{:S(2)}) async-start(bf16[128,8,128]{2,1,0:T(8,128)(2,1)} %bitcast.2), calls=%async_computation.1 | async-start | bytes 524288 | tf_op jit(solution)/shard_map/all_to_all | solution.py:101
  65.0 1.6 copy-start.5
  65.0 2.2 %copy-start.4 = (s32[2,512]{1,0:T(2,128)S(1)}, s32[2,512]{1,0:T(2,128)}, u32[]{:S(2)}) copy-start(s32[2,512]{1,0:T(2,128)} %param.11) | copy-start | bytes 12292
  70.9 32.3 %all-to-all-start.2 = ((bf16[128,8,128]{2,1,0:T(8,128)(2,1)}), bf16[128,8,128]{2,1,0:T(8,128)(2,1)S(1)}, u32[]{:S(2)}, u32[]{:S(2)}) async-start(bf16[128,8,128]{2,1,0:T(8,128)(2,1)} %bitcast.4), calls=%async_computation.2 | async-start | bytes 524288 | tf_op jit(solution)/shard_map/all_to_all | solution.py:101
  134.5 23.6 %copy-start.1 = (bf16[8,1,12288]{2,0,1:T(8,128)(2,1)S(1)}, bf16[8,1,12288]{2,0,1:T(8,128)(2,1)}, u32[]{:S(2)}) copy-start(bf16[8,1,12288]{2,0,1:T(8,128)(2,1)} %copy.29) | copy-start | bytes 589828
Sparse Core Ops, SparseCore 0:
  26.5 86.3 all-gather.1

commit v4 on v3

--- a/solution.py
+++ b/solution.py
@@ -131,17 +131,15 @@
     step_count, rows = batch_index.shape
     picked = obs_pick.shape[1]
     own = member_params.reshape(-1, features)
+    few = lax.axis_size(PAIR)
+    piece = exchange(own.reshape(few, -1, features), PAIR)
     weights = lax.all_gather(own, "r", axis=0, tiled=True)
-    few = lax.axis_size(PAIR)
-    piece = exchange(member_params.reshape(few, -1), PAIR)
-    perturbation, piece = lax.optimization_barrier((perturbation, piece))
-    noise = exchange(perturbation.reshape(members, -1, picked), MEM)
+    piece, weights = lax.optimization_barrier((piece, weights))
+    piece = piece.reshape(few, -1)
     everyone = lax.all_gather(piece, "z", axis=0, tiled=True)
     step_scale = DT * width ** (-0.5)
     current = states.astype(jnp.float32)
-    for turn in range(2):
-        if turn:
-            current, noise = lax.optimization_barrier((current, noise))
+    for _ in range(2):
         layer = hidden_layer(current, norm_gain, w_in, b_in)
         current = current + step_scale * jnp.dot(layer, weights, preferred_element_type=jnp.float32)
     feature_ids = lax.broadcasted_iota(jnp.int32, (step_count, features, picked), 1)
@@ -151,17 +149,18 @@
     narrowed = jnp.einsum("bs,ksf->kbf", current, selector, precision=HIGHEST)
     predicted = jnp.einsum("kib,kbf->kif", row_selector, narrowed, precision=HIGHEST)
     scaled = predicted * inv_sigma
-    aim = observed.astype(jnp.float32) * inv_sigma
     weighted = scaled.astype(jnp.bfloat16)
-    misfit_w = (aim + perturbation[0].astype(jnp.float32) - scaled).astype(jnp.bfloat16)
+    misfit_w = (
+        observed.astype(jnp.float32) * inv_sigma + perturbation[0].astype(jnp.float32) - scaled
+    ).astype(jnp.bfloat16)
     misfit_local = jnp.sum(jnp.square(misfit_w.astype(jnp.float32)))
     entries = members * step_count * rows * lax.axis_size("r") * picked
-    gathered = exchange(weighted.reshape(members, -1, picked), MEM).astype(jnp.float32)
-    depth = gathered.shape[1]
-    place = lax.axis_index(MEM) * depth
-    aim_here = lax.dynamic_slice_in_dim(aim.reshape(-1, picked), place, depth, 0)
+    sent = jnp.concatenate(
+        [weighted.reshape(members, -1, picked), misfit_w.reshape(members, -1, picked)], axis=1
+    )
+    gathered, misfit_here = jnp.split(exchange(sent, MEM), 2, axis=1)
+    gathered = gathered.astype(jnp.float32)
     anomaly = (gathered - jnp.mean(gathered, axis=0)).astype(jnp.bfloat16)
-    misfit_here = (aim_here + noise.astype(jnp.float32) - gathered).astype(jnp.bfloat16)
     both = jnp.concatenate([anomaly, misfit_here], axis=0)
     partial = lax.dot_general(
         both, anomaly, (((1, 2), (1, 2)), ((), ())), preferred_element_type=jnp.float32

time: 176 us -> 173 us (0.983)
  blocking collectives: 80.3 us -> 50.9 us
  waiting for transfers between devices: 30.8 us -> 44.4 us
  starting transfers between devices: 23.4 us -> 32.9 us
  matrix products: 10.1 us -> 11.9 us
    all_to_all x5 -> x3, blocking collectives: 67.4 us -> 39.3 us  [exchange(): return lax.all_to_all(value, axes, split_axis=0, concat_axis=0, tiled=True)]
    all_to_all x2 -> x3, waiting for transfers between devices: 30.8 us -> 44.4 us  [exchange(): return lax.all_to_all(value, axes, split_axis=0, concat_axis=0, tiled=True)]
    all_to_all x2 -> x3, starting transfers between devices: 23.4 us -> 32.9 us  [exchange(): return lax.all_to_all(value, axes, split_axis=0, concat_axis=0, tiled=True)]
    all_to_all x3 -> x0, other arithmetic: 3.59 us -> none  [exchange(): return lax.all_to_all(value, axes, split_axis=0, concat_axis=0, tiled=True)]
    dot_general x2, matrix products: 3.07 us -> 5.68 us  [on_device(): jnp.dot(layer, weights, preferred_element_type=jnp.float32)]
    convert_element_type x1 -> x3, other arithmetic: 0.12 us -> 2.28 us  [the longest x2 2.23 us: on_device(): renewed = (piece.astype(jnp.float32) + change).astype(jnp.bfloat16)]
  transfers between devices with their start and end apart: 3 -> 4, of which waited for: 2 -> 2; matrix products, arithmetic and copies ran while one was open for 5% -> 7% of each run, Pallas kernels for 5% -> 5%
where the time goes in v4:
time: 173 us
  blocking collectives  50.9 us (29%)
  waiting for transfers between devices  44.4 us (26%)
  starting transfers between devices  32.9 us (19%)
  between operations  14.2 us (8%)
  matrix products  11.9 us (7%)
  Pallas kernels  8.38 us (5%)
  other arithmetic  5.55 us (3%)
  local copies, waits for them, and re-layouts  4.52 us (3%)
    all_to_all x3, waiting for transfers between devices, exchange(): return lax.all_to_all(value, axes, split_axis=0, concat_axis=0, tiled=True)  44.4 us
    all_to_all x3, blocking collectives, exchange(): return lax.all_to_all(value, axes, split_axis=0, concat_axis=0, tiled=True)  39.3 us
    all_to_all x3, starting transfers between devices, exchange(): return lax.all_to_all(value, axes, split_axis=0, concat_axis=0, tiled=True)  32.9 us
    all_gather x1, blocking collectives, on_device(): weights = lax.all_gather(own, 'r', axis=0, tiled=True)  11.6 us
    pallas_call x1, Pallas kernels, centred_coefficients(): pl.pallas_call(solve_kernel, out_shape=jax.ShapeDtypeStruct((3 * few, n),...  8.38 us
    dot_general x2, matrix products, on_device(): jnp.dot(layer, weights, preferred_element_type=jnp.float32)  5.68 us
  transfers between devices with their start and end apart: 4, of which 2 were waited for; matrix products, arithmetic and copies ran while one was open for 7% of the time, Pallas kernels for 5%

profile of v4, /device:TPU:1, one launch (start us, length us, event | category | flops | bytes accessed | tf_op | source)
XLA Modules:
  0.0 172.8 jit_solution(7217072712755162548)
XLA Ops:
  6.5 2.2 %reduce = bf16[98304]{0:T(1024)(128)(2,1)S(1)} reduce(bf16[1,98304]{1,0:T(2,128)(2,1)} %param.16, bf16[]{:T(256)} %constant.31), dimensions={0}, to_apply=%param.16.reduce_sub_computation | reduce | bytes 393218 | tf_op args[6]
  8.7 0.8 reshape_reshape.3
  9.5 10.2 %all-to-all-start = ((bf16[8,32,384]{2,1,0:T(8,128)(2,1)}), bf16[8,32,384]{2,1,0:T(8,128)(2,1)S(1)}, u32[]{:S(2)}, u32[]{:S(2)}) async-start(bf16[8,32,384]{2,1,0:T(8,128)(2,1)} %reshape_reshape.3), calls=%async_computation | async-start | bytes 393216 | tf_op jit(solution)/shard_map/all_to_all | solution.py:101
  19.7 0.1 reshape.79
  19.8 11.6 %all_gather.6 = bf16[1024,384]{1,0:T(8,128)(2,1)S(1)} all-gather(bf16[256,384]{1,0:T(8,128)(2,1)S(1)} %reshape.79), channel_id=1, replica_groups=mesh['x'=4,'z'=16,'c'=2,'r'=4] {'r'}, dimensions={0}, use_global_device_ids=true | all-gather | bytes 983040 | tf_op jit(solution)/shard_map/all_gather | solution.py:136
  31.4 0.7 copy.27
  32.2 0.0 all-gather.2.cloned.1.call-update
  32.2 0.2 copy.17
  32.4 0.1 fusion.30
  32.6 2.6 %multiply_reduce_fusion = (f32[512]{0:T(512)S(1)}, f32[512,384]{0,1:T(8,128)}) fusion(bf16[1024,384]{1,0:T(8,128)(2,1)S(1)} %all_gather.6, bf16[384,1024]{1,0:T(8,128)(2,1)S(1)} %copy-done, f32[1024]{0:T(1024)S(1)} %copy-done.4, bf16[512,384]{0,1:T(8,128)(2,1)S(1)} %copy.17, f32[384]{0:T(512)S(1)} %copy-done.6, f32[512]{0:T(512)S(1)} %add_rsqrt_fusion.1), kind=kOutput, calls=%fused_computation.43 | convolution fusion | flops 812318208 | bytes 2762240 | tf_op jit(solution)/shard_map/dot_general | solution.py:144
  35.2 3.1 %fusion.20 = f32[512,384,1]{0,1,2:T(8,128)S(1)} fusion(f32[512,384]{0,1:T(8,128)} %get-tuple-element.15, bf16[1024,384]{1,0:T(8,128)(2,1)S(1)} %all_gather.6, bf16[384,1024]{1,0:T(8,128)(2,1)S(1)} %copy-done, f32[1024]{0:T(1024)S(1)} %copy-done.4, f32[512]{0:T(512)S(1)} %add_rsqrt_fusion, f32[384]{0:T(512)S(1)} %copy-done.6), kind=kOutput, calls=%fused_computation.26 | convolution fusion | flops 811532288 | bytes 3153408 | tf_op jit(solution)/shard_map/dot_general | solution.py:144
  38.3 0.7 fusion.49
  39.0 2.8 %multiply_reduce_fusion.1 = (f32[]{:T(128)}, bf16[2,512,128]{2,1,0:T(8,128)(2,1)S(1)}, bf16[2,512,128]{2,1,0:T(8,128)(2,1)S(1)}) fusion(bf16[1,2,512,128]{3,2,1,0:T(8,128)(2,1)} %param.18, f32[2,512,128]{2,1,0:T(8,128)S(1)} %copy-done.3, bf16[2,512,128]{2,1,0:T(8,128)(2,1)} %param.17, f32[2,128,512]{2,1,0:T(8,128)S(1)} %fusion.49, s32[2,512]{1,0:T(2,128)S(1)} %copy-done.5), kind=kOutput, calls=%fused_computation.54 | convolution fusion | flops 807272448 | bytes 2101252 | tf_op jit(solution)/shard_map/kib,kbf->kif/dot_general | solution.py:150
  41.8 0.9 pad_maximum_fusion
  42.7 17.4 %all-to-all-start.1 = ((bf16[128,16,128]{2,1,0:T(8,128)(2,1)}), bf16[128,16,128]{2,1,0:T(8,128)(2,1)S(1)}, u32[]{:S(2)}, u32[]{:S(2)}) async-start(bf16[128,16,128]{2,1,0:T(8,128)(2,1)} %pad_maximum_fusion), calls=%async_computation.1 | async-start | bytes 1048576 | tf_op jit(solution)/shard_map/all_to_all | solution.py:101
  60.7 37.2 %all-to-all-done.1 = bf16[128,16,128]{2,1,0:T(8,128)(2,1)S(1)} async-done(((bf16[128,16,128]{2,1,0:T(8,128)(2,1)}), bf16[128,16,128]{2,1,0:T(8,128)(2,1)S(1)}, u32[]{:S(2)}, u32[]{:S(2)}) %all-to-all-start.1) | async-done | bytes 524320 | tf_op jit(solution)/shard_map/all_to_all | solution.py:101
  98.0 0.1 fusion.35
  98.1 0.3 fusion.23
  98.4 16.0 %all_to_all.31 = f32[32,8,128]{2,1,0:T(8,128)S(1)} all-to-all(f32[32,8,128]{2,1,0:T(8,128)S(1)} %fusion.23), channel_id=1, replica_groups=mesh['x'=4,'z'=16,'c'=2,'r'=4] {'x','c','r'}, dimensions={0} | all-to-all | bytes 262144 | tf_op jit(solution)/shard_map/all_to_all | solution.py:101
  114.5 14.5 %all_to_all.32 = f32[16,8,128]{2,1,0:T(8,128)S(1)} all-to-all(f32[16,8,128]{2,1,0:T(8,128)S(1)} %broadcast_in_dim.14), channel_id=1, replica_groups=mesh['x'=4,'z'=16,'c'=2,'r'=4] {'z'}, dimensions={0} | all-to-all | bytes 131072 | tf_op jit(solution)/shard_map/all_to_all | solution.py:101
  129.0 0.7 broadcast_in_dim.15
  129.6 5.3 %all-to-all-start.4 = ((f32[32,8,128]{2,1,0:T(8,128)}), f32[32,8,128]{2,1,0:T(8,128)S(1)}, u32[]{:S(2)}, u32[]{:S(2)}) async-start(f32[32,8,128]{2,1,0:T(8,128)} %broadcast_in_dim.15), calls=%async_computation.4 | async-start | bytes 262144 | tf_op jit(solution)/shard_map/all_to_all | solution.py:101
  134.9 0.4 reshape.88
  135.3 7.2 %all-to-all-done.4 = f32[32,8,128]{2,1,0:T(8,128)S(1)} async-done(((f32[32,8,128]{2,1,0:T(8,128)}), f32[32,8,128]{2,1,0:T(8,128)S(1)}, u32[]{:S(2)}, u32[]{:S(2)}) %all-to-all-start.4) | async-done | bytes 131104 | tf_op jit(solution)/shard_map/all_to_all | solution.py:101
  142.5 8.4 %shard_map.100 = f32[24,128]{1,0:T(8,128)S(1)} custom-call(s32[1]{0:T(128)} %bitcast.first_ref, f32[256,128]{1,0:T(8,128)S(1)} %bitcast.33), custom_call_target="tpu_custom_call" | custom-call | flops 40000000 | bytes 200000 | tf_op jit(solution)/shard_map/pallas_call | solution.py:87
  150.9 2.5 %fusion.17 = f32[8,12288]{1,0:T(8,128)S(1)} fusion(bf16[128,12288]{1,0:T(8,128)(2,1)} %all-gather.2.cloned.1.call-done, f32[24,128]{1,0:T(8,128)S(1)} %shard_map.100), kind=kOutput, calls=%fused_computation.21 | convolution fusion | flops 75697152 | bytes 3551232 | tf_op jit(solution)/shard_map/dot_general | solution.py:174
  153.4 0.4 add_convert_fusion
  153.8 0.5 broadcast.105
  154.3 1.8 %reduce.2 = bf16[8,12288]{1,0:T(8,128)(2,1)S(1)} reduce(bf16[8,1,12288]{2,1,0:T(2,128)(2,1)S(1)} %add_convert_fusion, bf16[]{:T(256)} %broadcast.105), dimensions={1}, to_apply=%add_convert_fusion.reduce_sub_computation | reduce | bytes 393218 | tf_op jit(solution)/shard_map/convert_element_type | solution.py:176
  156.1 0.1 reshape.94
  156.2 8.8 %all_to_all.33 = bf16[8,2,6144]{2,1,0:T(2,128)(2,1)S(1)} all-to-all(bf16[8,2,6144]{2,1,0:T(2,128)(2,1)S(1)} %reshape.94), channel_id=1, replica_groups=mesh['x'=4,'z'=16,'c'=2,'r'=4] {'x','c'}, dimensions={0} | all-to-all | bytes 393216 | tf_op jit(solution)/shard_map/all_to_all | solution.py:101
  165.0 0.9 reshape.95
  (26 shorter events, 0.2 us)
Async XLA Ops:
  6.5 26.0 %copy-start = (bf16[384,1024]{1,0:T(8,128)(2,1)S(1)}, bf16[384,1024]{1,0:T(8,128)(2,1)}, u32[]{:S(2)}) copy-start(bf16[384,1024]{1,0:T(8,128)(2,1)} %param.14) | copy-start | bytes 2359300
  6.5 25.7 %copy-start.1 = (bf16[512,384]{1,0:T(8,128)(2,1)S(1)}, bf16[512,384]{1,0:T(8,128)(2,1)}, u32[]{:S(2)}) copy-start(bf16[512,384]{1,0:T(8,128)(2,1)} %param.10) | copy-start | bytes 1179652
  8.7 23.8 %copy-start.4 = (f32[1024]{0:T(1024)S(1)}, f32[1024]{0:T(1024)}, u32[]{:S(2)}) copy-start(f32[1024]{0:T(1024)} %param.15) | copy-start | bytes 12292
  8.7 23.8 %copy-start.6 = (f32[384]{0:T(512)S(1)}, f32[384]{0:T(512)}, u32[]{:S(2)}) copy-start(f32[384]{0:T(512)} %param.13) | copy-start | bytes 4612
  9.5 21.9 %all-to-all-start = ((bf16[8,32,384]{2,1,0:T(8,128)(2,1)}), bf16[8,32,384]{2,1,0:T(8,128)(2,1)S(1)}, u32[]{:S(2)}, u32[]{:S(2)}) async-start(bf16[8,32,384]{2,1,0:T(8,128)(2,1)} %reshape_reshape.3), calls=%async_computation | async-start | bytes 393216 | tf_op jit(solution)/shard_map/all_to_all | solution.py:101
  19.7 131.2 %all-gather.2.cloned.1.call-start = ((), (), s32[]{:S(2)}) async-start(), calls=%async_computation.6 | async-start | bytes 3342336 | tf_op jit(solution)/shard_map/all_gather | solution.py:139
  35.1 3.1 %copy-start.2 = (s32[2,128]{1,0:T(2,128)S(1)}, s32[2,128]{1,0:T(2,128)}, u32[]{:S(2)}) copy-start(s32[2,128]{1,0:T(2,128)} %param.12) | copy-start | bytes 3076
  35.1 3.8 %copy-start.3 = (f32[2,512,128]{2,1,0:T(8,128)S(1)}, f32[2,512,128]{2,1,0:T(8,128)}, u32[]{:S(2)}) copy-start(f32[2,512,128]{2,1,0:T(8,128)} %param.19) | copy-start | bytes 1572868
  35.2 3.8 %copy-start.5 = (s32[2,512]{1,0:T(2,128)S(1)}, s32[2,512]{1,0:T(2,128)}, u32[]{:S(2)}) copy-start(s32[2,512]{1,0:T(2,128)} %param.11) | copy-start | bytes 12292
  42.7 55.2 %all-to-all-start.1 = ((bf16[128,16,128]{2,1,0:T(8,128)(2,1)}), bf16[128,16,128]{2,1,0:T(8,128)(2,1)S(1)}, u32[]{:S(2)}, u32[]{:S(2)}) async-start(bf16[128,16,128]{2,1,0:T(8,128)(2,1)} %pad_maximum_fusion), calls=%async_computation.1 | async-start | bytes 1048576 | tf_op jit(solution)/shard_map/all_to_all | solution.py:101
  129.6 12.9 %all-to-all-start.4 = ((f32[32,8,128]{2,1,0:T(8,128)}), f32[32,8,128]{2,1,0:T(8,128)S(1)}, u32[]{:S(2)}, u32[]{:S(2)}) async-start(f32[32,8,128]{2,1,0:T(8,128)} %broadcast_in_dim.15), calls=%async_computation.4 | async-start | bytes 262144 | tf_op jit(solution)/shard_map/all_to_all | solution.py:101
Sparse Core Ops, SparseCore 0:
  32.3 90.7 all-gather.1

commit v5 on v2

--- a/solution.py
+++ b/solution.py
@@ -8,7 +8,8 @@
 
 EPS = 1e-06
 DT = 0.5
-MEM = ("x", "z", "c")
+MEM = ("z", "x", "c")
+OWNERS = ("x", "z", "c")
 NEAR = ("x", "c", "r")
 BLOCK = 8
 HIGHEST = lax.Precision.HIGHEST
@@ -119,13 +120,12 @@
     picked = obs_pick.shape[1]
     own = member_params.reshape(-1, features)
     weights = lax.all_gather(own, "r", axis=0, tiled=True)
-    noise = exchange(perturbation.reshape(members, -1, picked), MEM)
     param_block = exchange(own.reshape(members, -1, features), MEM)
     step_scale = DT * width ** (-0.5)
     current = states.astype(jnp.float32)
     for turn in range(2):
         if turn:
-            current, noise = lax.optimization_barrier((current, noise))
+            current, param_block = lax.optimization_barrier((current, param_block))
         layer = hidden_layer(current, norm_gain, w_in, b_in)
         current = current + step_scale * jnp.dot(layer, weights, preferred_element_type=jnp.float32)
     feature_ids = lax.broadcasted_iota(jnp.int32, (step_count, features, picked), 1)
@@ -135,17 +135,18 @@
     narrowed = jnp.einsum("bs,ksf->kbf", current, selector, precision=HIGHEST)
     predicted = jnp.einsum("kib,kbf->kif", row_selector, narrowed, precision=HIGHEST)
     scaled = predicted * inv_sigma
-    aim = observed.astype(jnp.float32) * inv_sigma
     weighted = scaled.astype(jnp.bfloat16)
-    misfit_w = (aim + perturbation[0].astype(jnp.float32) - scaled).astype(jnp.bfloat16)
+    misfit_w = (
+        observed.astype(jnp.float32) * inv_sigma + perturbation[0].astype(jnp.float32) - scaled
+    ).astype(jnp.bfloat16)
     misfit_local = jnp.sum(jnp.square(misfit_w.astype(jnp.float32)))
     entries = members * step_count * rows * lax.axis_size("r") * picked
-    gathered = exchange(weighted.reshape(members, -1, picked), MEM).astype(jnp.float32)
-    depth = gathered.shape[1]
-    place = lax.axis_index(MEM) * depth
-    aim_here = lax.dynamic_slice_in_dim(aim.reshape(-1, picked), place, depth, 0)
+    sent = jnp.concatenate(
+        [weighted.reshape(members, -1, picked), misfit_w.reshape(members, -1, picked)], axis=1
+    )
+    gathered, misfit_here = jnp.split(exchange(sent, MEM), 2, axis=1)
+    gathered = gathered.astype(jnp.float32)
     anomaly = (gathered - jnp.mean(gathered, axis=0)).astype(jnp.bfloat16)
-    misfit_here = (aim_here + noise.astype(jnp.float32) - gathered).astype(jnp.bfloat16)
     both = jnp.concatenate([anomaly, misfit_here], axis=0)
     partial = lax.dot_general(
         both, anomaly, (((1, 2), (1, 2)), ((), ())), preferred_element_type=jnp.float32
@@ -171,11 +172,11 @@
         P(),
         P(),
         P(),
-        P(MEM, "r"),
+        P(OWNERS, "r"),
         P(None, "r", None),
-        P(MEM, None, "r", None),
+        P(OWNERS, None, "r", None),
         P(None, "r", None),
     )
     return jax.shard_map(
-        on_device, mesh=fine, in_specs=placed, out_specs=P(MEM, "r"), check_vma=False
+        on_device, mesh=fine, in_specs=placed, out_specs=P(OWNERS, "r"), check_vma=False
     )

time: 181 us -> 170 us (0.939)
  waiting for transfers between devices: 47.1 us -> 33.4 us
  blocking collectives: 68.7 us -> 79.9 us
  starting transfers between devices: 42.6 us -> 34.5 us
  other arithmetic: 1.68 us -> 3.5 us
    all_to_all x4 -> x2, waiting for transfers between devices: 47.1 us -> 33.4 us  [exchange(): return lax.all_to_all(value, axes, split_axis=0, concat_axis=0, tiled=True)]
    all_to_all x3 -> x4, blocking collectives: 55.9 us -> 67 us  [exchange(): return lax.all_to_all(value, axes, split_axis=0, concat_axis=0, tiled=True)]
    all_to_all x4 -> x2, starting transfers between devices: 42.6 us -> 34.5 us  [exchange(): return lax.all_to_all(value, axes, split_axis=0, concat_axis=0, tiled=True)]
  transfers between devices with their start and end apart: 4 -> 2, of which waited for: 4 -> 2; matrix products, arithmetic and copies ran while one was open for 2% -> 1% of each run, Pallas kernels for 5% -> 0%
where the time goes in v5:
time: 170 us; the launch traced here: 169 us
  blocking collectives  79.9 us (47%)
  starting transfers between devices  34.5 us (20%)
  waiting for transfers between devices  33.4 us (20%)
  Pallas kernels  8.32 us (5%)
  matrix products  6.16 us (4%)
  other arithmetic  3.5 us (2%)
  local copies, waits for them, and re-layouts  2.59 us (2%)
    all_to_all x4, blocking collectives, exchange(): return lax.all_to_all(value, axes, split_axis=0, concat_axis=0, tiled=True)  67 us
    all_to_all x2, starting transfers between devices, exchange(): return lax.all_to_all(value, axes, split_axis=0, concat_axis=0, tiled=True)  34.5 us
    all_to_all x2, waiting for transfers between devices, exchange(): return lax.all_to_all(value, axes, split_axis=0, concat_axis=0, tiled=True)  33.4 us
    all_gather x1, blocking collectives, on_device(): weights = lax.all_gather(own, 'r', axis=0, tiled=True)  12.8 us
    pallas_call x1, Pallas kernels, centred_coefficients(): pl.pallas_call(solve_kernel, out_shape=jax.ShapeDtypeStruct((n, n), jnp.f...  8.32 us
  transfers between devices with their start and end apart: 2, of which 2 were waited for; matrix products, arithmetic and copies ran while one was open for 1% of the time, Pallas kernels for 0%

profile of v5, /device:TPU:1, one launch (start us, length us, event | category | flops | bytes accessed | tf_op | source)
XLA Modules:
  0.0 169.2 jit_solution(1951194331427336560)
XLA Ops:
  0.0 2.2 %reduce = bf16[98304]{0:T(1024)(128)(2,1)S(1)} reduce(bf16[1,98304]{1,0:T(2,128)(2,1)} %param.16, bf16[]{:T(256)} %constant.25), dimensions={0}, to_apply=%param.16.reduce_sub_computation | reduce | bytes 393218 | tf_op args[6]
  2.2 0.8 reshape_reshape.3
  3.0 20.4 %all-to-all-start = ((bf16[128,2,384]{2,1,0:T(2,128)(2,1)}), bf16[128,2,384]{2,1,0:T(2,128)(2,1)S(1)}, u32[]{:S(2)}, u32[]{:S(2)}) async-start(bf16[128,2,384]{2,1,0:T(2,128)(2,1)} %reshape_reshape.3), calls=%async_computation | async-start | bytes 393216 | tf_op jit(solution)/shard_map/all_to_all | solution.py:89
  23.4 0.2 fusion.30
  23.5 0.0 copy-start.8
  23.6 0.1 reshape.45
  23.7 12.8 %all_gather.3 = bf16[1024,384]{1,0:T(8,128)(2,1)S(1)} all-gather(bf16[256,384]{1,0:T(8,128)(2,1)S(1)} %reshape.45), channel_id=1, replica_groups=mesh['x'=4,'z'=16,'c'=2,'r'=4] {'r'}, dimensions={0}, use_global_device_ids=true | all-gather | bytes 983040 | tf_op jit(solution)/shard_map/all_gather | solution.py:122
  36.5 1.5 fusion.17
  38.1 3.3 %all-to-all-done = bf16[128,2,384]{2,1,0:T(2,128)(2,1)S(1)} async-done(((bf16[128,2,384]{2,1,0:T(2,128)(2,1)}), bf16[128,2,384]{2,1,0:T(2,128)(2,1)S(1)}, u32[]{:S(2)}, u32[]{:S(2)}) %all-to-all-start) | async-done | bytes 196640 | tf_op jit(solution)/shard_map/all_to_all | solution.py:89
  41.3 0.1 multiply_reduce_fusion
  41.5 0.0 copy-start.2
  41.5 1.5 fusion.19
  43.1 0.0 copy-start.3
  43.1 0.0 copy-start.4
  43.1 0.7 fusion.49
  43.8 0.3 copy-done.3
  44.1 0.1 copy-done.4
  44.2 0.1 copy-done.5
  44.3 1.8 %multiply_reduce_fusion.1 = (f32[]{:T(128)}, bf16[2,512,128]{2,1,0:T(8,128)(2,1)S(1)}, bf16[2,512,128]{2,1,0:T(8,128)(2,1)S(1)}) fusion(bf16[1,2,512,128]{3,2,1,0:T(8,128)(2,1)S(1)} %copy-done.4, f32[2,512,128]{2,1,0:T(8,128)S(1)} %copy-done.3, bf16[2,512,128]{2,1,0:T(8,128)(2,1)S(1)} %copy-done.5, f32[2,128,512]{2,1,0:T(8,128)S(1)} %fusion.49, ...), kind=kOutput, calls=%fused_computation.54 | convolution fusion | flops 807272448 | bytes 2101252 | tf_op jit(solution)/shard_map/kib,kbf->kif/dot_general | solution.py:136
  46.0 0.9 pad_maximum_fusion
  46.9 14.1 %all-to-all-start.1 = ((bf16[128,16,128]{2,1,0:T(8,128)(2,1)}), bf16[128,16,128]{2,1,0:T(8,128)(2,1)S(1)}, u32[]{:S(2)}, u32[]{:S(2)}) async-start(bf16[128,16,128]{2,1,0:T(8,128)(2,1)} %pad_maximum_fusion), calls=%async_computation.1 | async-start | bytes 1048576 | tf_op jit(solution)/shard_map/all_to_all | solution.py:89
  61.6 30.2 %all-to-all-done.1 = bf16[128,16,128]{2,1,0:T(8,128)(2,1)S(1)} async-done(((bf16[128,16,128]{2,1,0:T(8,128)(2,1)}), bf16[128,16,128]{2,1,0:T(8,128)(2,1)S(1)}, u32[]{:S(2)}, u32[]{:S(2)}) %all-to-all-start.1) | async-done | bytes 524320 | tf_op jit(solution)/shard_map/all_to_all | solution.py:89
  91.9 0.1 fusion.35
  92.0 0.3 fusion.23
  92.3 16.8 %all_to_all.30 = f32[32,8,128]{2,1,0:T(8,128)S(1)} all-to-all(f32[32,8,128]{2,1,0:T(8,128)S(1)} %fusion.23), channel_id=1, replica_groups=mesh['x'=4,'z'=16,'c'=2,'r'=4] {'x','c','r'}, dimensions={0} | all-to-all | bytes 262144 | tf_op jit(solution)/shard_map/all_to_all | solution.py:89
  109.1 14.2 %all_to_all.31 = f32[16,8,128]{2,1,0:T(8,128)S(1)} all-to-all(f32[16,8,128]{2,1,0:T(8,128)S(1)} %broadcast_in_dim.14), channel_id=1, replica_groups=mesh['x'=4,'z'=16,'c'=2,'r'=4] {'z'}, dimensions={0} | all-to-all | bytes 131072 | tf_op jit(solution)/shard_map/all_to_all | solution.py:89
  123.4 12.8 %all_to_all.32 = f32[32,8,128]{2,1,0:T(8,128)S(1)} all-to-all(f32[32,8,128]{2,1,0:T(8,128)S(1)} %broadcast_in_dim.15), channel_id=1, replica_groups=mesh['x'=4,'z'=16,'c'=2,'r'=4] {'x','c','r'}, dimensions={0} | all-to-all | bytes 262144 | tf_op jit(solution)/shard_map/all_to_all | solution.py:89
  136.1 8.3 %shard_map.100 = f32[128,128]{1,0:T(8,128)S(1)} custom-call(f32[256,128]{1,0:T(8,128)S(1)} %bitcast.27), custom_call_target="tpu_custom_call" | custom-call | flops 40000000 | bytes 200000 | tf_op jit(solution)/shard_map/pallas_call | solution.py:80
  144.5 0.4 fusion.21
  144.8 0.2 copy.30
  145.0 23.3 %all_to_all.33 = bf16[128,2,384]{2,1,0:T(2,128)(2,1)S(1)} all-to-all(bf16[128,2,384]{2,1,0:T(2,128)(2,1)S(1)} %copy.30), channel_id=1, replica_groups=mesh['x'=4,'z'=16,'c'=2,'r'=4] {'z','x','c'}, dimensions={0} | all-to-all | bytes 393216 | tf_op jit(solution)/shard_map/all_to_all | solution.py:89
  168.3 0.9 reshape.50
  (21 shorter events, 0.2 us)
Async XLA Ops:
  0.0 36.5 %copy-start = (bf16[384,1024]{1,0:T(8,128)(2,1)S(1)}, bf16[384,1024]{1,0:T(8,128)(2,1)}, u32[]{:S(2)}) copy-start(bf16[384,1024]{1,0:T(8,128)(2,1)} %param.14) | copy-start | bytes 2359300
  0.0 23.4 %copy-start.1 = (bf16[512,384]{1,0:T(8,128)(2,1)S(1)}, bf16[512,384]{1,0:T(8,128)(2,1)}, u32[]{:S(2)}) copy-start(bf16[512,384]{1,0:T(8,128)(2,1)} %param.10) | copy-start | bytes 1179652
  3.0 38.4 %all-to-all-start = ((bf16[128,2,384]{2,1,0:T(2,128)(2,1)}), bf16[128,2,384]{2,1,0:T(2,128)(2,1)S(1)}, u32[]{:S(2)}, u32[]{:S(2)}) async-start(bf16[128,2,384]{2,1,0:T(2,128)(2,1)} %reshape_reshape.3), calls=%async_computation | async-start | bytes 393216 | tf_op jit(solution)/shard_map/all_to_all | solution.py:89
  23.5 13.0 %copy-start.6 = (f32[1024]{0:T(1024)S(1)}, f32[1024]{0:T(1024)}, u32[]{:S(2)}) copy-start(f32[1024]{0:T(1024)} %param.15) | copy-start | bytes 12292
  23.5 13.0 %copy-start.8 = (f32[384]{0:T(512)S(1)}, f32[384]{0:T(512)}, u32[]{:S(2)}) copy-start(f32[384]{0:T(512)} %param.13) | copy-start | bytes 4612
  41.5 1.6 copy-start.2
  43.1 1.0 copy-start.3
  43.1 1.1 copy-start.4
  43.1 1.2 copy-start.5
  43.1 1.2 copy-start.7
  46.9 44.9 %all-to-all-start.1 = ((bf16[128,16,128]{2,1,0:T(8,128)(2,1)}), bf16[128,16,128]{2,1,0:T(8,128)(2,1)S(1)}, u32[]{:S(2)}, u32[]{:S(2)}) async-start(bf16[128,16,128]{2,1,0:T(8,128)(2,1)} %pad_maximum_fusion), calls=%async_computation.1 | async-start | bytes 1048576 | tf_op jit(solution)/shard_map/all_to_all | solution.py:89

commit v6 on v5

--- a/solution.py
+++ b/solution.py
@@ -119,7 +119,17 @@
     step_count, rows = batch_index.shape
     picked = obs_pick.shape[1]
     own = member_params.reshape(-1, features)
-    weights = lax.all_gather(own, "r", axis=0, tiled=True)
+    ring = lax.axis_size("r")
+    blocks = [own]
+    for d in (1, 3, 2):
+        blocks.insert(
+            len(blocks) if d != 2 else 2,
+            lax.ppermute(own, "r", [((i + d) % ring, i) for i in range(ring)]),
+        )
+    weights = jnp.concatenate(blocks, axis=0)
+    turned = lax.axis_index("r") * own.shape[0]
+    w_in = lax.dynamic_slice_in_dim(jnp.concatenate([w_in, w_in], axis=1), turned, width, 1)
+    b_in = lax.dynamic_slice_in_dim(jnp.concatenate([b_in, b_in]), turned, width, 0)
     param_block = exchange(own.reshape(members, -1, features), MEM)
     step_scale = DT * width ** (-0.5)
     current = states.astype(jnp.float32)

time: 170 us -> 175 us (1.029)
  blocking collectives: 79.9 us -> 65 us
  waiting for transfers between devices: 33.4 us -> 45.2 us
  starting transfers between devices: 34.5 us -> 40.1 us
    all_gather x1 -> x0, blocking collectives: 12.8 us -> none  [on_device(): weights = lax.all_gather(own, 'r', axis=0, tiled=True)]
    all_to_all x2, waiting for transfers between devices: 33.4 us -> 45.2 us  [exchange(): return lax.all_to_all(value, axes, split_axis=0, concat_axis=0, tiled=True)]
    ppermute x0 -> x3, starting transfers between devices: none -> 11.5 us  [on_device(): lax.ppermute(own, 'r', [((i + d) % ring, i) for i in range(ring)])]
    all_to_all x2, starting transfers between devices: 34.5 us -> 28.5 us  [exchange(): return lax.all_to_all(value, axes, split_axis=0, concat_axis=0, tiled=True)]
    all_to_all x4, blocking collectives: 67 us -> 65 us  [exchange(): return lax.all_to_all(value, axes, split_axis=0, concat_axis=0, tiled=True)]
  transfers between devices with their start and end apart: 2 -> 5, of which waited for: 2 -> 2; matrix products, arithmetic and copies ran while one was open for 1% -> 2% of each run, Pallas kernels for 0% -> 0%
where the time goes in v6:
time: 175 us; the launch traced here: 174 us
  blocking collectives  65 us (37%)
  waiting for transfers between devices  45.2 us (26%)
  starting transfers between devices  40.1 us (23%)
  Pallas kernels  8.32 us (5%)
  matrix products  7.47 us (4%)
  local copies, waits for them, and re-layouts  3.55 us (2%)
  other arithmetic  3.54 us (2%)
    all_to_all x4, blocking collectives, exchange(): return lax.all_to_all(value, axes, split_axis=0, concat_axis=0, tiled=True)  65 us
    all_to_all x2, waiting for transfers between devices, exchange(): return lax.all_to_all(value, axes, split_axis=0, concat_axis=0, tiled=True)  45.2 us
    all_to_all x2, starting transfers between devices, exchange(): return lax.all_to_all(value, axes, split_axis=0, concat_axis=0, tiled=True)  28.5 us
    ppermute x3, starting transfers between devices, on_device(): lax.ppermute(own, 'r', [((i + d) % ring, i) for i in range(ring)])  11.5 us
    pallas_call x1, Pallas kernels, centred_coefficients(): pl.pallas_call(solve_kernel, out_shape=jax.ShapeDtypeStruct((n, n), jnp.f...  8.32 us
    dot_general x2, matrix products, on_device(): jnp.dot(layer, weights, preferred_element_type=jnp.float32)  4.35 us
  transfers between devices with their start and end apart: 5, of which 2 were waited for; matrix products, arithmetic and copies ran while one was open for 2% of the time, Pallas kernels for 0%

profile of v6, /device:TPU:1, one launch (start us, length us, event | category | flops | bytes accessed | tf_op | source)
XLA Modules:
  0.0 174.1 jit_solution(714656930726678099)
XLA Ops:
  0.0 2.1 %reduce = bf16[98304]{0:T(1024)(128)(2,1)S(1)} reduce(bf16[1,98304]{1,0:T(2,128)(2,1)} %param.16, bf16[]{:T(256)} %constant.35), dimensions={0}, to_apply=%param.16.reduce_sub_computation | reduce | bytes 393218 | tf_op args[6]
  2.1 0.1 reshape.45
  2.2 4.0 %collective-permute-start.2 = (bf16[256,384]{1,0:T(8,128)(2,1)S(1)}, bf16[256,384]{1,0:T(8,128)(2,1)S(1)}, u32[]{:S(2)}, u32[]{:S(2)}) collective-permute-start(bf16[256,384]{1,0:T(8,128)(2,1)S(1)} %reshape.45), channel_id=1, source_target_pairs={{3,0},{0,1},{1,2},{2,3},{7,4},{4,5},{5,6},{6,7},{11,8},{8,9},{9,10... | collective-permute-start | bytes 589832 | tf_op jit(solution)/shard_map/ppermute | solution.py:127
  6.3 4.5 %collective-permute-start.1 = (bf16[256,384]{1,0:T(8,128)(2,1)S(1)}, bf16[256,384]{1,0:T(8,128)(2,1)S(1)}, u32[]{:S(2)}, u32[]{:S(2)}) collective-permute-start(bf16[256,384]{1,0:T(8,128)(2,1)S(1)} %reshape.45), channel_id=1, source_target_pairs={{2,0},{3,1},{0,2},{1,3},{6,4},{7,5},{4,6},{5,7},{10,8},{11,9},{8,1... | collective-permute-start | bytes 589832 | tf_op jit(solution)/shard_map/ppermute | solution.py:127
  10.8 3.0 %collective-permute-start = (bf16[256,384]{1,0:T(8,128)(2,1)S(1)}, bf16[256,384]{1,0:T(8,128)(2,1)S(1)}, u32[]{:S(2)}, u32[]{:S(2)}) collective-permute-start(bf16[256,384]{1,0:T(8,128)(2,1)S(1)} %reshape.45), channel_id=1, source_target_pairs={{1,0},{2,1},{3,2},{0,3},{5,4},{6,5},{7,6},{4,7},{9,8},{10,9},{11,1... | collective-permute-start | bytes 589832 | tf_op jit(solution)/shard_map/ppermute | solution.py:127
  13.8 0.8 reshape_reshape.3
  14.6 20.4 %all-to-all-start = ((bf16[128,2,384]{2,1,0:T(2,128)(2,1)}), bf16[128,2,384]{2,1,0:T(2,128)(2,1)S(1)}, u32[]{:S(2)}, u32[]{:S(2)}) async-start(bf16[128,2,384]{2,1,0:T(2,128)(2,1)} %reshape_reshape.3), calls=%async_computation | async-start | bytes 393216 | tf_op jit(solution)/shard_map/all_to_all | solution.py:89
  35.0 0.2 fusion.30
  35.3 0.1 fusion.54
  35.5 0.8 copy-done.3
  36.3 1.6 fusion.17
  38.0 15.0 %all-to-all-done = bf16[128,2,384]{2,1,0:T(2,128)(2,1)S(1)} async-done(((bf16[128,2,384]{2,1,0:T(2,128)(2,1)}), bf16[128,2,384]{2,1,0:T(2,128)(2,1)S(1)}, u32[]{:S(2)}, u32[]{:S(2)}) %all-to-all-start) | async-done | bytes 196640 | tf_op jit(solution)/shard_map/all_to_all | solution.py:89
  53.0 0.1 multiply_reduce_fusion
  53.1 2.7 %fusion.19 = f32[512,384,1]{1,0,2:T(8,128)S(1)} fusion(f32[512,384]{1,0:T(8,128)S(1)} %fusion.17, bf16[1024,384]{1,0:T(8,128)(2,1)S(1)} %constant_dynamic-update-slice_fusion, f32[1024]{0:T(1024)S(1)} %fusion.54, f32[512]{0:T(512)S(1)} %add_rsqrt_fusion, f32[384]{0:T(512)S(1)} %copy-done.8, s32[]{:T(128)S(6)} %select_n.8, bf16[384,1024]{1,0:T(8,128)(2,1)} %param.14), kind=kOutput, calls=%fused_computation.26 | convolution fusion | flops 813105152 | bytes 3940356 | tf_op jit(solution)/shard_map/dot_general | solution.py:140
  55.9 0.7 fusion.50
  56.6 0.3 copy-done.4
  56.9 0.1 copy-done.5
  57.0 0.1 copy-done.6
  57.1 1.8 %multiply_reduce_fusion.1 = (f32[]{:T(128)}, bf16[2,512,128]{2,1,0:T(8,128)(2,1)S(1)}, bf16[2,512,128]{2,1,0:T(8,128)(2,1)S(1)}) fusion(bf16[1,2,512,128]{3,2,1,0:T(8,128)(2,1)S(1)} %copy-done.5, f32[2,512,128]{2,1,0:T(8,128)S(1)} %copy-done.4, bf16[2,512,128]{2,1,0:T(8,128)(2,1)S(1)} %copy-done.6, f32[2,128,512]{2,1,0:T(8,128)S(1)} %fusion.50, ...), kind=kOutput, calls=%fused_computation.57 | convolution fusion | flops 807272448 | bytes 2101252 | tf_op jit(solution)/shard_map/kib,kbf->kif/dot_general | solution.py:146
  58.9 0.9 pad_maximum_fusion
  59.8 8.1 %all-to-all-start.1 = ((bf16[128,16,128]{2,1,0:T(8,128)(2,1)}), bf16[128,16,128]{2,1,0:T(8,128)(2,1)S(1)}, u32[]{:S(2)}, u32[]{:S(2)}) async-start(bf16[128,16,128]{2,1,0:T(8,128)(2,1)} %pad_maximum_fusion), calls=%async_computation.1 | async-start | bytes 1048576 | tf_op jit(solution)/shard_map/all_to_all | solution.py:89
  68.5 30.2 %all-to-all-done.1 = bf16[128,16,128]{2,1,0:T(8,128)(2,1)S(1)} async-done(((bf16[128,16,128]{2,1,0:T(8,128)(2,1)}), bf16[128,16,128]{2,1,0:T(8,128)(2,1)S(1)}, u32[]{:S(2)}, u32[]{:S(2)}) %all-to-all-start.1) | async-done | bytes 524320 | tf_op jit(solution)/shard_map/all_to_all | solution.py:89
  98.8 0.1 fusion.36
  98.9 0.3 fusion.23
  99.2 14.3 %all_to_all.30 = f32[32,8,128]{2,1,0:T(8,128)S(1)} all-to-all(f32[32,8,128]{2,1,0:T(8,128)S(1)} %fusion.23), channel_id=1, replica_groups=mesh['x'=4,'z'=16,'c'=2,'r'=4] {'x','c','r'}, dimensions={0} | all-to-all | bytes 262144 | tf_op jit(solution)/shard_map/all_to_all | solution.py:89
  113.5 14.6 %all_to_all.31 = f32[16,8,128]{2,1,0:T(8,128)S(1)} all-to-all(f32[16,8,128]{2,1,0:T(8,128)S(1)} %broadcast_in_dim.14), channel_id=1, replica_groups=mesh['x'=4,'z'=16,'c'=2,'r'=4] {'z'}, dimensions={0} | all-to-all | bytes 131072 | tf_op jit(solution)/shard_map/all_to_all | solution.py:89
  128.1 12.9 %all_to_all.32 = f32[32,8,128]{2,1,0:T(8,128)S(1)} all-to-all(f32[32,8,128]{2,1,0:T(8,128)S(1)} %broadcast_in_dim.15), channel_id=1, replica_groups=mesh['x'=4,'z'=16,'c'=2,'r'=4] {'x','c','r'}, dimensions={0} | all-to-all | bytes 262144 | tf_op jit(solution)/shard_map/all_to_all | solution.py:89
  141.0 8.3 %shard_map.100 = f32[128,128]{1,0:T(8,128)S(1)} custom-call(f32[256,128]{1,0:T(8,128)S(1)} %bitcast.25), custom_call_target="tpu_custom_call" | custom-call | flops 40000000 | bytes 200000 | tf_op jit(solution)/shard_map/pallas_call | solution.py:80
  149.3 0.4 fusion.21
  149.7 0.2 copy.30
  149.9 23.3 %all_to_all.33 = bf16[128,2,384]{2,1,0:T(2,128)(2,1)S(1)} all-to-all(bf16[128,2,384]{2,1,0:T(2,128)(2,1)S(1)} %copy.30), channel_id=1, replica_groups=mesh['x'=4,'z'=16,'c'=2,'r'=4] {'z','x','c'}, dimensions={0} | all-to-all | bytes 393216 | tf_op jit(solution)/shard_map/all_to_all | solution.py:89
  173.2 0.9 reshape.50
  (31 shorter events, 0.4 us)
Async XLA Ops:
  0.0 35.0 %copy-start = (bf16[512,384]{1,0:T(8,128)(2,1)S(1)}, bf16[512,384]{1,0:T(8,128)(2,1)}, u32[]{:S(2)}) copy-start(bf16[512,384]{1,0:T(8,128)(2,1)} %param.10) | copy-start | bytes 1179652
  2.2 33.0 %copy-start.1 = (f32[1024]{0:T(1024)S(1)}, f32[1024]{0:T(1024)}, u32[]{:S(2)}) copy-start(f32[1024]{0:T(1024)} %param.15) | copy-start | bytes 12292
  2.2 33.2 %collective-permute-start.2 = (bf16[256,384]{1,0:T(8,128)(2,1)S(1)}, bf16[256,384]{1,0:T(8,128)(2,1)S(1)}, u32[]{:S(2)}, u32[]{:S(2)}) collective-permute-start(bf16[256,384]{1,0:T(8,128)(2,1)S(1)} %reshape.45), channel_id=1, source_target_pairs={{3,0},{0,1},{1,2},{2,3},{7,4},{4,5},{5,6},{6,7},{11,8},{8,9},{9,10... | collective-permute-start | bytes 589832 | tf_op jit(solution)/shard_map/ppermute | solution.py:127
  6.3 29.1 %collective-permute-start.1 = (bf16[256,384]{1,0:T(8,128)(2,1)S(1)}, bf16[256,384]{1,0:T(8,128)(2,1)S(1)}, u32[]{:S(2)}, u32[]{:S(2)}) collective-permute-start(bf16[256,384]{1,0:T(8,128)(2,1)S(1)} %reshape.45), channel_id=1, source_target_pairs={{2,0},{3,1},{0,2},{1,3},{6,4},{7,5},{4,6},{5,7},{10,8},{11,9},{8,1... | collective-permute-start | bytes 589832 | tf_op jit(solution)/shard_map/ppermute | solution.py:127
  10.8 24.5 %collective-permute-start = (bf16[256,384]{1,0:T(8,128)(2,1)S(1)}, bf16[256,384]{1,0:T(8,128)(2,1)S(1)}, u32[]{:S(2)}, u32[]{:S(2)}) collective-permute-start(bf16[256,384]{1,0:T(8,128)(2,1)S(1)} %reshape.45), channel_id=1, source_target_pairs={{1,0},{2,1},{3,2},{0,3},{5,4},{6,5},{7,6},{4,7},{9,8},{10,9},{11,1... | collective-permute-start | bytes 589832 | tf_op jit(solution)/shard_map/ppermute | solution.py:127
  14.6 38.4 %all-to-all-start = ((bf16[128,2,384]{2,1,0:T(2,128)(2,1)}), bf16[128,2,384]{2,1,0:T(2,128)(2,1)S(1)}, u32[]{:S(2)}, u32[]{:S(2)}) async-start(bf16[128,2,384]{2,1,0:T(2,128)(2,1)} %reshape_reshape.3), calls=%async_computation | async-start | bytes 393216 | tf_op jit(solution)/shard_map/all_to_all | solution.py:89
  35.2 1.1 copy-start.3
  35.2 1.1 copy-start.8
  53.1 2.8 %copy-start.2 = (s32[2,128]{1,0:T(2,128)S(1)}, s32[2,128]{1,0:T(2,128)}, u32[]{:S(2)}) copy-start(s32[2,128]{1,0:T(2,128)} %param.12) | copy-start | bytes 3076
  55.9 1.0 copy-start.4
  55.9 1.1 copy-start.5
  55.9 1.2 copy-start.6
  55.9 1.2 copy-start.7
  59.8 38.9 %all-to-all-start.1 = ((bf16[128,16,128]{2,1,0:T(8,128)(2,1)}), bf16[128,16,128]{2,1,0:T(8,128)(2,1)S(1)}, u32[]{:S(2)}, u32[]{:S(2)}) async-start(bf16[128,16,128]{2,1,0:T(8,128)(2,1)} %pad_maximum_fusion), calls=%async_computation.1 | async-start | bytes 1048576 | tf_op jit(solution)/shard_map/all_to_all | solution.py:89

commit v7 on v5

--- a/solution.py
+++ b/solution.py
@@ -118,14 +118,12 @@
     features = w_in.shape[0]
     step_count, rows = batch_index.shape
     picked = obs_pick.shape[1]
+    noise = exchange(perturbation.reshape(members, -1, picked), MEM)
     own = member_params.reshape(-1, features)
     weights = lax.all_gather(own, "r", axis=0, tiled=True)
-    param_block = exchange(own.reshape(members, -1, features), MEM)
     step_scale = DT * width ** (-0.5)
     current = states.astype(jnp.float32)
-    for turn in range(2):
-        if turn:
-            current, param_block = lax.optimization_barrier((current, param_block))
+    for _ in range(2):
         layer = hidden_layer(current, norm_gain, w_in, b_in)
         current = current + step_scale * jnp.dot(layer, weights, preferred_element_type=jnp.float32)
     feature_ids = lax.broadcasted_iota(jnp.int32, (step_count, features, picked), 1)
@@ -141,15 +139,27 @@
     ).astype(jnp.bfloat16)
     misfit_local = jnp.sum(jnp.square(misfit_w.astype(jnp.float32)))
     entries = members * step_count * rows * lax.axis_size("r") * picked
-    sent = jnp.concatenate(
-        [weighted.reshape(members, -1, picked), misfit_w.reshape(members, -1, picked)], axis=1
+    pairs = (members, -1, 2, picked)
+    sent = jnp.concatenate([weighted.reshape(pairs), own.reshape(pairs)], axis=1)
+    sent, noise = lax.optimization_barrier((sent, noise))
+    arrived = exchange(sent, MEM)
+    noise = noise.reshape(pairs)
+    depth = noise.shape[1]
+    gathered = arrived[:, :depth].astype(jnp.float32)
+    param_block = arrived[:, depth:]
+    place = lax.axis_index(MEM) * (2 * depth)
+    aim = lax.dynamic_slice_in_dim(
+        observed.reshape(-1, picked), place, 2 * depth, 0
+    ).astype(jnp.float32) * lax.dynamic_slice_in_dim(
+        inv_sigma.reshape(-1, picked), place, 2 * depth, 0
     )
-    gathered, misfit_here = jnp.split(exchange(sent, MEM), 2, axis=1)
-    gathered = gathered.astype(jnp.float32)
     anomaly = (gathered - jnp.mean(gathered, axis=0)).astype(jnp.bfloat16)
+    misfit_here = (
+        aim.reshape(depth, 2, picked) + noise.astype(jnp.float32) - gathered
+    ).astype(jnp.bfloat16)
     both = jnp.concatenate([anomaly, misfit_here], axis=0)
     partial = lax.dot_general(
-        both, anomaly, (((1, 2), (1, 2)), ((), ())), preferred_element_type=jnp.float32
+        both, anomaly, (((1, 2, 3), (1, 2, 3)), ((), ())), preferred_element_type=jnp.float32
     )
     unit = lax.broadcasted_iota(jnp.int32, partial.shape, 0) == lax.broadcasted_iota(
         jnp.int32, partial.shape, 1
@@ -158,7 +168,7 @@
     total = total_of(partial)
     centred = centred_coefficients(total)
     params_f = param_block.astype(jnp.float32)
-    change = jnp.einsum("kj,kap->jap", centred, params_f, precision=HIGHEST)
+    change = jnp.einsum("kj,kabp->jabp", centred, params_f, precision=HIGHEST)
     renewed = (params_f + change).astype(jnp.bfloat16)
     return exchange(renewed, MEM).reshape(member_params.shape)
 

time: 170 us -> 171 us (level)
  blocking collectives: 79.9 us -> 66.8 us
  starting transfers between devices: 34.5 us -> 43.6 us
  matrix products: 6.16 us -> 8.72 us
    all_to_all x4 -> x3, blocking collectives: 67 us -> 54 us  [exchange(): return lax.all_to_all(value, axes, split_axis=0, concat_axis=0, tiled=True)]
    all_to_all x2 -> x3, starting transfers between devices: 34.5 us -> 43.6 us  [exchange(): return lax.all_to_all(value, axes, split_axis=0, concat_axis=0, tiled=True)]
    dot_general x2, matrix products: 3.06 us -> 5.63 us  [on_device(): jnp.dot(layer, weights, preferred_element_type=jnp.float32)]
    all_to_all x2 -> x3, waiting for transfers between devices: 33.4 us -> 34.3 us  [exchange(): return lax.all_to_all(value, axes, split_axis=0, concat_axis=0, tiled=True)]
  transfers between devices with their start and end apart: 2 -> 3, of which waited for: 2 -> 2; matrix products, arithmetic and copies ran while one was open for 1% -> 7% of each run, Pallas kernels for 0% -> 0%
where the time goes in v7:
time: 171 us; the launch traced here: 169 us
  blocking collectives  66.8 us (39%)
  starting transfers between devices  43.6 us (25%)
  waiting for transfers between devices  34.3 us (20%)
  matrix products  8.72 us (5%)
  Pallas kernels  8.32 us (5%)
  other arithmetic  3.58 us (2%)
  local copies, waits for them, and re-layouts  3.23 us (2%)
    all_to_all x3, blocking collectives, exchange(): return lax.all_to_all(value, axes, split_axis=0, concat_axis=0, tiled=True)  54 us
    all_to_all x3, starting transfers between devices, exchange(): return lax.all_to_all(value, axes, split_axis=0, concat_axis=0, tiled=True)  43.6 us
    all_to_all x3, waiting for transfers between devices, exchange(): return lax.all_to_all(value, axes, split_axis=0, concat_axis=0, tiled=True)  34.3 us
    all_gather x1, blocking collectives, on_device(): weights = lax.all_gather(own, 'r', axis=0, tiled=True)  12.8 us
    pallas_call x1, Pallas kernels, centred_coefficients(): pl.pallas_call(solve_kernel, out_shape=jax.ShapeDtypeStruct((n, n), jnp.f...  8.32 us
    dot_general x2, matrix products, on_device(): jnp.dot(layer, weights, preferred_element_type=jnp.float32)  5.63 us
  transfers between devices with their start and end apart: 3, of which 2 were waited for; matrix products, arithmetic and copies ran while one was open for 7% of the time, Pallas kernels for 0%

profile of v7, /device:TPU:1, one launch (start us, length us, event | category | flops | bytes accessed | tf_op | source)
XLA Modules:
  0.0 169.4 jit_solution(7361758111567255954)
XLA Ops:
  0.0 20.5 %all-to-all-start = ((bf16[128,8,128]{2,1,0:T(8,128)(2,1)}), bf16[128,8,128]{2,1,0:T(8,128)(2,1)S(1)}, u32[]{:S(2)}, u32[]{:S(2)}) async-start(bf16[128,8,128]{2,1,0:T(8,128)(2,1)} %bitcast.37), calls=%async_computation | async-start | bytes 524288 | tf_op jit(solution)/shard_map/all_to_all | solution.py:89
  20.5 1.2 reduce
  21.7 0.1 reshape.55
  21.8 12.8 %all_gather.3 = bf16[1024,384]{1,0:T(8,128)(2,1)S(1)} all-gather(bf16[256,384]{1,0:T(8,128)(2,1)S(1)} %reshape.55), channel_id=1, replica_groups=mesh['x'=4,'z'=16,'c'=2,'r'=4] {'r'}, dimensions={0}, use_global_device_ids=true | all-gather | bytes 983040 | tf_op jit(solution)/shard_map/all_gather | solution.py:123
  34.7 0.2 copy.29
  34.9 0.1 fusion.30
  35.0 0.4 copy-done.7
  35.4 2.6 %multiply_reduce_fusion = (f32[512]{0:T(512)S(1)}, f32[512,384]{0,1:T(8,128)}) fusion(bf16[1024,384]{1,0:T(8,128)(2,1)S(1)} %all_gather.3, bf16[384,1024]{1,0:T(8,128)(2,1)S(1)} %copy-done, f32[1024]{0:T(1024)S(1)} %copy-done.7, bf16[512,384]{0,1:T(8,128)(2,1)S(1)} %copy.29, f32[384]{0:T(512)S(1)} %copy-done.9, f32[512]{0:T(512)S(1)} %add_rsqrt_fusion.1), kind=kOutput, calls=%fused_computation.46 | convolution fusion | flops 812318208 | bytes 2762240 | tf_op jit(solution)/shard_map/dot_general | solution.py:128
  38.0 3.1 %fusion.19 = f32[512,384,1]{0,1,2:T(8,128)S(1)} fusion(f32[512,384]{0,1:T(8,128)} %get-tuple-element.14, bf16[1024,384]{1,0:T(8,128)(2,1)S(1)} %all_gather.3, bf16[384,1024]{1,0:T(8,128)(2,1)S(1)} %copy-done, f32[1024]{0:T(1024)S(1)} %copy-done.7, f32[512]{0:T(512)S(1)} %add_rsqrt_fusion, f32[384]{0:T(512)S(1)} %copy-done.9), kind=kOutput, calls=%fused_computation.24 | convolution fusion | flops 811532288 | bytes 3153408 | tf_op jit(solution)/shard_map/dot_general | solution.py:128
  41.1 0.7 fusion.50
  41.8 0.2 copy-done.3
  42.0 0.2 copy-done.5
  42.2 0.1 copy-done.6
  42.2 1.8 %multiply_reduce_fusion.1 = (f32[]{:T(128)}, bf16[2,512,128]{2,1,0:T(8,128)(2,1)S(1)}) fusion(f32[2,512,128]{2,1,0:T(8,128)S(1)} %copy-done.5, bf16[2,512,128]{2,1,0:T(8,128)(2,1)S(1)} %copy-done.6, bf16[1,2,512,128]{3,2,1,0:T(8,128)(2,1)S(1)} %copy-done.3, f32[2,128,512]{2,1,0:T(8,128)S(1)} %fusion.50, s32[2,512]{1,0:T(2,128)S(1)} %copy-done.8), kind=kOutput, calls=%fused_computation.55 | convolution fusion | flops 807272448 | bytes 1839108 | tf_op jit(solution)/shard_map/kib,kbf->kif/dot_general | solution.py:134
  44.0 1.4 pad_maximum_fusion
  45.4 17.3 %all-to-all-start.1 = ((bf16[128,7,2,128]{3,2,1,0:T(2,128)(2,1)}), bf16[128,7,2,128]{3,2,1,0:T(2,128)(2,1)S(1)}, u32[]{:S(2)}, u32[]{:S(2)}) async-start(bf16[128,7,2,128]{3,2,1,0:T(2,128)(2,1)} %pad_maximum_fusion), calls=%async_computation.1 | async-start | bytes 917504 | tf_op jit(solution)/shard_map/all_to_all | solution.py:89
  63.4 0.7 dynamic-slice_multiply_fusion
  64.1 26.7 %all-to-all-done.1 = bf16[128,7,2,128]{3,2,1,0:T(2,128)(2,1)S(1)} async-done(((bf16[128,7,2,128]{3,2,1,0:T(2,128)(2,1)}), bf16[128,7,2,128]{3,2,1,0:T(2,128)(2,1)S(1)}, u32[]{:S(2)}, u32[]{:S(2)}) %all-to-all-start.1) | async-done | bytes 458784 | tf_op jit(solution)/shard_map/all_to_all | solution.py:89
  90.9 0.2 slice.9
  91.1 0.1 fusion.36
  91.2 0.3 fusion.23
  91.5 16.6 %all_to_all.30 = f32[32,8,128]{2,1,0:T(8,128)S(1)} all-to-all(f32[32,8,128]{2,1,0:T(8,128)S(1)} %fusion.23), channel_id=1, replica_groups=mesh['x'=4,'z'=16,'c'=2,'r'=4] {'x','c','r'}, dimensions={0} | all-to-all | bytes 262144 | tf_op jit(solution)/shard_map/all_to_all | solution.py:89
  108.2 14.2 %all_to_all.31 = f32[16,8,128]{2,1,0:T(8,128)S(1)} all-to-all(f32[16,8,128]{2,1,0:T(8,128)S(1)} %broadcast_in_dim.14), channel_id=1, replica_groups=mesh['x'=4,'z'=16,'c'=2,'r'=4] {'z'}, dimensions={0} | all-to-all | bytes 131072 | tf_op jit(solution)/shard_map/all_to_all | solution.py:89
  122.4 0.7 broadcast_in_dim.15
  123.1 5.7 %all-to-all-start.4 = ((f32[32,8,128]{2,1,0:T(8,128)}), f32[32,8,128]{2,1,0:T(8,128)S(1)}, u32[]{:S(2)}, u32[]{:S(2)}) async-start(f32[32,8,128]{2,1,0:T(8,128)} %broadcast_in_dim.15), calls=%async_computation.4 | async-start | bytes 262144 | tf_op jit(solution)/shard_map/all_to_all | solution.py:89
  128.8 0.1 slice.8
  129.0 7.5 %all-to-all-done.4 = f32[32,8,128]{2,1,0:T(8,128)S(1)} async-done(((f32[32,8,128]{2,1,0:T(8,128)}), f32[32,8,128]{2,1,0:T(8,128)S(1)}, u32[]{:S(2)}, u32[]{:S(2)}) %all-to-all-start.4) | async-done | bytes 131104 | tf_op jit(solution)/shard_map/all_to_all | solution.py:89
  136.5 8.3 %shard_map.100 = f32[128,128]{1,0:T(8,128)S(1)} custom-call(f32[256,128]{1,0:T(8,128)S(1)} %bitcast.33), custom_call_target="tpu_custom_call" | custom-call | flops 40000000 | bytes 200000 | tf_op jit(solution)/shard_map/pallas_call | solution.py:80
  144.8 0.4 fusion.21
  145.2 0.2 copy.36
  145.4 23.2 %all_to_all.32 = bf16[128,3,2,128]{3,2,1,0:T(2,128)(2,1)S(1)} all-to-all(bf16[128,3,2,128]{3,2,1,0:T(2,128)(2,1)S(1)} %copy.36), channel_id=1, replica_groups=mesh['x'=4,'z'=16,'c'=2,'r'=4] {'z','x','c'}, dimensions={0} | all-to-all | bytes 393216 | tf_op jit(solution)/shard_map/all_to_all | solution.py:89
  168.6 0.8 reshape.62
  (25 shorter events, 0.2 us)
Async XLA Ops:
  0.0 35.0 %copy-start = (bf16[384,1024]{1,0:T(8,128)(2,1)S(1)}, bf16[384,1024]{1,0:T(8,128)(2,1)}, u32[]{:S(2)}) copy-start(bf16[384,1024]{1,0:T(8,128)(2,1)} %param.14) | copy-start | bytes 2359300
  0.0 20.5 %copy-start.2 = (bf16[1,98304]{1,0:T(2,128)(2,1)S(1)}, bf16[1,98304]{1,0:T(2,128)(2,1)}, u32[]{:S(2)}) copy-start(bf16[1,98304]{1,0:T(2,128)(2,1)} %param.16) | copy-start | bytes 589828
  0.0 45.4 %all-to-all-start = ((bf16[128,8,128]{2,1,0:T(8,128)(2,1)}), bf16[128,8,128]{2,1,0:T(8,128)(2,1)S(1)}, u32[]{:S(2)}, u32[]{:S(2)}) async-start(bf16[128,8,128]{2,1,0:T(8,128)(2,1)} %bitcast.37), calls=%async_computation | async-start | bytes 524288 | tf_op jit(solution)/shard_map/all_to_all | solution.py:89
  21.7 13.0 %copy-start.1 = (bf16[512,384]{1,0:T(8,128)(2,1)S(1)}, bf16[512,384]{1,0:T(8,128)(2,1)}, u32[]{:S(2)}) copy-start(bf16[512,384]{1,0:T(8,128)(2,1)} %param.10) | copy-start | bytes 1179652
  34.7 0.7 copy-start.7
  34.7 0.7 copy-start.9
  38.0 3.1 %copy-start.4 = (s32[2,128]{1,0:T(2,128)S(1)}, s32[2,128]{1,0:T(2,128)}, u32[]{:S(2)}) copy-start(s32[2,128]{1,0:T(2,128)} %param.12) | copy-start | bytes 3076
  41.0 1.0 copy-start.3
  41.1 1.1 copy-start.5
  41.1 1.2 copy-start.6
  41.1 1.2 copy-start.8
  45.4 45.5 %all-to-all-start.1 = ((bf16[128,7,2,128]{3,2,1,0:T(2,128)(2,1)}), bf16[128,7,2,128]{3,2,1,0:T(2,128)(2,1)S(1)}, u32[]{:S(2)}, u32[]{:S(2)}) async-start(bf16[128,7,2,128]{3,2,1,0:T(2,128)(2,1)} %pad_maximum_fusion), calls=%async_computation.1 | async-start | bytes 917504 | tf_op jit(solution)/shard_map/all_to_all | solution.py:89
  123.1 13.4 %all-to-all-start.4 = ((f32[32,8,128]{2,1,0:T(8,128)}), f32[32,8,128]{2,1,0:T(8,128)S(1)}, u32[]{:S(2)}, u32[]{:S(2)}) async-start(f32[32,8,128]{2,1,0:T(8,128)} %broadcast_in_dim.15), calls=%async_computation.4 | async-start | bytes 262144 | tf_op jit(solution)/shard_map/all_to_all | solution.py:89

commit v8 on v7

--- a/solution.py
+++ b/solution.py
@@ -118,7 +118,6 @@
     features = w_in.shape[0]
     step_count, rows = batch_index.shape
     picked = obs_pick.shape[1]
-    noise = exchange(perturbation.reshape(members, -1, picked), MEM)
     own = member_params.reshape(-1, features)
     weights = lax.all_gather(own, "r", axis=0, tiled=True)
     step_scale = DT * width ** (-0.5)
@@ -140,23 +139,14 @@
     misfit_local = jnp.sum(jnp.square(misfit_w.astype(jnp.float32)))
     entries = members * step_count * rows * lax.axis_size("r") * picked
     pairs = (members, -1, 2, picked)
-    sent = jnp.concatenate([weighted.reshape(pairs), own.reshape(pairs)], axis=1)
-    sent, noise = lax.optimization_barrier((sent, noise))
-    arrived = exchange(sent, MEM)
-    noise = noise.reshape(pairs)
-    depth = noise.shape[1]
+    pairs = (members, -1, 2, picked)
+    sent = [weighted.reshape(pairs), misfit_w.reshape(pairs), own.reshape(pairs)]
+    depth = sent[0].shape[1]
+    arrived = exchange(jnp.concatenate(sent, axis=1), MEM)
     gathered = arrived[:, :depth].astype(jnp.float32)
-    param_block = arrived[:, depth:]
-    place = lax.axis_index(MEM) * (2 * depth)
-    aim = lax.dynamic_slice_in_dim(
-        observed.reshape(-1, picked), place, 2 * depth, 0
-    ).astype(jnp.float32) * lax.dynamic_slice_in_dim(
-        inv_sigma.reshape(-1, picked), place, 2 * depth, 0
-    )
+    misfit_here = arrived[:, depth : 2 * depth]
+    param_block = arrived[:, 2 * depth :]
     anomaly = (gathered - jnp.mean(gathered, axis=0)).astype(jnp.bfloat16)
-    misfit_here = (
-        aim.reshape(depth, 2, picked) + noise.astype(jnp.float32) - gathered
-    ).astype(jnp.bfloat16)
     both = jnp.concatenate([anomaly, misfit_here], axis=0)
     partial = lax.dot_general(
         both, anomaly, (((1, 2, 3), (1, 2, 3)), ((), ())), preferred_element_type=jnp.float32

time: 171 us -> 164 us (0.959)
  starting transfers between devices: 43.6 us -> 27.8 us
  waiting for transfers between devices: 34.3 us -> 45.8 us
  matrix products: 8.72 us -> 6.48 us
    all_to_all x3 -> x2, starting transfers between devices: 43.6 us -> 27.8 us  [exchange(): return lax.all_to_all(value, axes, split_axis=0, concat_axis=0, tiled=True)]
    all_to_all x3 -> x2, waiting for transfers between devices: 34.3 us -> 45.8 us  [exchange(): return lax.all_to_all(value, axes, split_axis=0, concat_axis=0, tiled=True)]
    dot_general x2, matrix products: 5.63 us -> 3.39 us  [on_device(): jnp.dot(layer, weights, preferred_element_type=jnp.float32)]
  transfers between devices with their start and end apart: 3 -> 2, of which waited for: 2 -> 2; matrix products, arithmetic and copies ran while one was open for 7% -> 0% of each run, Pallas kernels for 0% -> 0%
where the time goes in v8:
time: 164 us; the launch traced here: 163 us
  blocking collectives  66.6 us (41%)
  waiting for transfers between devices  45.8 us (28%)
  starting transfers between devices  27.8 us (17%)
  Pallas kernels  8.32 us (5%)
  matrix products  6.48 us (4%)
  other arithmetic  4.33 us (3%)
  local copies, waits for them, and re-layouts  3.04 us (2%)
    all_to_all x3, blocking collectives, exchange(): return lax.all_to_all(value, axes, split_axis=0, concat_axis=0, tiled=True)  54.4 us
    all_to_all x2, waiting for transfers between devices, exchange(): return lax.all_to_all(value, axes, split_axis=0, concat_axis=0, tiled=True)  45.8 us
    all_to_all x2, starting transfers between devices, exchange(): return lax.all_to_all(value, axes, split_axis=0, concat_axis=0, tiled=True)  27.8 us
    all_gather x1, blocking collectives, on_device(): weights = lax.all_gather(own, 'r', axis=0, tiled=True)  12.2 us
    pallas_call x1, Pallas kernels, centred_coefficients(): pl.pallas_call(solve_kernel, out_shape=jax.ShapeDtypeStruct((n, n), jnp.f...  8.32 us
    dot_general x2, matrix products, on_device(): jnp.dot(layer, weights, preferred_element_type=jnp.float32)  3.39 us
  transfers between devices with their start and end apart: 2, of which 2 were waited for; matrix products, arithmetic and copies ran while one was open for 0% of the time, Pallas kernels for 0%

profile of v8, /device:TPU:1, one launch (start us, length us, event | category | flops | bytes accessed | tf_op | source)
XLA Modules:
  0.0 163.2 jit_solution(1862862181674814566)
XLA Ops:
  0.0 2.2 %reduce = bf16[98304]{0:T(1024)(128)(2,1)S(1)} reduce(bf16[1,98304]{1,0:T(2,128)(2,1)} %param.16, bf16[]{:T(256)} %constant.25), dimensions={0}, to_apply=%param.16.reduce_sub_computation | reduce | bytes 393218 | tf_op args[6]
  2.2 0.1 reshape.45
  2.3 0.2 copy.29
  2.5 0.0 copy-start.8
  2.5 0.1 fusion.30
  2.6 12.2 %all_gather.3 = bf16[1024,384]{1,0:T(8,128)(2,1)S(1)} all-gather(bf16[256,384]{1,0:T(8,128)(2,1)S(1)} %reshape.45), channel_id=1, replica_groups=mesh['x'=4,'z'=16,'c'=2,'r'=4] {'r'}, dimensions={0}, use_global_device_ids=true | all-gather | bytes 983040 | tf_op jit(solution)/shard_map/all_gather | solution.py:122
  14.9 1.7 %multiply_reduce_fusion = (f32[512]{0:T(512)S(1)}, f32[512,384]{0,1:T(8,128)S(1)}) fusion(bf16[1024,384]{1,0:T(8,128)(2,1)S(1)} %all_gather.3, bf16[384,1024]{1,0:T(8,128)(2,1)S(1)} %copy-done, f32[1024]{0:T(1024)S(1)} %copy-done.6, bf16[512,384]{0,1:T(8,128)(2,1)S(1)} %copy.29, f32[384]{0:T(512)S(1)} %copy-done.8, f32[512]{0:T(512)S(1)} %add_rsqrt_fusion.1), kind=kOutput, calls=%fused_computation.43 | convolution fusion | flops 812318208 | bytes 2762240 | tf_op jit(solution)/shard_map/dot_general | solution.py:127
  16.6 1.7 %fusion.19 = f32[512,384,1]{0,1,2:T(8,128)S(1)} fusion(f32[512,384]{0,1:T(8,128)S(1)} %get-tuple-element.11, bf16[1024,384]{1,0:T(8,128)(2,1)S(1)} %all_gather.3, bf16[384,1024]{1,0:T(8,128)(2,1)S(1)} %copy-done, f32[1024]{0:T(1024)S(1)} %copy-done.6, f32[512]{0:T(512)S(1)} %add_rsqrt_fusion, f32[384]{0:T(512)S(1)} %copy-done.8), kind=kOutput, calls=%fused_computation.24 | convolution fusion | flops 811532288 | bytes 3153408 | tf_op jit(solution)/shard_map/dot_general | solution.py:127
  18.3 0.0 copy-start.4
  18.3 0.0 copy-start.5
  18.4 0.7 fusion.49
  19.0 0.3 copy-done.3
  19.3 0.1 copy-done.4
  19.4 0.1 copy-done.5
  19.5 1.8 %multiply_reduce_fusion.1 = (f32[]{:T(128)}, bf16[2,512,128]{2,1,0:T(8,128)(2,1)S(1)}, bf16[2,512,128]{2,1,0:T(8,128)(2,1)S(1)}) fusion(bf16[1,2,512,128]{3,2,1,0:T(8,128)(2,1)S(1)} %copy-done.4, f32[2,512,128]{2,1,0:T(8,128)S(1)} %copy-done.3, bf16[2,512,128]{2,1,0:T(8,128)(2,1)S(1)} %copy-done.5, f32[2,128,512]{2,1,0:T(8,128)S(1)} %fusion.49, ...), kind=kOutput, calls=%fused_computation.54 | convolution fusion | flops 807272448 | bytes 2101252 | tf_op jit(solution)/shard_map/kib,kbf->kif/dot_general | solution.py:133
  21.3 1.9 %pad_maximum_fusion = bf16[128,11,2,128]{3,2,1,0:T(2,128)(2,1)} fusion(bf16[128,3,2,128]{3,2,1,0:T(2,128)(2,1)S(1)} %bitcast.31, bf16[128,4,2,128]{3,2,1,0:T(2,128)(2,1)S(1)} %bitcast.32, bf16[128,4,2,128]{3,2,1,0:T(2,128)(2,1)S(1)} %bitcast.33), kind=kLoop, calls=%fused_computation.44 | loop fusion | flops 720896 | bytes 1441792 | tf_op jit(solution)/shard_map/concatenate | solution.py:145
  23.1 22.0 %all-to-all-start = ((bf16[128,11,2,128]{3,2,1,0:T(2,128)(2,1)}), bf16[128,11,2,128]{3,2,1,0:T(2,128)(2,1)S(1)}, u32[]{:S(2)}, u32[]{:S(2)}) async-start(bf16[128,11,2,128]{3,2,1,0:T(2,128)(2,1)} %pad_maximum_fusion), calls=%async_computation | async-start | bytes 1441792 | tf_op jit(solution)/shard_map/all_to_all | solution.py:89
  45.8 38.3 %all-to-all-done = bf16[128,11,2,128]{3,2,1,0:T(2,128)(2,1)S(1)} async-done(((bf16[128,11,2,128]{3,2,1,0:T(2,128)(2,1)}), bf16[128,11,2,128]{3,2,1,0:T(2,128)(2,1)S(1)}, u32[]{:S(2)}, u32[]{:S(2)}) %all-to-all-start) | async-done | bytes 720928 | tf_op jit(solution)/shard_map/all_to_all | solution.py:89
  84.1 0.4 fusion.63
  84.6 0.1 fusion.35
  84.6 0.3 fusion.23
  84.9 16.9 %all_to_all.25 = f32[32,8,128]{2,1,0:T(8,128)S(1)} all-to-all(f32[32,8,128]{2,1,0:T(8,128)S(1)} %fusion.23), channel_id=1, replica_groups=mesh['x'=4,'z'=16,'c'=2,'r'=4] {'x','c','r'}, dimensions={0} | all-to-all | bytes 262144 | tf_op jit(solution)/shard_map/all_to_all | solution.py:89
  101.9 14.3 %all_to_all.26 = f32[16,8,128]{2,1,0:T(8,128)S(1)} all-to-all(f32[16,8,128]{2,1,0:T(8,128)S(1)} %broadcast_in_dim.14), channel_id=1, replica_groups=mesh['x'=4,'z'=16,'c'=2,'r'=4] {'z'}, dimensions={0} | all-to-all | bytes 131072 | tf_op jit(solution)/shard_map/all_to_all | solution.py:89
  116.2 0.7 broadcast_in_dim.15
  116.9 5.8 %all-to-all-start.3 = ((f32[32,8,128]{2,1,0:T(8,128)}), f32[32,8,128]{2,1,0:T(8,128)S(1)}, u32[]{:S(2)}, u32[]{:S(2)}) async-start(f32[32,8,128]{2,1,0:T(8,128)} %broadcast_in_dim.15), calls=%async_computation.3 | async-start | bytes 262144 | tf_op jit(solution)/shard_map/all_to_all | solution.py:89
  122.7 0.1 slice.12
  122.8 7.5 %all-to-all-done.3 = f32[32,8,128]{2,1,0:T(8,128)S(1)} async-done(((f32[32,8,128]{2,1,0:T(8,128)}), f32[32,8,128]{2,1,0:T(8,128)S(1)}, u32[]{:S(2)}, u32[]{:S(2)}) %all-to-all-start.3) | async-done | bytes 131104 | tf_op jit(solution)/shard_map/all_to_all | solution.py:89
  130.3 8.3 %shard_map.100 = f32[128,128]{1,0:T(8,128)S(1)} custom-call(f32[256,128]{1,0:T(8,128)S(1)} %bitcast.30), custom_call_target="tpu_custom_call" | custom-call | flops 40000000 | bytes 200000 | tf_op jit(solution)/shard_map/pallas_call | solution.py:80
  138.7 0.4 fusion.21
  139.0 0.2 copy.36
  139.2 23.2 %all_to_all.27 = bf16[128,3,2,128]{3,2,1,0:T(2,128)(2,1)S(1)} all-to-all(bf16[128,3,2,128]{3,2,1,0:T(2,128)(2,1)S(1)} %copy.36), channel_id=1, replica_groups=mesh['x'=4,'z'=16,'c'=2,'r'=4] {'z','x','c'}, dimensions={0} | all-to-all | bytes 393216 | tf_op jit(solution)/shard_map/all_to_all | solution.py:89
  162.4 0.8 reshape.50
  (20 shorter events, 0.2 us)
Async XLA Ops:
  0.0 14.9 %copy-start = (bf16[384,1024]{1,0:T(8,128)(2,1)S(1)}, bf16[384,1024]{1,0:T(8,128)(2,1)}, u32[]{:S(2)}) copy-start(bf16[384,1024]{1,0:T(8,128)(2,1)} %param.14) | copy-start | bytes 2359300
  0.0 2.3 %copy-start.1 = (bf16[512,384]{1,0:T(8,128)(2,1)S(1)}, bf16[512,384]{1,0:T(8,128)(2,1)}, u32[]{:S(2)}) copy-start(bf16[512,384]{1,0:T(8,128)(2,1)} %param.10) | copy-start | bytes 1179652
  2.5 12.4 %copy-start.6 = (f32[1024]{0:T(1024)S(1)}, f32[1024]{0:T(1024)}, u32[]{:S(2)}) copy-start(f32[1024]{0:T(1024)} %param.15) | copy-start | bytes 12292
  2.5 12.4 %copy-start.8 = (f32[384]{0:T(512)S(1)}, f32[384]{0:T(512)}, u32[]{:S(2)}) copy-start(f32[384]{0:T(512)} %param.13) | copy-start | bytes 4612
  16.6 1.7 %copy-start.2 = (s32[2,128]{1,0:T(2,128)S(1)}, s32[2,128]{1,0:T(2,128)}, u32[]{:S(2)}) copy-start(s32[2,128]{1,0:T(2,128)} %param.12) | copy-start | bytes 3076
  18.3 1.0 copy-start.3
  18.3 1.1 copy-start.4
  18.3 1.2 copy-start.5
  18.3 1.2 copy-start.7
  23.1 61.0 %all-to-all-start = ((bf16[128,11,2,128]{3,2,1,0:T(2,128)(2,1)}), bf16[128,11,2,128]{3,2,1,0:T(2,128)(2,1)S(1)}, u32[]{:S(2)}, u32[]{:S(2)}) async-start(bf16[128,11,2,128]{3,2,1,0:T(2,128)(2,1)} %pad_maximum_fusion), calls=%async_computation | async-start | bytes 1441792 | tf_op jit(solution)/shard_map/all_to_all | solution.py:89
  116.9 13.4 %all-to-all-start.3 = ((f32[32,8,128]{2,1,0:T(8,128)}), f32[32,8,128]{2,1,0:T(8,128)S(1)}, u32[]{:S(2)}, u32[]{:S(2)}) async-start(f32[32,8,128]{2,1,0:T(8,128)} %broadcast_in_dim.15), calls=%async_computation.3 | async-start | bytes 262144 | tf_op jit(solution)/shard_map/all_to_all | solution.py:89

commit v9 on v8

--- a/solution.py
+++ b/solution.py
@@ -27,22 +27,24 @@
 def eliminate(left, right):
     wide = lambda v: jnp.broadcast_to(v, left[0].shape)
     cols = [[wide(tile[:, q : q + 1]) for q in range(BLOCK)] for tile in left]
-    pivots = [[wide(cols[0][q][p : p + 1]) for q in range(BLOCK)] for p in range(BLOCK)]
+    pivots = [[wide(cols[0][q][p : p + 1]) for q in range(p + 1)] for p in range(BLOCK)]
     top = [wide(left[0][p : p + 1]) for p in range(BLOCK)]
     side = [wide(right[0][p : p + 1]) for p in range(BLOCK)]
+    factors = {}
     for p in range(BLOCK):
         inverse = 1.0 / pivots[p][p]
-        for c in range(p + 1, BLOCK):
-            pivots[p][c] = pivots[p][c] * inverse
+        for q in range(p + 1, BLOCK):
+            factors[q, p] = factor = pivots[q][p] * inverse
+            for c in range(p + 1, q + 1):
+                pivots[q][c] = pivots[q][c] - factor * pivots[c][p]
+            top[q] = top[q] - factor * top[p]
+            side[q] = side[q] - factor * side[p]
         top[p] = top[p] * inverse
         side[p] = side[p] * inverse
-        for q in range(BLOCK):
-            if q != p:
-                factor = pivots[q][p]
-                for c in range(p + 1, BLOCK):
-                    pivots[q][c] = pivots[q][c] - factor * pivots[p][c]
-                top[q] = top[q] - factor * top[p]
-                side[q] = side[q] - factor * side[p]
+    for p in reversed(range(BLOCK)):
+        for q in range(p):
+            top[q] = top[q] - factors[p, q] * top[p]
+            side[q] = side[q] - factors[p, q] * side[p]
     row = lax.broadcasted_iota(jnp.int32, left[0].shape, 0)
     last_left, last_right = top[0], side[0]
     for p in range(1, BLOCK):
@@ -146,6 +148,7 @@
     gathered = arrived[:, :depth].astype(jnp.float32)
     misfit_here = arrived[:, depth : 2 * depth]
     param_block = arrived[:, 2 * depth :]
+    param_block, gathered = lax.optimization_barrier((param_block, gathered))
     anomaly = (gathered - jnp.mean(gathered, axis=0)).astype(jnp.bfloat16)
     both = jnp.concatenate([anomaly, misfit_here], axis=0)
     partial = lax.dot_general(

time: 164 us -> 162 us (0.988)
  blocking collectives: 66.6 us -> 79.5 us
  waiting for transfers between devices: 45.8 us -> 38.3 us
  starting transfers between devices: 27.8 us -> 22 us
    all_to_all x3 -> x4, blocking collectives: 54.4 us -> 67.3 us  [exchange(): return lax.all_to_all(value, axes, split_axis=0, concat_axis=0, tiled=True)]
    all_to_all x2 -> x1, waiting for transfers between devices: 45.8 us -> 38.3 us  [exchange(): return lax.all_to_all(value, axes, split_axis=0, concat_axis=0, tiled=True)]
    all_to_all x2 -> x1, starting transfers between devices: 27.8 us -> 22 us  [exchange(): return lax.all_to_all(value, axes, split_axis=0, concat_axis=0, tiled=True)]
  transfers between devices with their start and end apart: 2 -> 1, of which waited for: 2 -> 1; matrix products, arithmetic and copies ran while one was open for 0% -> 0% of each run, Pallas kernels for 0% -> 0%
where the time goes in v9:
time: 162 us; the launch traced here: 161 us
  blocking collectives  79.5 us (49%)
  waiting for transfers between devices  38.3 us (24%)
  starting transfers between devices  22 us (14%)
  Pallas kernels  7.13 us (4%)
  matrix products  6.48 us (4%)
  other arithmetic  4.37 us (3%)
  local copies, waits for them, and re-layouts  2.42 us (1%)
    all_to_all x4, blocking collectives, exchange(): return lax.all_to_all(value, axes, split_axis=0, concat_axis=0, tiled=True)  67.3 us
    all_to_all x1, waiting for transfers between devices, exchange(): return lax.all_to_all(value, axes, split_axis=0, concat_axis=0, tiled=True)  38.3 us
    all_to_all x1, starting transfers between devices, exchange(): return lax.all_to_all(value, axes, split_axis=0, concat_axis=0, tiled=True)  22 us
    all_gather x1, blocking collectives, on_device(): weights = lax.all_gather(own, 'r', axis=0, tiled=True)  12.2 us
    pallas_call x1, Pallas kernels, centred_coefficients(): pl.pallas_call(solve_kernel, out_shape=jax.ShapeDtypeStruct((n, n), jnp.f...  7.13 us
    dot_general x2, matrix products, on_device(): jnp.dot(layer, weights, preferred_element_type=jnp.float32)  3.39 us
  transfers between devices with their start and end apart: 1, of which 1 were waited for; matrix products, arithmetic and copies ran while one was open for 0% of the time, Pallas kernels for 0%

profile of v9, /device:TPU:1, one launch (start us, length us, event | category | flops | bytes accessed | tf_op | source)
XLA Modules:
  0.0 161.1 jit_solution(13338169186336930645)
XLA Ops:
  0.0 2.2 %reduce = bf16[98304]{0:T(1024)(128)(2,1)S(1)} reduce(bf16[1,98304]{1,0:T(2,128)(2,1)} %param.16, bf16[]{:T(256)} %constant.25), dimensions={0}, to_apply=%param.16.reduce_sub_computation | reduce | bytes 393218 | tf_op args[6]
  2.2 0.1 reshape.45
  2.3 0.2 copy.29
  2.5 0.0 copy-start.6
  2.5 0.0 copy-start.8
  2.5 0.1 fusion.30
  2.6 12.2 %all_gather.3 = bf16[1024,384]{1,0:T(8,128)(2,1)S(1)} all-gather(bf16[256,384]{1,0:T(8,128)(2,1)S(1)} %reshape.45), channel_id=1, replica_groups=mesh['x'=4,'z'=16,'c'=2,'r'=4] {'r'}, dimensions={0}, use_global_device_ids=true | all-gather | bytes 983040 | tf_op jit(solution)/shard_map/all_gather | solution.py:124
  14.9 1.7 %multiply_reduce_fusion = (f32[512]{0:T(512)S(1)}, f32[512,384]{0,1:T(8,128)S(1)}) fusion(bf16[1024,384]{1,0:T(8,128)(2,1)S(1)} %all_gather.3, bf16[384,1024]{1,0:T(8,128)(2,1)S(1)} %copy-done, f32[1024]{0:T(1024)S(1)} %copy-done.6, bf16[512,384]{0,1:T(8,128)(2,1)S(1)} %copy.29, f32[384]{0:T(512)S(1)} %copy-done.8, f32[512]{0:T(512)S(1)} %add_rsqrt_fusion.1), kind=kOutput, calls=%fused_computation.43 | convolution fusion | flops 812318208 | bytes 2762240 | tf_op jit(solution)/shard_map/dot_general | solution.py:129
  16.6 0.0 copy-start.2
  16.6 1.7 %fusion.19 = f32[512,384,1]{0,1,2:T(8,128)S(1)} fusion(f32[512,384]{0,1:T(8,128)S(1)} %get-tuple-element.15, bf16[1024,384]{1,0:T(8,128)(2,1)S(1)} %all_gather.3, bf16[384,1024]{1,0:T(8,128)(2,1)S(1)} %copy-done, f32[1024]{0:T(1024)S(1)} %copy-done.6, f32[512]{0:T(512)S(1)} %add_rsqrt_fusion, f32[384]{0:T(512)S(1)} %copy-done.8), kind=kOutput, calls=%fused_computation.24 | convolution fusion | flops 811532288 | bytes 3153408 | tf_op jit(solution)/shard_map/dot_general | solution.py:129
  18.3 0.0 copy-start.3
  18.3 0.0 copy-start.4
  18.3 0.0 copy-start.5
  18.4 0.7 fusion.48
  19.0 0.3 copy-done.3
  19.3 0.1 copy-done.4
  19.4 0.1 copy-done.5
  19.5 1.8 %multiply_reduce_fusion.1 = (f32[]{:T(128)}, bf16[2,512,128]{2,1,0:T(8,128)(2,1)S(1)}, bf16[2,512,128]{2,1,0:T(8,128)(2,1)S(1)}) fusion(bf16[1,2,512,128]{3,2,1,0:T(8,128)(2,1)S(1)} %copy-done.4, f32[2,512,128]{2,1,0:T(8,128)S(1)} %copy-done.3, bf16[2,512,128]{2,1,0:T(8,128)(2,1)S(1)} %copy-done.5, f32[2,128,512]{2,1,0:T(8,128)S(1)} %fusion.48, ...), kind=kOutput, calls=%fused_computation.51 | convolution fusion | flops 807272448 | bytes 2101252 | tf_op jit(solution)/shard_map/kib,kbf->kif/dot_general | solution.py:135
  21.3 1.9 %pad_maximum_fusion = bf16[128,11,2,128]{3,2,1,0:T(2,128)(2,1)} fusion(bf16[128,3,2,128]{3,2,1,0:T(2,128)(2,1)S(1)} %bitcast.32, bf16[128,4,2,128]{3,2,1,0:T(2,128)(2,1)S(1)} %bitcast.33, bf16[128,4,2,128]{3,2,1,0:T(2,128)(2,1)S(1)} %bitcast.34), kind=kLoop, calls=%fused_computation.44 | loop fusion | flops 720896 | bytes 1441792 | tf_op jit(solution)/shard_map/concatenate | solution.py:147
  23.1 22.0 %all-to-all-start = ((bf16[128,11,2,128]{3,2,1,0:T(2,128)(2,1)}), bf16[128,11,2,128]{3,2,1,0:T(2,128)(2,1)S(1)}, u32[]{:S(2)}, u32[]{:S(2)}) async-start(bf16[128,11,2,128]{3,2,1,0:T(2,128)(2,1)} %pad_maximum_fusion), calls=%async_computation | async-start | bytes 1441792 | tf_op jit(solution)/shard_map/all_to_all | solution.py:91
  45.8 38.3 %all-to-all-done = bf16[128,11,2,128]{3,2,1,0:T(2,128)(2,1)S(1)} async-done(((bf16[128,11,2,128]{3,2,1,0:T(2,128)(2,1)}), bf16[128,11,2,128]{3,2,1,0:T(2,128)(2,1)S(1)}, u32[]{:S(2)}, u32[]{:S(2)}) %all-to-all-start) | async-done | bytes 720928 | tf_op jit(solution)/shard_map/all_to_all | solution.py:91
  84.1 0.4 fusion.61
  84.5 0.1 slice.12
  84.9 0.3 fusion.23
  85.2 16.9 %all_to_all.25 = f32[32,8,128]{2,1,0:T(8,128)S(1)} all-to-all(f32[32,8,128]{2,1,0:T(8,128)S(1)} %fusion.23), channel_id=1, replica_groups=mesh['x'=4,'z'=16,'c'=2,'r'=4] {'x','c','r'}, dimensions={0} | all-to-all | bytes 262144 | tf_op jit(solution)/shard_map/all_to_all | solution.py:91
  102.1 14.3 %all_to_all.26 = f32[16,8,128]{2,1,0:T(8,128)S(1)} all-to-all(f32[16,8,128]{2,1,0:T(8,128)S(1)} %broadcast_in_dim.14), channel_id=1, replica_groups=mesh['x'=4,'z'=16,'c'=2,'r'=4] {'z'}, dimensions={0} | all-to-all | bytes 131072 | tf_op jit(solution)/shard_map/all_to_all | solution.py:91
  116.4 12.9 %all_to_all.27 = f32[32,8,128]{2,1,0:T(8,128)S(1)} all-to-all(f32[32,8,128]{2,1,0:T(8,128)S(1)} %broadcast_in_dim.15), channel_id=1, replica_groups=mesh['x'=4,'z'=16,'c'=2,'r'=4] {'x','c','r'}, dimensions={0} | all-to-all | bytes 262144 | tf_op jit(solution)/shard_map/all_to_all | solution.py:91
  129.3 7.1 %shard_map.100 = f32[128,128]{1,0:T(8,128)S(1)} custom-call(f32[256,128]{1,0:T(8,128)S(1)} %bitcast.31), custom_call_target="tpu_custom_call" | custom-call | flops 40000000 | bytes 200000 | tf_op jit(solution)/shard_map/pallas_call | solution.py:82
  136.4 0.4 fusion.21
  136.8 0.2 copy.36
  137.0 23.3 %all_to_all.28 = bf16[128,3,2,128]{3,2,1,0:T(2,128)(2,1)S(1)} all-to-all(bf16[128,3,2,128]{3,2,1,0:T(2,128)(2,1)S(1)} %copy.36), channel_id=1, replica_groups=mesh['x'=4,'z'=16,'c'=2,'r'=4] {'z','x','c'}, dimensions={0} | all-to-all | bytes 393216 | tf_op jit(solution)/shard_map/all_to_all | solution.py:91
  160.3 0.8 reshape.50
  (21 shorter events, 0.3 us)
Async XLA Ops:
  0.0 14.9 %copy-start = (bf16[384,1024]{1,0:T(8,128)(2,1)S(1)}, bf16[384,1024]{1,0:T(8,128)(2,1)}, u32[]{:S(2)}) copy-start(bf16[384,1024]{1,0:T(8,128)(2,1)} %param.14) | copy-start | bytes 2359300
  0.0 2.3 %copy-start.1 = (bf16[512,384]{1,0:T(8,128)(2,1)S(1)}, bf16[512,384]{1,0:T(8,128)(2,1)}, u32[]{:S(2)}) copy-start(bf16[512,384]{1,0:T(8,128)(2,1)} %param.10) | copy-start | bytes 1179652
  2.5 12.4 %copy-start.6 = (f32[1024]{0:T(1024)S(1)}, f32[1024]{0:T(1024)}, u32[]{:S(2)}) copy-start(f32[1024]{0:T(1024)} %param.15) | copy-start | bytes 12292
  2.5 12.4 %copy-start.8 = (f32[384]{0:T(512)S(1)}, f32[384]{0:T(512)}, u32[]{:S(2)}) copy-start(f32[384]{0:T(512)} %param.13) | copy-start | bytes 4612
  16.6 1.7 %copy-start.2 = (s32[2,128]{1,0:T(2,128)S(1)}, s32[2,128]{1,0:T(2,128)}, u32[]{:S(2)}) copy-start(s32[2,128]{1,0:T(2,128)} %param.12) | copy-start | bytes 3076
  18.3 1.0 copy-start.3
  18.3 1.1 copy-start.4
  18.3 1.2 copy-start.5
  18.3 1.2 copy-start.7
  23.1 61.0 %all-to-all-start = ((bf16[128,11,2,128]{3,2,1,0:T(2,128)(2,1)}), bf16[128,11,2,128]{3,2,1,0:T(2,128)(2,1)S(1)}, u32[]{:S(2)}, u32[]{:S(2)}) async-start(bf16[128,11,2,128]{3,2,1,0:T(2,128)(2,1)} %pad_maximum_fusion), calls=%async_computation | async-start | bytes 1441792 | tf_op jit(solution)/shard_map/all_to_all | solution.py:91

commit v10 on v9

--- a/solution.py
+++ b/solution.py
@@ -12,6 +12,7 @@
 OWNERS = ("x", "z", "c")
 NEAR = ("x", "c", "r")
 BLOCK = 8
+LANES = 128
 HIGHEST = lax.Precision.HIGHEST
 
 
@@ -24,56 +25,82 @@
     )
 
 
-def eliminate(left, right):
-    wide = lambda v: jnp.broadcast_to(v, left[0].shape)
-    cols = [[wide(tile[:, q : q + 1]) for q in range(BLOCK)] for tile in left]
-    pivots = [[wide(cols[0][q][p : p + 1]) for q in range(p + 1)] for p in range(BLOCK)]
-    top = [wide(left[0][p : p + 1]) for p in range(BLOCK)]
-    side = [wide(right[0][p : p + 1]) for p in range(BLOCK)]
+def wide(value):
+    return jnp.broadcast_to(value, (BLOCK, value.shape[1] if value.shape[1] > 1 else LANES))
+
+
+def split(value):
+    head = value.astype(jnp.bfloat16).astype(jnp.float32)
+    rest = value - head
+    middle = rest.astype(jnp.bfloat16).astype(jnp.float32)
+    return head, middle, rest - middle
+
+
+def pivot_rows(left, right):
+    cols = [wide(left[:, q : q + 1]) for q in range(BLOCK)]
+    pivots = [[wide(cols[q][p : p + 1]) for q in range(p + 1)] for p in range(BLOCK)]
+    top = [wide(left[p : p + 1]) for p in range(BLOCK)]
+    side = [wide(right[p : p + 1]) for p in range(BLOCK)]
     factors = {}
-    for p in range(BLOCK):
-        inverse = 1.0 / pivots[p][p]
-        for q in range(p + 1, BLOCK):
-            factors[q, p] = factor = pivots[q][p] * inverse
-            for c in range(p + 1, q + 1):
-                pivots[q][c] = pivots[q][c] - factor * pivots[c][p]
-            top[q] = top[q] - factor * top[p]
-            side[q] = side[q] - factor * side[p]
-        top[p] = top[p] * inverse
-        side[p] = side[p] * inverse
-    for p in reversed(range(BLOCK)):
-        for q in range(p):
+    for p in range(0, BLOCK, 2):
+        a, b, d = pivots[p][p], pivots[p + 1][p], pivots[p + 1][p + 1]
+        inverse = 1.0 / (a * d - b * b)
+        ia, ib, id_ = d * inverse, -(b * inverse), a * inverse
+        for q in range(p + 2, BLOCK):
+            factors[q, p] = f = pivots[q][p] * ia + pivots[q][p + 1] * ib
+            factors[q, p + 1] = g = pivots[q][p] * ib + pivots[q][p + 1] * id_
+            for c in range(p + 2, q + 1):
+                pivots[q][c] = pivots[q][c] - f * pivots[c][p] - g * pivots[c][p + 1]
+            top[q] = top[q] - f * top[p] - g * top[p + 1]
+            side[q] = side[q] - f * side[p] - g * side[p + 1]
+        for rows in (top, side):
+            rows[p], rows[p + 1] = ia * rows[p] + ib * rows[p + 1], ib * rows[p] + id_ * rows[p + 1]
+    for p in reversed(range(2, BLOCK)):
+        for q in range(p // 2 * 2):
             top[q] = top[q] - factors[p, q] * top[p]
             side[q] = side[q] - factors[p, q] * side[p]
-    row = lax.broadcasted_iota(jnp.int32, left[0].shape, 0)
-    last_left, last_right = top[0], side[0]
+    row = lax.broadcasted_iota(jnp.int32, left.shape, 0)
+    tile, side_tile = top[0], side[0]
     for p in range(1, BLOCK):
-        last_left = jnp.where(row == p, top[p], last_left)
-        last_right = jnp.where(row == p, side[p], last_right)
-    next_left, next_right = [], []
-    for t in range(1, len(left)):
-        a, b = left[t], right[t]
-        for q in range(BLOCK):
-            a = a - cols[t][q] * top[q]
-            b = b - cols[t][q] * side[q]
-        next_left.append(a)
-        next_right.append(b)
-    next_left.append(last_left)
-    next_right.append(last_right)
-    turn = left[0].shape[1] - BLOCK
-    return [pltpu.roll(a, turn, 1) for a in next_left], next_right
+        tile = jnp.where(row == p, top[p], tile)
+        side_tile = jnp.where(row == p, side[p], side_tile)
+    return tile, side_tile, top, side
+
+
+def eliminate(left, right, tile, side_tile):
+    n = left.shape[0]
+    tile, side_tile, top, side = pivot_rows(tile, side_tile)
+    near, near_side = left[BLOCK : 2 * BLOCK], right[BLOCK : 2 * BLOCK]
+    cols = [wide(near[:, q : q + 1]) for q in range(BLOCK)]
+    for q in range(BLOCK):
+        near = near - cols[q] * top[q]
+        near_side = near_side - cols[q] * side[q]
+    column = lax.broadcasted_iota(jnp.int32, left.shape, 1)
+    a, b, c = split(jnp.where(column < BLOCK, left, 0.0))
+    factor = a
+    for place, part in enumerate((a, a, b, b, c)):
+        factor = factor + pltpu.roll(part, (place + 1) * BLOCK, 1)
+    a, b, c = split(jnp.concatenate([tile, side_tile], axis=1))
+    unused = jnp.zeros((n - 6 * BLOCK, 2 * n), jnp.float32)
+    rows = jnp.concatenate([a, b, c, a, b, a, unused], axis=0)
+    change = jnp.dot(
+        factor.astype(jnp.bfloat16), rows.astype(jnp.bfloat16), preferred_element_type=jnp.float32
+    )
+    left = jnp.concatenate([(left - change[:, :n])[BLOCK:], tile], axis=0)
+    right = jnp.concatenate([(right - change[:, n:])[BLOCK:], side_tile], axis=0)
+    return pltpu.roll(left, n - BLOCK, 1), right, pltpu.roll(near, n - BLOCK, 1), near_side
 
 
 def solve_kernel(total_ref, out_ref):
     n = out_ref.shape[0]
     row = lax.broadcasted_iota(jnp.int32, (n, n), 0)
     column = lax.broadcasted_iota(jnp.int32, (n, n), 1)
-    system = total_ref[:n] + jnp.where(row == column, n - 1.0, 0.0)
-    right_side = total_ref[n:].T
-    left = [system[t : t + BLOCK] for t in range(0, n, BLOCK)]
-    right = [right_side[t : t + BLOCK] for t in range(0, n, BLOCK)]
-    _, solved = lax.fori_loop(0, n // BLOCK, lambda _, lr: eliminate(*lr), (left, right))
-    solved = jnp.concatenate(solved, axis=0)
+    left = total_ref[:n] + jnp.where(row == column, n - 1.0, 0.0)
+    right = total_ref[n:].T
+    state = (left, right, left[:BLOCK], right[:BLOCK])
+    for _ in range(n // BLOCK):
+        state = eliminate(*state)
+    solved = state[1]
     out_ref[...] = solved - jnp.mean(solved, axis=0, keepdims=True)
 
 
@@ -83,7 +110,7 @@
         solve_kernel,
         out_shape=jax.ShapeDtypeStruct((n, n), jnp.float32),
         cost_estimate=pl.CostEstimate(flops=40000000, bytes_accessed=200000, transcendentals=0),
-        compiler_params=pltpu.CompilerParams(vmem_limit_bytes=4 * 1024 * 1024),
+        compiler_params=pltpu.CompilerParams(vmem_limit_bytes=8 * 1024 * 1024),
     )(total)
 
 
@@ -142,9 +169,13 @@
     entries = members * step_count * rows * lax.axis_size("r") * picked
     pairs = (members, -1, 2, picked)
     pairs = (members, -1, 2, picked)
-    sent = [weighted.reshape(pairs), misfit_w.reshape(pairs), own.reshape(pairs)]
-    depth = sent[0].shape[1]
-    arrived = exchange(jnp.concatenate(sent, axis=1), MEM)
+    depth = step_count * rows // members // 2
+    sent = lax.pad(
+        own.reshape(pairs), jnp.bfloat16(0), ((0, 0, 0), (2 * depth, 0, 0), (0, 0, 0), (0, 0, 0))
+    )
+    sent = lax.dynamic_update_slice(sent, weighted.reshape(pairs), (0, 0, 0, 0))
+    sent = lax.dynamic_update_slice(sent, misfit_w.reshape(pairs), (0, depth, 0, 0))
+    arrived = exchange(sent, MEM)
     gathered = arrived[:, :depth].astype(jnp.float32)
     misfit_here = arrived[:, depth : 2 * depth]
     param_block = arrived[:, 2 * depth :]

time: 162 us -> 161 us (level)
  local copies, waits for them, and re-layouts: 2.42 us -> 5.03 us
  Pallas kernels: 7.13 us -> 4.91 us
  other arithmetic: 4.37 us -> 2.48 us
    pallas_call x1, Pallas kernels: 7.13 us -> 4.91 us  [centred_coefficients(): pl.pallas_call(solve_kernel, out_shape=jax.ShapeDtypeStruct((n, n), jnp.f...]
    concatenate x1 -> x0, other arithmetic: 1.89 us -> none  [on_device(): arrived = exchange(jnp.concatenate(sent, axis=1), MEM)]
    dynamic_update_slice x0 -> x2, local copies, waits for them, and re-layouts: none -> 1.81 us  [the longest x1 0.91 us: on_device(): lax.dynamic_update_slice(sent, misfit_w.reshape(pairs), (0, depth, 0, 0))]
where the time goes in v10:
time: 161 us; the launch traced here: 160 us
  blocking collectives  79.5 us (49%)
  waiting for transfers between devices  38.3 us (24%)
  starting transfers between devices  22 us (14%)
  matrix products  6.52 us (4%)
  local copies, waits for them, and re-layouts  5.03 us (3%)
  Pallas kernels  4.91 us (3%)
  other arithmetic  2.48 us (2%)
    all_to_all x4, blocking collectives, exchange(): return lax.all_to_all(value, axes, split_axis=0, concat_axis=0, tiled=True)  67.3 us
    all_to_all x1, waiting for transfers between devices, exchange(): return lax.all_to_all(value, axes, split_axis=0, concat_axis=0, tiled=True)  38.3 us
    all_to_all x1, starting transfers between devices, exchange(): return lax.all_to_all(value, axes, split_axis=0, concat_axis=0, tiled=True)  22 us
    all_gather x1, blocking collectives, on_device(): weights = lax.all_gather(own, 'r', axis=0, tiled=True)  12.2 us
    pallas_call x1, Pallas kernels, centred_coefficients(): pl.pallas_call(solve_kernel, out_shape=jax.ShapeDtypeStruct((n, n), jnp.f...  4.91 us
    dot_general x2, matrix products, on_device(): jnp.dot(layer, weights, preferred_element_type=jnp.float32)  3.39 us
  transfers between devices with their start and end apart: 1, of which 1 were waited for; matrix products, arithmetic and copies ran while one was open for 0% of the time, Pallas kernels for 0%

profile of v10, /device:TPU:1, one launch (start us, length us, event | category | flops | bytes accessed | tf_op | source)
XLA Modules:
  0.0 159.7 jit_solution(3851962404919582671)
XLA Ops:
  0.0 2.2 %reduce = bf16[98304]{0:T(1024)(128)(2,1)S(1)} reduce(bf16[1,98304]{1,0:T(2,128)(2,1)} %param.16, bf16[]{:T(256)} %constant.33), dimensions={0}, to_apply=%param.16.reduce_sub_computation | reduce | bytes 393218 | tf_op args[6]
  2.2 0.1 reshape.45
  2.3 0.2 copy.29
  2.5 0.0 copy-start.6
  2.5 0.0 copy-start.8
  2.5 0.1 fusion.30
  2.6 12.2 %all_gather.3 = bf16[1024,384]{1,0:T(8,128)(2,1)S(1)} all-gather(bf16[256,384]{1,0:T(8,128)(2,1)S(1)} %reshape.45), channel_id=1, replica_groups=mesh['x'=4,'z'=16,'c'=2,'r'=4] {'r'}, dimensions={0}, use_global_device_ids=true | all-gather | bytes 983040 | tf_op jit(solution)/shard_map/all_gather | solution.py:151
  14.9 1.7 %multiply_reduce_fusion = (f32[512]{0:T(512)S(1)}, f32[512,384]{0,1:T(8,128)S(1)}) fusion(bf16[1024,384]{1,0:T(8,128)(2,1)S(1)} %all_gather.3, bf16[384,1024]{1,0:T(8,128)(2,1)S(1)} %copy-done, f32[1024]{0:T(1024)S(1)} %copy-done.6, bf16[512,384]{0,1:T(8,128)(2,1)S(1)} %copy.29, f32[384]{0:T(512)S(1)} %copy-done.8, f32[512]{0:T(512)S(1)} %add_rsqrt_fusion.1), kind=kOutput, calls=%fused_computation.43 | convolution fusion | flops 812318208 | bytes 2762240 | tf_op jit(solution)/shard_map/dot_general | solution.py:156
  16.6 0.0 copy-start.2
  16.6 1.7 %fusion.19 = f32[512,384,1]{0,1,2:T(8,128)S(1)} fusion(f32[512,384]{0,1:T(8,128)S(1)} %get-tuple-element.15, bf16[1024,384]{1,0:T(8,128)(2,1)S(1)} %all_gather.3, bf16[384,1024]{1,0:T(8,128)(2,1)S(1)} %copy-done, f32[1024]{0:T(1024)S(1)} %copy-done.6, f32[512]{0:T(512)S(1)} %add_rsqrt_fusion, f32[384]{0:T(512)S(1)} %copy-done.8), kind=kOutput, calls=%fused_computation.24 | convolution fusion | flops 811532288 | bytes 3153408 | tf_op jit(solution)/shard_map/dot_general | solution.py:156
  18.3 0.0 copy-start.5
  18.3 0.7 fusion.48
  19.0 0.0 copy-start.3
  19.0 0.0 copy-start.4
  19.0 0.0 copy-start.7
  19.0 1.3 pad.3
  20.3 1.8 %multiply_reduce_fusion.1 = (f32[]{:T(128)}, bf16[2,512,128]{2,1,0:T(8,128)(2,1)S(1)}, bf16[2,512,128]{2,1,0:T(8,128)(2,1)S(1)}) fusion(bf16[1,2,512,128]{3,2,1,0:T(8,128)(2,1)S(1)} %copy-done.4, f32[2,512,128]{2,1,0:T(8,128)S(1)} %copy-done.3, bf16[2,512,128]{2,1,0:T(8,128)(2,1)S(1)} %copy-done.5, f32[2,128,512]{2,1,0:T(8,128)S(1)} %fusion.48, ...), kind=kOutput, calls=%fused_computation.50 | convolution fusion | flops 807272448 | bytes 2101252 | tf_op jit(solution)/shard_map/kib,kbf->kif/dot_general | solution.py:162
  22.1 0.9 constant_dynamic-update-slice_fusion.1
  23.0 0.9 constant_dynamic-update-slice_fusion
  23.9 22.0 %all-to-all-start = ((bf16[128,11,2,128]{3,2,1,0:T(2,128)(2,1)}), bf16[128,11,2,128]{3,2,1,0:T(2,128)(2,1)S(1)}, u32[]{:S(2)}, u32[]{:S(2)}) async-start(bf16[128,11,2,128]{3,2,1,0:T(2,128)(2,1)} %constant_dynamic-update-slice_fusion), calls=%async_computation | async-start | bytes 1441792 | tf_op jit(solution)/shard_map/all_to_all | solution.py:118
  46.6 38.3 %all-to-all-done = bf16[128,11,2,128]{3,2,1,0:T(2,128)(2,1)S(1)} async-done(((bf16[128,11,2,128]{3,2,1,0:T(2,128)(2,1)}), bf16[128,11,2,128]{3,2,1,0:T(2,128)(2,1)S(1)}, u32[]{:S(2)}, u32[]{:S(2)}) %all-to-all-start) | async-done | bytes 720928 | tf_op jit(solution)/shard_map/all_to_all | solution.py:118
  84.9 0.4 fusion.61
  85.3 0.1 slice.12
  85.6 0.3 fusion.23
  85.9 16.9 %all_to_all.25 = f32[32,8,128]{2,1,0:T(8,128)S(1)} all-to-all(f32[32,8,128]{2,1,0:T(8,128)S(1)} %fusion.23), channel_id=1, replica_groups=mesh['x'=4,'z'=16,'c'=2,'r'=4] {'x','c','r'}, dimensions={0} | all-to-all | bytes 262144 | tf_op jit(solution)/shard_map/all_to_all | solution.py:118
  102.9 14.3 %all_to_all.26 = f32[16,8,128]{2,1,0:T(8,128)S(1)} all-to-all(f32[16,8,128]{2,1,0:T(8,128)S(1)} %broadcast_in_dim.14), channel_id=1, replica_groups=mesh['x'=4,'z'=16,'c'=2,'r'=4] {'z'}, dimensions={0} | all-to-all | bytes 131072 | tf_op jit(solution)/shard_map/all_to_all | solution.py:118
  117.2 12.9 %all_to_all.27 = f32[32,8,128]{2,1,0:T(8,128)S(1)} all-to-all(f32[32,8,128]{2,1,0:T(8,128)S(1)} %broadcast_in_dim.15), channel_id=1, replica_groups=mesh['x'=4,'z'=16,'c'=2,'r'=4] {'x','c','r'}, dimensions={0} | all-to-all | bytes 262144 | tf_op jit(solution)/shard_map/all_to_all | solution.py:118
  130.1 4.9 %shard_map.100 = f32[128,128]{1,0:T(8,128)S(1)} custom-call(f32[256,128]{1,0:T(8,128)S(1)} %bitcast.31), custom_call_target="tpu_custom_call" | custom-call | flops 40000000 | bytes 200000 | tf_op jit(solution)/shard_map/pallas_call | solution.py:109
  135.0 0.4 fusion.21
  135.4 0.2 copy.36
  135.6 23.3 %all_to_all.28 = bf16[128,3,2,128]{3,2,1,0:T(2,128)(2,1)S(1)} all-to-all(bf16[128,3,2,128]{3,2,1,0:T(2,128)(2,1)S(1)} %copy.36), channel_id=1, replica_groups=mesh['x'=4,'z'=16,'c'=2,'r'=4] {'z','x','c'}, dimensions={0} | all-to-all | bytes 393216 | tf_op jit(solution)/shard_map/all_to_all | solution.py:118
  158.8 0.8 reshape.50
  (23 shorter events, 0.3 us)
Async XLA Ops:
  0.0 14.9 %copy-start = (bf16[384,1024]{1,0:T(8,128)(2,1)S(1)}, bf16[384,1024]{1,0:T(8,128)(2,1)}, u32[]{:S(2)}) copy-start(bf16[384,1024]{1,0:T(8,128)(2,1)} %param.14) | copy-start | bytes 2359300
  0.0 2.3 %copy-start.1 = (bf16[512,384]{1,0:T(8,128)(2,1)S(1)}, bf16[512,384]{1,0:T(8,128)(2,1)}, u32[]{:S(2)}) copy-start(bf16[512,384]{1,0:T(8,128)(2,1)} %param.10) | copy-start | bytes 1179652
  2.5 12.4 %copy-start.6 = (f32[1024]{0:T(1024)S(1)}, f32[1024]{0:T(1024)}, u32[]{:S(2)}) copy-start(f32[1024]{0:T(1024)} %param.15) | copy-start | bytes 12292
  2.5 12.4 %copy-start.8 = (f32[384]{0:T(512)S(1)}, f32[384]{0:T(512)}, u32[]{:S(2)}) copy-start(f32[384]{0:T(512)} %param.13) | copy-start | bytes 4612
  16.6 1.7 %copy-start.2 = (s32[2,128]{1,0:T(2,128)S(1)}, s32[2,128]{1,0:T(2,128)}, u32[]{:S(2)}) copy-start(s32[2,128]{1,0:T(2,128)} %param.12) | copy-start | bytes 3076
  18.3 2.0 %copy-start.5 = (bf16[2,512,128]{2,1,0:T(8,128)(2,1)S(1)}, bf16[2,512,128]{2,1,0:T(8,128)(2,1)}, u32[]{:S(2)}) copy-start(bf16[2,512,128]{2,1,0:T(8,128)(2,1)} %param.17) | copy-start | bytes 786436
  19.0 1.3 copy-start.3
  19.0 1.3 copy-start.4
  19.0 1.3 copy-start.7
  23.9 61.0 %all-to-all-start = ((bf16[128,11,2,128]{3,2,1,0:T(2,128)(2,1)}), bf16[128,11,2,128]{3,2,1,0:T(2,128)(2,1)S(1)}, u32[]{:S(2)}, u32[]{:S(2)}) async-start(bf16[128,11,2,128]{3,2,1,0:T(2,128)(2,1)} %constant_dynamic-update-slice_fusion), calls=%async_computation | async-start | bytes 1441792 | tf_op jit(solution)/shard_map/all_to_all | solution.py:118

commit v11 on v10

--- a/solution.py
+++ b/solution.py
@@ -169,12 +169,10 @@
     entries = members * step_count * rows * lax.axis_size("r") * picked
     pairs = (members, -1, 2, picked)
     pairs = (members, -1, 2, picked)
-    depth = step_count * rows // members // 2
-    sent = lax.pad(
-        own.reshape(pairs), jnp.bfloat16(0), ((0, 0, 0), (2 * depth, 0, 0), (0, 0, 0), (0, 0, 0))
-    )
-    sent = lax.dynamic_update_slice(sent, weighted.reshape(pairs), (0, 0, 0, 0))
-    sent = lax.dynamic_update_slice(sent, misfit_w.reshape(pairs), (0, depth, 0, 0))
+    sent = [weighted.reshape(pairs), misfit_w.reshape(pairs), own.reshape(pairs)]
+    depth = sent[0].shape[1]
+    misfit_share = misfit_local * ((members - 1) / entries)
+    sent, misfit_share = lax.optimization_barrier((jnp.concatenate(sent, axis=1), misfit_share))
     arrived = exchange(sent, MEM)
     gathered = arrived[:, :depth].astype(jnp.float32)
     misfit_here = arrived[:, depth : 2 * depth]
@@ -188,7 +186,7 @@
     unit = lax.broadcasted_iota(jnp.int32, partial.shape, 0) == lax.broadcasted_iota(
         jnp.int32, partial.shape, 1
     )
-    partial = partial + jnp.where(unit, misfit_local * ((members - 1) / entries), 0.0)
+    partial = partial + jnp.where(unit, misfit_share, 0.0)
     total = total_of(partial)
     centred = centred_coefficients(total)
     params_f = param_block.astype(jnp.float32)

time: 161 us -> 160 us (level)
  blocking collectives: 79.5 us -> 140 us
  waiting for transfers between devices: 38.3 us -> 0 us
  starting transfers between devices: 22 us -> 0 us
  local copies, waits for them, and re-layouts: 5.03 us -> 2.42 us
    all_to_all x4 -> x5, blocking collectives: 67.3 us -> 128 us  [exchange(): return lax.all_to_all(value, axes, split_axis=0, concat_axis=0, tiled=True)]
    all_to_all x1 -> x0, waiting for transfers between devices: 38.3 us -> none  [exchange(): return lax.all_to_all(value, axes, split_axis=0, concat_axis=0, tiled=True)]
    all_to_all x1 -> x0, starting transfers between devices: 22 us -> none  [exchange(): return lax.all_to_all(value, axes, split_axis=0, concat_axis=0, tiled=True)]
    dynamic_update_slice x2 -> x0, local copies, waits for them, and re-layouts: 1.81 us -> none  [the longest x1 0.91 us: on_device(): lax.dynamic_update_slice(sent, misfit_w.reshape(pairs), (0, depth, 0, 0))]
  transfers between devices with their start and end apart: 1 -> 0, of which waited for: 1 -> 0; matrix products, arithmetic and copies ran while one was open for 0% -> 0% of each run, Pallas kernels for 0% -> 0%
where the time goes in v11:
time: 160 us; the launch traced here: 158 us
  blocking collectives  140 us (88%)
  matrix products  6.48 us (4%)
  Pallas kernels  4.91 us (3%)
  other arithmetic  3.52 us (2%)
  local copies, waits for them, and re-layouts  2.42 us (2%)
    all_to_all x5, blocking collectives, exchange(): return lax.all_to_all(value, axes, split_axis=0, concat_axis=0, tiled=True)  128 us
    all_gather x1, blocking collectives, on_device(): weights = lax.all_gather(own, 'r', axis=0, tiled=True)  12.2 us
    pallas_call x1, Pallas kernels, centred_coefficients(): pl.pallas_call(solve_kernel, out_shape=jax.ShapeDtypeStruct((n, n), jnp.f...  4.91 us
    dot_general x2, matrix products, on_device(): jnp.dot(layer, weights, preferred_element_type=jnp.float32)  3.39 us

profile of v11, /device:TPU:1, one launch (start us, length us, event | category | flops | bytes accessed | tf_op | source)
XLA Modules:
  0.0 158.5 jit_solution(2209357384306450379)
XLA Ops:
  0.0 2.2 %reduce = bf16[98304]{0:T(1024)(128)(2,1)S(1)} reduce(bf16[1,98304]{1,0:T(2,128)(2,1)} %param.16, bf16[]{:T(256)} %constant.25), dimensions={0}, to_apply=%param.16.reduce_sub_computation | reduce | bytes 393218 | tf_op args[6]
  2.2 0.1 reshape.45
  2.3 0.2 copy.29
  2.5 0.0 copy-start.6
  2.5 0.0 copy-start.8
  2.5 0.1 fusion.30
  2.6 12.2 %all_gather.3 = bf16[1024,384]{1,0:T(8,128)(2,1)S(1)} all-gather(bf16[256,384]{1,0:T(8,128)(2,1)S(1)} %reshape.45), channel_id=1, replica_groups=mesh['x'=4,'z'=16,'c'=2,'r'=4] {'r'}, dimensions={0}, use_global_device_ids=true | all-gather | bytes 983040 | tf_op jit(solution)/shard_map/all_gather | solution.py:151
  14.9 1.7 %multiply_reduce_fusion = (f32[512]{0:T(512)S(1)}, f32[512,384]{0,1:T(8,128)S(1)}) fusion(bf16[1024,384]{1,0:T(8,128)(2,1)S(1)} %all_gather.3, bf16[384,1024]{1,0:T(8,128)(2,1)S(1)} %copy-done, f32[1024]{0:T(1024)S(1)} %copy-done.6, bf16[512,384]{0,1:T(8,128)(2,1)S(1)} %copy.29, f32[384]{0:T(512)S(1)} %copy-done.8, f32[512]{0:T(512)S(1)} %add_rsqrt_fusion.1), kind=kOutput, calls=%fused_computation.43 | convolution fusion | flops 812318208 | bytes 2762240 | tf_op jit(solution)/shard_map/dot_general | solution.py:156
  16.6 0.0 copy-start.2
  16.6 1.7 %fusion.19 = f32[512,384,1]{0,1,2:T(8,128)S(1)} fusion(f32[512,384]{0,1:T(8,128)S(1)} %get-tuple-element.19, bf16[1024,384]{1,0:T(8,128)(2,1)S(1)} %all_gather.3, bf16[384,1024]{1,0:T(8,128)(2,1)S(1)} %copy-done, f32[1024]{0:T(1024)S(1)} %copy-done.6, f32[512]{0:T(512)S(1)} %add_rsqrt_fusion, f32[384]{0:T(512)S(1)} %copy-done.8), kind=kOutput, calls=%fused_computation.24 | convolution fusion | flops 811532288 | bytes 3153408 | tf_op jit(solution)/shard_map/dot_general | solution.py:156
  18.3 0.0 copy-start.3
  18.3 0.0 copy-start.4
  18.3 0.0 copy-start.5
  18.3 0.0 copy-start.7
  18.4 0.7 fusion.48
  19.0 0.3 copy-done.3
  19.3 0.1 copy-done.4
  19.4 0.1 copy-done.5
  19.5 1.8 %multiply_reduce_fusion.1 = (f32[]{:T(128)}, bf16[2,512,128]{2,1,0:T(8,128)(2,1)S(1)}, bf16[2,512,128]{2,1,0:T(8,128)(2,1)S(1)}) fusion(bf16[1,2,512,128]{3,2,1,0:T(8,128)(2,1)S(1)} %copy-done.4, f32[2,512,128]{2,1,0:T(8,128)S(1)} %copy-done.3, bf16[2,512,128]{2,1,0:T(8,128)(2,1)S(1)} %copy-done.5, f32[2,128,512]{2,1,0:T(8,128)S(1)} %fusion.48, ...), kind=kOutput, calls=%fused_computation.52 | convolution fusion | flops 807272448 | bytes 2101252 | tf_op jit(solution)/shard_map/kib,kbf->kif/dot_general | solution.py:162
  21.9 1.0 pad_maximum_fusion
  23.0 60.8 %all_to_all.25 = bf16[128,11,2,128]{3,2,1,0:T(2,128)(2,1)S(1)} all-to-all(bf16[128,11,2,128]{3,2,1,0:T(2,128)(2,1)S(1)} %pad_maximum_fusion), channel_id=1, replica_groups=mesh['x'=4,'z'=16,'c'=2,'r'=4] {'z','x','c'}, dimensions={0} | all-to-all | bytes 1441792 | tf_op jit(solution)/shard_map/all_to_all | solution.py:118
  83.7 0.4 fusion.61
  84.1 0.1 slice.12
  84.5 0.3 fusion.23
  84.8 16.9 %all_to_all.26 = f32[32,8,128]{2,1,0:T(8,128)S(1)} all-to-all(f32[32,8,128]{2,1,0:T(8,128)S(1)} %fusion.23), channel_id=1, replica_groups=mesh['x'=4,'z'=16,'c'=2,'r'=4] {'x','c','r'}, dimensions={0} | all-to-all | bytes 262144 | tf_op jit(solution)/shard_map/all_to_all | solution.py:118
  101.7 14.3 %all_to_all.27 = f32[16,8,128]{2,1,0:T(8,128)S(1)} all-to-all(f32[16,8,128]{2,1,0:T(8,128)S(1)} %broadcast_in_dim.14), channel_id=1, replica_groups=mesh['x'=4,'z'=16,'c'=2,'r'=4] {'z'}, dimensions={0} | all-to-all | bytes 131072 | tf_op jit(solution)/shard_map/all_to_all | solution.py:118
  116.0 12.9 %all_to_all.28 = f32[32,8,128]{2,1,0:T(8,128)S(1)} all-to-all(f32[32,8,128]{2,1,0:T(8,128)S(1)} %broadcast_in_dim.15), channel_id=1, replica_groups=mesh['x'=4,'z'=16,'c'=2,'r'=4] {'x','c','r'}, dimensions={0} | all-to-all | bytes 262144 | tf_op jit(solution)/shard_map/all_to_all | solution.py:118
  128.9 4.9 %shard_map.100 = f32[128,128]{1,0:T(8,128)S(1)} custom-call(f32[256,128]{1,0:T(8,128)S(1)} %bitcast.31), custom_call_target="tpu_custom_call" | custom-call | flops 40000000 | bytes 200000 | tf_op jit(solution)/shard_map/pallas_call | solution.py:109
  133.8 0.4 fusion.21
  134.2 0.2 copy.36
  134.4 23.3 %all_to_all.29 = bf16[128,3,2,128]{3,2,1,0:T(2,128)(2,1)S(1)} all-to-all(bf16[128,3,2,128]{3,2,1,0:T(2,128)(2,1)S(1)} %copy.36), channel_id=1, replica_groups=mesh['x'=4,'z'=16,'c'=2,'r'=4] {'z','x','c'}, dimensions={0} | all-to-all | bytes 393216 | tf_op jit(solution)/shard_map/all_to_all | solution.py:118
  157.7 0.8 reshape.50
  (20 shorter events, 0.3 us)
Async XLA Ops:
  0.0 14.9 %copy-start = (bf16[384,1024]{1,0:T(8,128)(2,1)S(1)}, bf16[384,1024]{1,0:T(8,128)(2,1)}, u32[]{:S(2)}) copy-start(bf16[384,1024]{1,0:T(8,128)(2,1)} %param.14) | copy-start | bytes 2359300
  0.0 2.3 %copy-start.1 = (bf16[512,384]{1,0:T(8,128)(2,1)S(1)}, bf16[512,384]{1,0:T(8,128)(2,1)}, u32[]{:S(2)}) copy-start(bf16[512,384]{1,0:T(8,128)(2,1)} %param.10) | copy-start | bytes 1179652
  2.5 12.4 %copy-start.6 = (f32[1024]{0:T(1024)S(1)}, f32[1024]{0:T(1024)}, u32[]{:S(2)}) copy-start(f32[1024]{0:T(1024)} %param.15) | copy-start | bytes 12292
  2.5 12.4 %copy-start.8 = (f32[384]{0:T(512)S(1)}, f32[384]{0:T(512)}, u32[]{:S(2)}) copy-start(f32[384]{0:T(512)} %param.13) | copy-start | bytes 4612
  16.6 1.7 %copy-start.2 = (s32[2,128]{1,0:T(2,128)S(1)}, s32[2,128]{1,0:T(2,128)}, u32[]{:S(2)}) copy-start(s32[2,128]{1,0:T(2,128)} %param.12) | copy-start | bytes 3076
  18.3 1.0 copy-start.3
  18.3 1.1 copy-start.4
  18.3 1.2 copy-start.5
  18.3 1.2 copy-start.7

commit v12 on v11

--- a/solution.py
+++ b/solution.py
@@ -114,6 +114,19 @@
     )(total)
 
 
+def relayout_kernel(row_ref, out_ref):
+    out_ref[...] = row_ref[...].reshape(out_ref.shape)
+
+
+def lane_rows(row):
+    return pl.pallas_call(
+        relayout_kernel,
+        out_shape=jax.ShapeDtypeStruct((row.shape[1] // LANES, LANES), row.dtype),
+        cost_estimate=pl.CostEstimate(flops=0, bytes_accessed=4 * row.size, transcendentals=0),
+        compiler_params=pltpu.CompilerParams(vmem_limit_bytes=4 * 1024 * 1024),
+    )(row)
+
+
 def exchange(value, axes):
     return lax.all_to_all(value, axes, split_axis=0, concat_axis=0, tiled=True)
 
@@ -147,7 +160,7 @@
     features = w_in.shape[0]
     step_count, rows = batch_index.shape
     picked = obs_pick.shape[1]
-    own = member_params.reshape(-1, features)
+    own = lane_rows(member_params).reshape(-1, features)
     weights = lax.all_gather(own, "r", axis=0, tiled=True)
     step_scale = DT * width ** (-0.5)
     current = states.astype(jnp.float32)
@@ -171,9 +184,7 @@
     pairs = (members, -1, 2, picked)
     sent = [weighted.reshape(pairs), misfit_w.reshape(pairs), own.reshape(pairs)]
     depth = sent[0].shape[1]
-    misfit_share = misfit_local * ((members - 1) / entries)
-    sent, misfit_share = lax.optimization_barrier((jnp.concatenate(sent, axis=1), misfit_share))
-    arrived = exchange(sent, MEM)
+    arrived = exchange(jnp.concatenate(sent, axis=1), MEM)
     gathered = arrived[:, :depth].astype(jnp.float32)
     misfit_here = arrived[:, depth : 2 * depth]
     param_block = arrived[:, 2 * depth :]
@@ -186,7 +197,7 @@
     unit = lax.broadcasted_iota(jnp.int32, partial.shape, 0) == lax.broadcasted_iota(
         jnp.int32, partial.shape, 1
     )
-    partial = partial + jnp.where(unit, misfit_share, 0.0)
+    partial = partial + jnp.where(unit, (members - 1) / entries, 0.0) * misfit_local
     total = total_of(partial)
     centred = centred_coefficients(total)
     params_f = param_block.astype(jnp.float32)

time: 160 us -> 159 us (level)
  other arithmetic: 3.52 us -> 1.34 us
  local copies, waits for them, and re-layouts: 2.42 us -> 4.34 us
    unnamed x1 -> x0, other arithmetic: 2.17 us -> none
    unnamed x20 -> x22, local copies, waits for them, and re-layouts: 0.74 us -> 2.67 us
where the time goes in v12:
time: 159 us; the launch traced here: 158 us
  blocking collectives  140 us (88%)
  matrix products  7.12 us (4%)
  Pallas kernels  4.94 us (3%)
  local copies, waits for them, and re-layouts  4.34 us (3%)
    all_to_all x5, blocking collectives, exchange(): return lax.all_to_all(value, axes, split_axis=0, concat_axis=0, tiled=True)  128 us
    all_gather x1, blocking collectives, on_device(): weights = lax.all_gather(own, 'r', axis=0, tiled=True)  12.2 us
    pallas_call x1, Pallas kernels, centred_coefficients(): pl.pallas_call(solve_kernel, out_shape=jax.ShapeDtypeStruct((n, n), jnp.f...  4.91 us
    dot_general x2, matrix products, on_device(): jnp.dot(layer, weights, preferred_element_type=jnp.float32)  3.39 us

profile of v12, /device:TPU:1, one launch (start us, length us, event | category | flops | bytes accessed | tf_op | source)
XLA Modules:
  0.0 158.3 jit_solution(17601609641487234126)
XLA Ops:
  0.0 1.1 copy-done.1
  1.1 0.1 reshape.45
  1.2 0.9 copy-done.2
  2.1 0.2 copy.30
  2.3 0.0 copy-start.7
  2.3 0.0 copy-start.9
  2.3 0.1 fusion.30
  2.4 12.2 %all_gather.3 = bf16[1024,384]{1,0:T(8,128)(2,1)S(1)} all-gather(bf16[256,384]{1,0:T(8,128)(2,1)S(1)} %reshape.45), channel_id=1, replica_groups=mesh['x'=4,'z'=16,'c'=2,'r'=4] {'r'}, dimensions={0}, use_global_device_ids=true | all-gather | bytes 983040 | tf_op jit(solution)/shard_map/all_gather | solution.py:164
  14.6 1.7 %multiply_reduce_fusion = (f32[512]{0:T(512)S(1)}, f32[512,384]{0,1:T(8,128)S(1)}) fusion(bf16[1024,384]{1,0:T(8,128)(2,1)S(1)} %all_gather.3, bf16[384,1024]{1,0:T(8,128)(2,1)S(1)} %copy-done, f32[1024]{0:T(1024)S(1)} %copy-done.7, bf16[512,384]{0,1:T(8,128)(2,1)S(1)} %copy.30, f32[384]{0:T(512)S(1)} %copy-done.9, f32[512]{0:T(512)S(1)} %add_rsqrt_fusion.1), kind=kOutput, calls=%fused_computation.43 | convolution fusion | flops 812318208 | bytes 2762240 | tf_op jit(solution)/shard_map/dot_general | solution.py:169
  16.4 0.0 copy-start.3
  16.4 1.7 %fusion.19 = f32[512,384,1]{0,1,2:T(8,128)S(1)} fusion(f32[512,384]{0,1:T(8,128)S(1)} %get-tuple-element.15, bf16[1024,384]{1,0:T(8,128)(2,1)S(1)} %all_gather.3, bf16[384,1024]{1,0:T(8,128)(2,1)S(1)} %copy-done, f32[1024]{0:T(1024)S(1)} %copy-done.7, f32[512]{0:T(512)S(1)} %add_rsqrt_fusion, f32[384]{0:T(512)S(1)} %copy-done.9), kind=kOutput, calls=%fused_computation.24 | convolution fusion | flops 811532288 | bytes 3153408 | tf_op jit(solution)/shard_map/dot_general | solution.py:169
  18.1 0.0 copy-start.4
  18.1 0.0 copy-start.5
  18.1 0.0 copy-start.6
  18.1 0.7 fusion.48
  18.8 0.3 copy-done.4
  19.1 0.1 copy-done.5
  19.2 0.1 copy-done.6
  19.3 1.8 %multiply_reduce_fusion.1 = (f32[]{:T(128)}, bf16[2,512,128]{2,1,0:T(8,128)(2,1)S(1)}, bf16[2,512,128]{2,1,0:T(8,128)(2,1)S(1)}) fusion(bf16[1,2,512,128]{3,2,1,0:T(8,128)(2,1)S(1)} %copy-done.5, f32[2,512,128]{2,1,0:T(8,128)S(1)} %copy-done.4, bf16[2,512,128]{2,1,0:T(8,128)(2,1)S(1)} %copy-done.6, f32[2,128,512]{2,1,0:T(8,128)S(1)} %fusion.48, ...), kind=kOutput, calls=%fused_computation.51 | convolution fusion | flops 807272448 | bytes 2101252 | tf_op jit(solution)/shard_map/kib,kbf->kif/dot_general | solution.py:175
  21.0 1.0 pad_maximum_fusion
  22.1 60.8 %all_to_all.25 = bf16[128,11,2,128]{3,2,1,0:T(2,128)(2,1)S(1)} all-to-all(bf16[128,11,2,128]{3,2,1,0:T(2,128)(2,1)S(1)} %pad_maximum_fusion), channel_id=1, replica_groups=mesh['x'=4,'z'=16,'c'=2,'r'=4] {'z','x','c'}, dimensions={0} | all-to-all | bytes 1441792 | tf_op jit(solution)/shard_map/all_to_all | solution.py:131
  82.8 0.4 fusion.61
  83.2 0.1 slice.12
  83.6 0.9 fusion.23
  84.5 16.9 %all_to_all.26 = f32[32,8,128]{2,1,0:T(8,128)S(1)} all-to-all(f32[32,8,128]{2,1,0:T(8,128)S(1)} %fusion.23), channel_id=1, replica_groups=mesh['x'=4,'z'=16,'c'=2,'r'=4] {'x','c','r'}, dimensions={0} | all-to-all | bytes 262144 | tf_op jit(solution)/shard_map/all_to_all | solution.py:131
  101.5 14.3 %all_to_all.27 = f32[16,8,128]{2,1,0:T(8,128)S(1)} all-to-all(f32[16,8,128]{2,1,0:T(8,128)S(1)} %broadcast_in_dim.14), channel_id=1, replica_groups=mesh['x'=4,'z'=16,'c'=2,'r'=4] {'z'}, dimensions={0} | all-to-all | bytes 131072 | tf_op jit(solution)/shard_map/all_to_all | solution.py:131
  115.8 12.9 %all_to_all.28 = f32[32,8,128]{2,1,0:T(8,128)S(1)} all-to-all(f32[32,8,128]{2,1,0:T(8,128)S(1)} %broadcast_in_dim.15), channel_id=1, replica_groups=mesh['x'=4,'z'=16,'c'=2,'r'=4] {'x','c','r'}, dimensions={0} | all-to-all | bytes 262144 | tf_op jit(solution)/shard_map/all_to_all | solution.py:131
  128.7 4.9 %shard_map.101 = f32[128,128]{1,0:T(8,128)S(1)} custom-call(f32[256,128]{1,0:T(8,128)S(1)} %bitcast.32), custom_call_target="tpu_custom_call" | custom-call | flops 40000000 | bytes 200000 | tf_op jit(solution)/shard_map/pallas_call | solution.py:109
  133.6 0.4 fusion.21
  134.0 0.2 copy.37
  134.2 23.3 %all_to_all.29 = bf16[128,3,2,128]{3,2,1,0:T(2,128)(2,1)S(1)} all-to-all(bf16[128,3,2,128]{3,2,1,0:T(2,128)(2,1)S(1)} %copy.37), channel_id=1, replica_groups=mesh['x'=4,'z'=16,'c'=2,'r'=4] {'z','x','c'}, dimensions={0} | all-to-all | bytes 393216 | tf_op jit(solution)/shard_map/all_to_all | solution.py:131
  157.4 0.8 reshape.50
  (22 shorter events, 0.3 us)
Async XLA Ops:
  0.0 14.6 %copy-start = (bf16[384,1024]{1,0:T(8,128)(2,1)S(1)}, bf16[384,1024]{1,0:T(8,128)(2,1)}, u32[]{:S(2)}) copy-start(bf16[384,1024]{1,0:T(8,128)(2,1)} %param.14) | copy-start | bytes 2359300
  0.0 1.1 copy-start.1
  1.1 1.0 copy-start.2
  2.3 12.4 %copy-start.7 = (f32[1024]{0:T(1024)S(1)}, f32[1024]{0:T(1024)}, u32[]{:S(2)}) copy-start(f32[1024]{0:T(1024)} %param.15) | copy-start | bytes 12292
  2.3 12.4 %copy-start.9 = (f32[384]{0:T(512)S(1)}, f32[384]{0:T(512)}, u32[]{:S(2)}) copy-start(f32[384]{0:T(512)} %param.13) | copy-start | bytes 4612
  16.4 1.7 %copy-start.3 = (s32[2,128]{1,0:T(2,128)S(1)}, s32[2,128]{1,0:T(2,128)}, u32[]{:S(2)}) copy-start(s32[2,128]{1,0:T(2,128)} %param.12) | copy-start | bytes 3076
  18.1 1.0 copy-start.4
  18.1 1.1 copy-start.5
  18.1 1.2 copy-start.6
  18.1 1.2 copy-start.8

commit v13 on v12

--- a/solution.py
+++ b/solution.py
@@ -162,6 +162,7 @@
     picked = obs_pick.shape[1]
     own = lane_rows(member_params).reshape(-1, features)
     weights = lax.all_gather(own, "r", axis=0, tiled=True)
+    weights, states = lax.optimization_barrier((weights, states))
     step_scale = DT * width ** (-0.5)
     current = states.astype(jnp.float32)
     for _ in range(2):

time: 159 us -> 159 us (level)
  no operation moved by 1% of the time
where the time goes in v13:
time: 159 us; the launch traced here: 158 us
  blocking collectives  140 us (88%)
  matrix products  7.12 us (4%)
  Pallas kernels  4.94 us (3%)
  local copies, waits for them, and re-layouts  3.85 us (2%)
    all_to_all x5, blocking collectives, exchange(): return lax.all_to_all(value, axes, split_axis=0, concat_axis=0, tiled=True)  128 us
    all_gather x1, blocking collectives, on_device(): weights = lax.all_gather(own, 'r', axis=0, tiled=True)  12.2 us
    pallas_call x1, Pallas kernels, centred_coefficients(): pl.pallas_call(solve_kernel, out_shape=jax.ShapeDtypeStruct((n, n), jnp.f...  4.91 us
    dot_general x2, matrix products, on_device(): jnp.dot(layer, weights, preferred_element_type=jnp.float32)  3.38 us

profile of v13, /device:TPU:1, one launch (start us, length us, event | category | flops | bytes accessed | tf_op | source)
XLA Modules:
  0.0 157.8 jit_solution(13935736690783990862)
XLA Ops:
  0.0 1.1 copy-done.1
  1.1 0.0 copy-start.2
  1.1 0.1 reshape.45
  1.2 12.2 %all_gather.3 = bf16[1024,384]{1,0:T(8,128)(2,1)S(1)} all-gather(bf16[256,384]{1,0:T(8,128)(2,1)S(1)} %reshape.45), channel_id=1, replica_groups=mesh['x'=4,'z'=16,'c'=2,'r'=4] {'r'}, dimensions={0}, use_global_device_ids=true | all-gather | bytes 983040 | tf_op jit(solution)/shard_map/all_gather | solution.py:164
  13.5 0.2 copy.30
  13.7 0.1 fusion.30
  13.8 0.4 copy-done.7
  14.1 0.0 copy-done.9
  14.2 1.7 %multiply_reduce_fusion = (f32[512]{0:T(512)S(1)}, f32[512,384]{0,1:T(8,128)S(1)}) fusion(bf16[1024,384]{1,0:T(8,128)(2,1)S(1)} %all_gather.3, bf16[384,1024]{1,0:T(8,128)(2,1)S(1)} %copy-done, f32[1024]{0:T(1024)S(1)} %copy-done.7, bf16[512,384]{0,1:T(8,128)(2,1)S(1)} %copy.30, f32[384]{0:T(512)S(1)} %copy-done.9, f32[512]{0:T(512)S(1)} %add_rsqrt_fusion.1), kind=kOutput, calls=%fused_computation.43 | convolution fusion | flops 812318208 | bytes 2762240 | tf_op jit(solution)/shard_map/dot_general | solution.py:170
  15.9 0.0 copy-start.3
  15.9 1.7 %fusion.19 = f32[512,384,1]{0,1,2:T(8,128)S(1)} fusion(f32[512,384]{0,1:T(8,128)S(1)} %get-tuple-element.19, bf16[1024,384]{1,0:T(8,128)(2,1)S(1)} %all_gather.3, bf16[384,1024]{1,0:T(8,128)(2,1)S(1)} %copy-done, f32[1024]{0:T(1024)S(1)} %copy-done.7, f32[512]{0:T(512)S(1)} %add_rsqrt_fusion, f32[384]{0:T(512)S(1)} %copy-done.9), kind=kOutput, calls=%fused_computation.24 | convolution fusion | flops 811532288 | bytes 3153408 | tf_op jit(solution)/shard_map/dot_general | solution.py:170
  17.6 0.0 copy-start.4
  17.6 0.0 copy-start.5
  17.6 0.0 copy-start.6
  17.6 0.7 fusion.48
  18.3 0.3 copy-done.4
  18.6 0.1 copy-done.5
  18.7 0.1 copy-done.6
  18.8 1.8 %multiply_reduce_fusion.1 = (f32[]{:T(128)}, bf16[2,512,128]{2,1,0:T(8,128)(2,1)S(1)}, bf16[2,512,128]{2,1,0:T(8,128)(2,1)S(1)}) fusion(bf16[1,2,512,128]{3,2,1,0:T(8,128)(2,1)S(1)} %copy-done.5, f32[2,512,128]{2,1,0:T(8,128)S(1)} %copy-done.4, bf16[2,512,128]{2,1,0:T(8,128)(2,1)S(1)} %copy-done.6, f32[2,128,512]{2,1,0:T(8,128)S(1)} %fusion.48, ...), kind=kOutput, calls=%fused_computation.51 | convolution fusion | flops 807272448 | bytes 2101252 | tf_op jit(solution)/shard_map/kib,kbf->kif/dot_general | solution.py:176
  20.5 1.0 pad_maximum_fusion
  21.6 60.8 %all_to_all.25 = bf16[128,11,2,128]{3,2,1,0:T(2,128)(2,1)S(1)} all-to-all(bf16[128,11,2,128]{3,2,1,0:T(2,128)(2,1)S(1)} %pad_maximum_fusion), channel_id=1, replica_groups=mesh['x'=4,'z'=16,'c'=2,'r'=4] {'z','x','c'}, dimensions={0} | all-to-all | bytes 1441792 | tf_op jit(solution)/shard_map/all_to_all | solution.py:131
  82.3 0.4 fusion.61
  82.7 0.1 slice.12
  83.1 0.9 fusion.23
  84.0 16.9 %all_to_all.26 = f32[32,8,128]{2,1,0:T(8,128)S(1)} all-to-all(f32[32,8,128]{2,1,0:T(8,128)S(1)} %fusion.23), channel_id=1, replica_groups=mesh['x'=4,'z'=16,'c'=2,'r'=4] {'x','c','r'}, dimensions={0} | all-to-all | bytes 262144 | tf_op jit(solution)/shard_map/all_to_all | solution.py:131
  101.0 14.3 %all_to_all.27 = f32[16,8,128]{2,1,0:T(8,128)S(1)} all-to-all(f32[16,8,128]{2,1,0:T(8,128)S(1)} %broadcast_in_dim.14), channel_id=1, replica_groups=mesh['x'=4,'z'=16,'c'=2,'r'=4] {'z'}, dimensions={0} | all-to-all | bytes 131072 | tf_op jit(solution)/shard_map/all_to_all | solution.py:131
  115.3 12.9 %all_to_all.28 = f32[32,8,128]{2,1,0:T(8,128)S(1)} all-to-all(f32[32,8,128]{2,1,0:T(8,128)S(1)} %broadcast_in_dim.15), channel_id=1, replica_groups=mesh['x'=4,'z'=16,'c'=2,'r'=4] {'x','c','r'}, dimensions={0} | all-to-all | bytes 262144 | tf_op jit(solution)/shard_map/all_to_all | solution.py:131
  128.2 4.9 %shard_map.101 = f32[128,128]{1,0:T(8,128)S(1)} custom-call(f32[256,128]{1,0:T(8,128)S(1)} %bitcast.32), custom_call_target="tpu_custom_call" | custom-call | flops 40000000 | bytes 200000 | tf_op jit(solution)/shard_map/pallas_call | solution.py:109
  133.1 0.4 fusion.21
  133.5 0.2 copy.37
  133.7 23.3 %all_to_all.29 = bf16[128,3,2,128]{3,2,1,0:T(2,128)(2,1)S(1)} all-to-all(bf16[128,3,2,128]{3,2,1,0:T(2,128)(2,1)S(1)} %copy.37), channel_id=1, replica_groups=mesh['x'=4,'z'=16,'c'=2,'r'=4] {'z','x','c'}, dimensions={0} | all-to-all | bytes 393216 | tf_op jit(solution)/shard_map/all_to_all | solution.py:131
  156.9 0.8 reshape.50
  (22 shorter events, 0.3 us)
Async XLA Ops:
  0.0 13.8 %copy-start = (bf16[384,1024]{1,0:T(8,128)(2,1)S(1)}, bf16[384,1024]{1,0:T(8,128)(2,1)}, u32[]{:S(2)}) copy-start(bf16[384,1024]{1,0:T(8,128)(2,1)} %param.14) | copy-start | bytes 2359300
  0.0 1.1 copy-start.1
  1.1 12.3 %copy-start.2 = (bf16[512,384]{1,0:T(8,128)(2,1)S(1)}, bf16[512,384]{1,0:T(8,128)(2,1)}, u32[]{:S(2)}) copy-start(bf16[512,384]{1,0:T(8,128)(2,1)} %param.10) | copy-start | bytes 1179652
  13.5 0.7 copy-start.7
  13.5 0.7 copy-start.9
  15.9 1.7 %copy-start.3 = (s32[2,128]{1,0:T(2,128)S(1)}, s32[2,128]{1,0:T(2,128)}, u32[]{:S(2)}) copy-start(s32[2,128]{1,0:T(2,128)} %param.12) | copy-start | bytes 3076
  17.6 1.0 copy-start.4
  17.6 1.1 copy-start.5
  17.6 1.2 copy-start.6
  17.6 1.2 copy-start.8

commit v14 on v13

--- a/solution.py
+++ b/solution.py
@@ -10,7 +10,7 @@
 DT = 0.5
 MEM = ("z", "x", "c")
 OWNERS = ("x", "z", "c")
-NEAR = ("x", "c", "r")
+NEAR = ("x", "r", "c")
 BLOCK = 8
 LANES = 128
 HIGHEST = lax.Precision.HIGHEST

time: 159 us -> 159 us (level)
  no operation moved by 1% of the time
where the time goes in v14:
time: 159 us; the launch traced here: 158 us
  blocking collectives  140 us (88%)
  matrix products  7.12 us (4%)
  Pallas kernels  4.94 us (3%)
  local copies, waits for them, and re-layouts  3.85 us (2%)
    all_to_all x5, blocking collectives, exchange(): return lax.all_to_all(value, axes, split_axis=0, concat_axis=0, tiled=True)  128 us
    all_gather x1, blocking collectives, on_device(): weights = lax.all_gather(own, 'r', axis=0, tiled=True)  12.2 us
    pallas_call x1, Pallas kernels, centred_coefficients(): pl.pallas_call(solve_kernel, out_shape=jax.ShapeDtypeStruct((n, n), jnp.f...  4.91 us
    dot_general x2, matrix products, on_device(): jnp.dot(layer, weights, preferred_element_type=jnp.float32)  3.38 us

profile of v14, /device:TPU:1, one launch (start us, length us, event | category | flops | bytes accessed | tf_op | source)
XLA Modules:
  0.0 157.8 jit_solution(4687522103782876272)
XLA Ops:
  0.0 1.1 copy-done.1
  1.1 0.0 copy-start.2
  1.1 0.1 reshape.45
  1.2 12.2 %all_gather.3 = bf16[1024,384]{1,0:T(8,128)(2,1)S(1)} all-gather(bf16[256,384]{1,0:T(8,128)(2,1)S(1)} %reshape.45), channel_id=1, replica_groups=mesh['x'=4,'z'=16,'c'=2,'r'=4] {'r'}, dimensions={0}, use_global_device_ids=true | all-gather | bytes 983040 | tf_op jit(solution)/shard_map/all_gather | solution.py:164
  13.5 0.2 copy.30
  13.7 0.1 fusion.30
  13.8 0.4 copy-done.7
  14.1 0.0 copy-done.9
  14.2 1.7 %multiply_reduce_fusion = (f32[512]{0:T(512)S(1)}, f32[512,384]{0,1:T(8,128)S(1)}) fusion(bf16[1024,384]{1,0:T(8,128)(2,1)S(1)} %all_gather.3, bf16[384,1024]{1,0:T(8,128)(2,1)S(1)} %copy-done, f32[1024]{0:T(1024)S(1)} %copy-done.7, bf16[512,384]{0,1:T(8,128)(2,1)S(1)} %copy.30, f32[384]{0:T(512)S(1)} %copy-done.9, f32[512]{0:T(512)S(1)} %add_rsqrt_fusion.1), kind=kOutput, calls=%fused_computation.43 | convolution fusion | flops 812318208 | bytes 2762240 | tf_op jit(solution)/shard_map/dot_general | solution.py:170
  15.9 0.0 copy-start.3
  15.9 1.7 %fusion.19 = f32[512,384,1]{0,1,2:T(8,128)S(1)} fusion(f32[512,384]{0,1:T(8,128)S(1)} %get-tuple-element.19, bf16[1024,384]{1,0:T(8,128)(2,1)S(1)} %all_gather.3, bf16[384,1024]{1,0:T(8,128)(2,1)S(1)} %copy-done, f32[1024]{0:T(1024)S(1)} %copy-done.7, f32[512]{0:T(512)S(1)} %add_rsqrt_fusion, f32[384]{0:T(512)S(1)} %copy-done.9), kind=kOutput, calls=%fused_computation.24 | convolution fusion | flops 811532288 | bytes 3153408 | tf_op jit(solution)/shard_map/dot_general | solution.py:170
  17.6 0.0 copy-start.4
  17.6 0.0 copy-start.5
  17.6 0.0 copy-start.6
  17.6 0.7 fusion.48
  18.3 0.3 copy-done.4
  18.6 0.1 copy-done.5
  18.7 0.1 copy-done.6
  18.8 1.8 %multiply_reduce_fusion.1 = (f32[]{:T(128)}, bf16[2,512,128]{2,1,0:T(8,128)(2,1)S(1)}, bf16[2,512,128]{2,1,0:T(8,128)(2,1)S(1)}) fusion(bf16[1,2,512,128]{3,2,1,0:T(8,128)(2,1)S(1)} %copy-done.5, f32[2,512,128]{2,1,0:T(8,128)S(1)} %copy-done.4, bf16[2,512,128]{2,1,0:T(8,128)(2,1)S(1)} %copy-done.6, f32[2,128,512]{2,1,0:T(8,128)S(1)} %fusion.48, ...), kind=kOutput, calls=%fused_computation.51 | convolution fusion | flops 807272448 | bytes 2101252 | tf_op jit(solution)/shard_map/kib,kbf->kif/dot_general | solution.py:176
  20.5 1.0 pad_maximum_fusion
  21.6 60.8 %all_to_all.25 = bf16[128,11,2,128]{3,2,1,0:T(2,128)(2,1)S(1)} all-to-all(bf16[128,11,2,128]{3,2,1,0:T(2,128)(2,1)S(1)} %pad_maximum_fusion), channel_id=1, replica_groups=mesh['x'=4,'z'=16,'c'=2,'r'=4] {'z','x','c'}, dimensions={0} | all-to-all | bytes 1441792 | tf_op jit(solution)/shard_map/all_to_all | solution.py:131
  82.3 0.4 fusion.61
  82.7 0.1 slice.12
  83.1 0.9 fusion.23
  84.0 17.1 %all_to_all.26 = f32[32,8,128]{2,1,0:T(8,128)S(1)} all-to-all(f32[32,8,128]{2,1,0:T(8,128)S(1)} %fusion.23), channel_id=1, replica_groups=mesh['x'=4,'z'=16,'c'=2,'r'=4] {'x','r','c'}, dimensions={0} | all-to-all | bytes 262144 | tf_op jit(solution)/shard_map/all_to_all | solution.py:131
  101.1 14.3 %all_to_all.27 = f32[16,8,128]{2,1,0:T(8,128)S(1)} all-to-all(f32[16,8,128]{2,1,0:T(8,128)S(1)} %broadcast_in_dim.14), channel_id=1, replica_groups=mesh['x'=4,'z'=16,'c'=2,'r'=4] {'z'}, dimensions={0} | all-to-all | bytes 131072 | tf_op jit(solution)/shard_map/all_to_all | solution.py:131
  115.5 12.8 %all_to_all.28 = f32[32,8,128]{2,1,0:T(8,128)S(1)} all-to-all(f32[32,8,128]{2,1,0:T(8,128)S(1)} %broadcast_in_dim.15), channel_id=1, replica_groups=mesh['x'=4,'z'=16,'c'=2,'r'=4] {'x','r','c'}, dimensions={0} | all-to-all | bytes 262144 | tf_op jit(solution)/shard_map/all_to_all | solution.py:131
  128.3 4.9 %shard_map.101 = f32[128,128]{1,0:T(8,128)S(1)} custom-call(f32[256,128]{1,0:T(8,128)S(1)} %bitcast.32), custom_call_target="tpu_custom_call" | custom-call | flops 40000000 | bytes 200000 | tf_op jit(solution)/shard_map/pallas_call | solution.py:109
  133.2 0.4 fusion.21
  133.6 0.2 copy.37
  133.8 23.1 %all_to_all.29 = bf16[128,3,2,128]{3,2,1,0:T(2,128)(2,1)S(1)} all-to-all(bf16[128,3,2,128]{3,2,1,0:T(2,128)(2,1)S(1)} %copy.37), channel_id=1, replica_groups=mesh['x'=4,'z'=16,'c'=2,'r'=4] {'z','x','c'}, dimensions={0} | all-to-all | bytes 393216 | tf_op jit(solution)/shard_map/all_to_all | solution.py:131
  157.0 0.8 reshape.50
  (22 shorter events, 0.3 us)
Async XLA Ops:
  0.0 13.8 %copy-start = (bf16[384,1024]{1,0:T(8,128)(2,1)S(1)}, bf16[384,1024]{1,0:T(8,128)(2,1)}, u32[]{:S(2)}) copy-start(bf16[384,1024]{1,0:T(8,128)(2,1)} %param.14) | copy-start | bytes 2359300
  0.0 1.1 copy-start.1
  1.1 12.3 %copy-start.2 = (bf16[512,384]{1,0:T(8,128)(2,1)S(1)}, bf16[512,384]{1,0:T(8,128)(2,1)}, u32[]{:S(2)}) copy-start(bf16[512,384]{1,0:T(8,128)(2,1)} %param.10) | copy-start | bytes 1179652
  13.5 0.7 copy-start.7
  13.5 0.7 copy-start.9
  15.9 1.7 %copy-start.3 = (s32[2,128]{1,0:T(2,128)S(1)}, s32[2,128]{1,0:T(2,128)}, u32[]{:S(2)}) copy-start(s32[2,128]{1,0:T(2,128)} %param.12) | copy-start | bytes 3076
  17.6 1.0 copy-start.4
  17.6 1.1 copy-start.5
  17.6 1.2 copy-start.6
  17.6 1.2 copy-start.8

commit v15 on v13

--- a/solution.py
+++ b/solution.py
@@ -179,7 +179,10 @@
     misfit_w = (
         observed.astype(jnp.float32) * inv_sigma + perturbation[0].astype(jnp.float32) - scaled
     ).astype(jnp.bfloat16)
-    misfit_local = jnp.sum(jnp.square(misfit_w.astype(jnp.float32)))
+    misfit_lanes = jnp.sum(jnp.square(misfit_w.astype(jnp.float32)), axis=(0, 1))
+    misfit_local = jnp.dot(
+        misfit_lanes[None], jnp.ones((picked, members), jnp.float32), precision=HIGHEST
+    )
     entries = members * step_count * rows * lax.axis_size("r") * picked
     pairs = (members, -1, 2, picked)
     pairs = (members, -1, 2, picked)

time: 159 us -> 159 us (level)
  blocking collectives: 140 us -> 79.5 us
  waiting for transfers between devices: 0 us -> 38.8 us
  starting transfers between devices: 0 us -> 22 us
    all_to_all x5 -> x4, blocking collectives: 128 us -> 67.3 us  [exchange(): return lax.all_to_all(value, axes, split_axis=0, concat_axis=0, tiled=True)]
    all_to_all x0 -> x1, waiting for transfers between devices: none -> 38.8 us  [exchange(): return lax.all_to_all(value, axes, split_axis=0, concat_axis=0, tiled=True)]
    all_to_all x0 -> x1, starting transfers between devices: none -> 22 us  [exchange(): return lax.all_to_all(value, axes, split_axis=0, concat_axis=0, tiled=True)]
  transfers between devices with their start and end apart: 0 -> 1, of which waited for: 0 -> 1; matrix products, arithmetic and copies ran while one was open for 0% -> 0% of each run, Pallas kernels for 0% -> 0%
where the time goes in v15:
time: 159 us; the launch traced here: 158 us
  blocking collectives  79.5 us (50%)
  waiting for transfers between devices  38.8 us (24%)
  starting transfers between devices  22 us (14%)
  matrix products  6.02 us (4%)
  Pallas kernels  4.94 us (3%)
  local copies, waits for them, and re-layouts  3.85 us (2%)
  other arithmetic  2.2 us (1%)
    all_to_all x4, blocking collectives, exchange(): return lax.all_to_all(value, axes, split_axis=0, concat_axis=0, tiled=True)  67.3 us
    all_to_all x1, waiting for transfers between devices, exchange(): return lax.all_to_all(value, axes, split_axis=0, concat_axis=0, tiled=True)  38.8 us
    all_to_all x1, starting transfers between devices, exchange(): return lax.all_to_all(value, axes, split_axis=0, concat_axis=0, tiled=True)  22 us
    all_gather x1, blocking collectives, on_device(): weights = lax.all_gather(own, 'r', axis=0, tiled=True)  12.2 us
    pallas_call x1, Pallas kernels, centred_coefficients(): pl.pallas_call(solve_kernel, out_shape=jax.ShapeDtypeStruct((n, n), jnp.f...  4.91 us
    dot_general x2, matrix products, on_device(): jnp.dot(layer, weights, preferred_element_type=jnp.float32)  3.38 us
  transfers between devices with their start and end apart: 1, of which 1 were waited for; matrix products, arithmetic and copies ran while one was open for 0% of the time, Pallas kernels for 0%

profile of v15, /device:TPU:1, one launch (start us, length us, event | category | flops | bytes accessed | tf_op | source)
XLA Modules:
  0.0 157.6 jit_solution(17425321971376171912)
XLA Ops:
  0.0 1.1 copy-done.1
  1.1 0.1 reshape.49
  1.2 12.2 %all_gather.3 = bf16[1024,384]{1,0:T(8,128)(2,1)S(1)} all-gather(bf16[256,384]{1,0:T(8,128)(2,1)S(1)} %reshape.49), channel_id=1, replica_groups=mesh['x'=4,'z'=16,'c'=2,'r'=4] {'r'}, dimensions={0}, use_global_device_ids=true | all-gather | bytes 983040 | tf_op jit(solution)/shard_map/all_gather | solution.py:164
  13.5 0.2 copy.30
  13.7 0.1 fusion.30
  13.8 0.4 copy-done.7
  14.1 0.0 copy-done.9
  14.2 1.7 %multiply_reduce_fusion = (f32[512]{0:T(512)S(1)}, f32[512,384]{0,1:T(8,128)S(1)}) fusion(bf16[1024,384]{1,0:T(8,128)(2,1)S(1)} %all_gather.3, bf16[384,1024]{1,0:T(8,128)(2,1)S(1)} %copy-done, f32[1024]{0:T(1024)S(1)} %copy-done.7, bf16[512,384]{0,1:T(8,128)(2,1)S(1)} %copy.30, f32[384]{0:T(512)S(1)} %copy-done.9, f32[512]{0:T(512)S(1)} %add_rsqrt_fusion.1), kind=kOutput, calls=%fused_computation.44 | convolution fusion | flops 812318208 | bytes 2762240 | tf_op jit(solution)/shard_map/dot_general | solution.py:170
  15.9 0.0 copy-start.3
  15.9 1.7 %fusion.19 = f32[512,384,1]{0,1,2:T(8,128)S(1)} fusion(f32[512,384]{0,1:T(8,128)S(1)} %get-tuple-element.19, bf16[1024,384]{1,0:T(8,128)(2,1)S(1)} %all_gather.3, bf16[384,1024]{1,0:T(8,128)(2,1)S(1)} %copy-done, f32[1024]{0:T(1024)S(1)} %copy-done.7, f32[512]{0:T(512)S(1)} %add_rsqrt_fusion, f32[384]{0:T(512)S(1)} %copy-done.9), kind=kOutput, calls=%fused_computation.24 | convolution fusion | flops 811532288 | bytes 3153408 | tf_op jit(solution)/shard_map/dot_general | solution.py:170
  17.6 0.0 copy-start.5
  17.6 0.0 copy-start.6
  17.6 0.7 fusion.48
  18.3 0.3 copy-done.4
  18.6 0.1 copy-done.5
  18.7 0.1 copy-done.6
  18.8 1.2 multiply_reduce_fusion.1
  20.0 1.9 %pad_maximum_fusion = bf16[128,11,2,128]{3,2,1,0:T(2,128)(2,1)} fusion(bf16[128,3,2,128]{3,2,1,0:T(2,128)(2,1)S(1)} %bitcast.36, bf16[128,4,2,128]{3,2,1,0:T(2,128)(2,1)S(1)} %bitcast.38, bf16[128,4,2,128]{3,2,1,0:T(2,128)(2,1)S(1)} %bitcast.39), kind=kLoop, calls=%fused_computation.45 | loop fusion | flops 720896 | bytes 1441792 | tf_op jit(solution)/shard_map/concatenate | solution.py:191
  21.8 22.0 %all-to-all-start = ((bf16[128,11,2,128]{3,2,1,0:T(2,128)(2,1)}), bf16[128,11,2,128]{3,2,1,0:T(2,128)(2,1)S(1)}, u32[]{:S(2)}, u32[]{:S(2)}) async-start(bf16[128,11,2,128]{3,2,1,0:T(2,128)(2,1)} %pad_maximum_fusion), calls=%async_computation | async-start | bytes 1441792 | tf_op jit(solution)/shard_map/all_to_all | solution.py:131
  43.9 0.1 convolution_bitcast_fusion.1
  44.0 38.8 %all-to-all-done = bf16[128,11,2,128]{3,2,1,0:T(2,128)(2,1)S(1)} async-done(((bf16[128,11,2,128]{3,2,1,0:T(2,128)(2,1)}), bf16[128,11,2,128]{3,2,1,0:T(2,128)(2,1)S(1)}, u32[]{:S(2)}, u32[]{:S(2)}) %all-to-all-start) | async-done | bytes 720928 | tf_op jit(solution)/shard_map/all_to_all | solution.py:131
  82.8 0.4 fusion.64
  83.2 0.1 slice.12
  83.6 0.3 fusion.23
  83.9 16.9 %all_to_all.25 = f32[32,8,128]{2,1,0:T(8,128)S(1)} all-to-all(f32[32,8,128]{2,1,0:T(8,128)S(1)} %fusion.23), channel_id=1, replica_groups=mesh['x'=4,'z'=16,'c'=2,'r'=4] {'x','c','r'}, dimensions={0} | all-to-all | bytes 262144 | tf_op jit(solution)/shard_map/all_to_all | solution.py:131
  100.8 14.3 %all_to_all.26 = f32[16,8,128]{2,1,0:T(8,128)S(1)} all-to-all(f32[16,8,128]{2,1,0:T(8,128)S(1)} %broadcast_in_dim.17), channel_id=1, replica_groups=mesh['x'=4,'z'=16,'c'=2,'r'=4] {'z'}, dimensions={0} | all-to-all | bytes 131072 | tf_op jit(solution)/shard_map/all_to_all | solution.py:131
  115.1 12.9 %all_to_all.27 = f32[32,8,128]{2,1,0:T(8,128)S(1)} all-to-all(f32[32,8,128]{2,1,0:T(8,128)S(1)} %broadcast_in_dim.18), channel_id=1, replica_groups=mesh['x'=4,'z'=16,'c'=2,'r'=4] {'x','c','r'}, dimensions={0} | all-to-all | bytes 262144 | tf_op jit(solution)/shard_map/all_to_all | solution.py:131
  128.0 4.9 %shard_map.101 = f32[128,128]{1,0:T(8,128)S(1)} custom-call(f32[256,128]{1,0:T(8,128)S(1)} %bitcast.37), custom_call_target="tpu_custom_call" | custom-call | flops 40000000 | bytes 200000 | tf_op jit(solution)/shard_map/pallas_call | solution.py:109
  132.9 0.4 fusion.21
  133.3 0.2 copy.37
  133.5 23.3 %all_to_all.28 = bf16[128,3,2,128]{3,2,1,0:T(2,128)(2,1)S(1)} all-to-all(bf16[128,3,2,128]{3,2,1,0:T(2,128)(2,1)S(1)} %copy.37), channel_id=1, replica_groups=mesh['x'=4,'z'=16,'c'=2,'r'=4] {'z','x','c'}, dimensions={0} | all-to-all | bytes 393216 | tf_op jit(solution)/shard_map/all_to_all | solution.py:131
  156.8 0.8 reshape.54
  (24 shorter events, 0.3 us)
Async XLA Ops:
  0.0 13.8 %copy-start = (bf16[384,1024]{1,0:T(8,128)(2,1)S(1)}, bf16[384,1024]{1,0:T(8,128)(2,1)}, u32[]{:S(2)}) copy-start(bf16[384,1024]{1,0:T(8,128)(2,1)} %param.14) | copy-start | bytes 2359300
  0.0 1.1 copy-start.1
  1.1 12.3 %copy-start.2 = (bf16[512,384]{1,0:T(8,128)(2,1)S(1)}, bf16[512,384]{1,0:T(8,128)(2,1)}, u32[]{:S(2)}) copy-start(bf16[512,384]{1,0:T(8,128)(2,1)} %param.10) | copy-start | bytes 1179652
  13.5 0.7 copy-start.7
  13.5 0.7 copy-start.9
  15.9 1.7 %copy-start.3 = (s32[2,128]{1,0:T(2,128)S(1)}, s32[2,128]{1,0:T(2,128)}, u32[]{:S(2)}) copy-start(s32[2,128]{1,0:T(2,128)} %param.12) | copy-start | bytes 3076
  17.6 1.0 copy-start.4
  17.6 1.1 copy-start.5
  17.6 1.2 copy-start.6
  17.6 1.2 copy-start.8
  21.8 61.0 %all-to-all-start = ((bf16[128,11,2,128]{3,2,1,0:T(2,128)(2,1)}), bf16[128,11,2,128]{3,2,1,0:T(2,128)(2,1)S(1)}, u32[]{:S(2)}, u32[]{:S(2)}) async-start(bf16[128,11,2,128]{3,2,1,0:T(2,128)(2,1)} %pad_maximum_fusion), calls=%async_computation | async-start | bytes 1441792 | tf_op jit(solution)/shard_map/all_to_all | solution.py:131

commit v16 on v15

--- a/solution.py
+++ b/solution.py
@@ -188,7 +188,8 @@
     pairs = (members, -1, 2, picked)
     sent = [weighted.reshape(pairs), misfit_w.reshape(pairs), own.reshape(pairs)]
     depth = sent[0].shape[1]
-    arrived = exchange(jnp.concatenate(sent, axis=1), MEM)
+    sent, misfit_local = lax.optimization_barrier((jnp.concatenate(sent, axis=1), misfit_local))
+    arrived = exchange(sent, MEM)
     gathered = arrived[:, :depth].astype(jnp.float32)
     misfit_here = arrived[:, depth : 2 * depth]
     param_block = arrived[:, 2 * depth :]

time: 159 us -> 158 us (level)
  blocking collectives: 79.5 us -> 140 us
  waiting for transfers between devices: 38.8 us -> 0 us
  starting transfers between devices: 22 us -> 0 us
    all_to_all x4 -> x5, blocking collectives: 67.3 us -> 128 us  [exchange(): return lax.all_to_all(value, axes, split_axis=0, concat_axis=0, tiled=True)]
    all_to_all x1 -> x0, waiting for transfers between devices: 38.8 us -> none  [exchange(): return lax.all_to_all(value, axes, split_axis=0, concat_axis=0, tiled=True)]
    all_to_all x1 -> x0, starting transfers between devices: 22 us -> none  [exchange(): return lax.all_to_all(value, axes, split_axis=0, concat_axis=0, tiled=True)]
  transfers between devices with their start and end apart: 1 -> 0, of which waited for: 1 -> 0; matrix products, arithmetic and copies ran while one was open for 0% -> 0% of each run, Pallas kernels for 0% -> 0%
where the time goes in v16:
time: 158 us; the launch traced here: 157 us
  blocking collectives  140 us (89%)
  matrix products  6.03 us (4%)
  Pallas kernels  4.94 us (3%)
  local copies, waits for them, and re-layouts  3.85 us (2%)
    all_to_all x5, blocking collectives, exchange(): return lax.all_to_all(value, axes, split_axis=0, concat_axis=0, tiled=True)  128 us
    all_gather x1, blocking collectives, on_device(): weights = lax.all_gather(own, 'r', axis=0, tiled=True)  12.2 us
    pallas_call x1, Pallas kernels, centred_coefficients(): pl.pallas_call(solve_kernel, out_shape=jax.ShapeDtypeStruct((n, n), jnp.f...  4.91 us
    dot_general x2, matrix products, on_device(): jnp.dot(layer, weights, preferred_element_type=jnp.float32)  3.38 us

profile of v16, /device:TPU:1, one launch (start us, length us, event | category | flops | bytes accessed | tf_op | source)
XLA Modules:
  0.0 156.7 jit_solution(4008088879552642934)
XLA Ops:
  0.0 1.1 copy-done.1
  1.1 0.0 copy-start.2
  1.1 0.1 reshape.48
  1.2 12.2 %all_gather.3 = bf16[1024,384]{1,0:T(8,128)(2,1)S(1)} all-gather(bf16[256,384]{1,0:T(8,128)(2,1)S(1)} %reshape.48), channel_id=1, replica_groups=mesh['x'=4,'z'=16,'c'=2,'r'=4] {'r'}, dimensions={0}, use_global_device_ids=true | all-gather | bytes 983040 | tf_op jit(solution)/shard_map/all_gather | solution.py:164
  13.5 0.2 copy.30
  13.7 0.1 fusion.30
  13.8 0.4 copy-done.7
  14.1 0.0 copy-done.9
  14.2 1.7 %multiply_reduce_fusion = (f32[512]{0:T(512)S(1)}, f32[512,384]{0,1:T(8,128)S(1)}) fusion(bf16[1024,384]{1,0:T(8,128)(2,1)S(1)} %all_gather.3, bf16[384,1024]{1,0:T(8,128)(2,1)S(1)} %copy-done, f32[1024]{0:T(1024)S(1)} %copy-done.7, bf16[512,384]{0,1:T(8,128)(2,1)S(1)} %copy.30, f32[384]{0:T(512)S(1)} %copy-done.9, f32[512]{0:T(512)S(1)} %add_rsqrt_fusion.1), kind=kOutput, calls=%fused_computation.43 | convolution fusion | flops 812318208 | bytes 2762240 | tf_op jit(solution)/shard_map/dot_general | solution.py:170
  15.9 0.0 copy-start.3
  15.9 1.7 %fusion.19 = f32[512,384,1]{0,1,2:T(8,128)S(1)} fusion(f32[512,384]{0,1:T(8,128)S(1)} %get-tuple-element.23, bf16[1024,384]{1,0:T(8,128)(2,1)S(1)} %all_gather.3, bf16[384,1024]{1,0:T(8,128)(2,1)S(1)} %copy-done, f32[1024]{0:T(1024)S(1)} %copy-done.7, f32[512]{0:T(512)S(1)} %add_rsqrt_fusion, f32[384]{0:T(512)S(1)} %copy-done.9), kind=kOutput, calls=%fused_computation.24 | convolution fusion | flops 811532288 | bytes 3153408 | tf_op jit(solution)/shard_map/dot_general | solution.py:170
  17.6 0.0 copy-start.4
  17.6 0.0 copy-start.5
  17.6 0.7 fusion.48
  18.3 0.3 copy-done.4
  18.6 0.1 copy-done.5
  18.7 0.1 copy-done.6
  18.8 1.2 multiply_reduce_fusion.1
  20.0 0.1 fusion.51
  20.1 1.1 pad_maximum_fusion
  21.1 60.8 %all_to_all.25 = bf16[128,11,2,128]{3,2,1,0:T(2,128)(2,1)S(1)} all-to-all(bf16[128,11,2,128]{3,2,1,0:T(2,128)(2,1)S(1)} %pad_maximum_fusion), channel_id=1, replica_groups=mesh['x'=4,'z'=16,'c'=2,'r'=4] {'z','x','c'}, dimensions={0} | all-to-all | bytes 1441792 | tf_op jit(solution)/shard_map/all_to_all | solution.py:131
  81.9 0.4 fusion.65
  82.3 0.1 slice.12
  82.7 0.3 fusion.23
  83.0 16.9 %all_to_all.26 = f32[32,8,128]{2,1,0:T(8,128)S(1)} all-to-all(f32[32,8,128]{2,1,0:T(8,128)S(1)} %fusion.23), channel_id=1, replica_groups=mesh['x'=4,'z'=16,'c'=2,'r'=4] {'x','c','r'}, dimensions={0} | all-to-all | bytes 262144 | tf_op jit(solution)/shard_map/all_to_all | solution.py:131
  99.9 14.3 %all_to_all.27 = f32[16,8,128]{2,1,0:T(8,128)S(1)} all-to-all(f32[16,8,128]{2,1,0:T(8,128)S(1)} %broadcast_in_dim.17), channel_id=1, replica_groups=mesh['x'=4,'z'=16,'c'=2,'r'=4] {'z'}, dimensions={0} | all-to-all | bytes 131072 | tf_op jit(solution)/shard_map/all_to_all | solution.py:131
  114.2 12.9 %all_to_all.28 = f32[32,8,128]{2,1,0:T(8,128)S(1)} all-to-all(f32[32,8,128]{2,1,0:T(8,128)S(1)} %broadcast_in_dim.18), channel_id=1, replica_groups=mesh['x'=4,'z'=16,'c'=2,'r'=4] {'x','c','r'}, dimensions={0} | all-to-all | bytes 262144 | tf_op jit(solution)/shard_map/all_to_all | solution.py:131
  127.1 4.9 %shard_map.101 = f32[128,128]{1,0:T(8,128)S(1)} custom-call(f32[256,128]{1,0:T(8,128)S(1)} %bitcast.37), custom_call_target="tpu_custom_call" | custom-call | flops 40000000 | bytes 200000 | tf_op jit(solution)/shard_map/pallas_call | solution.py:109
  132.0 0.4 fusion.21
  132.4 0.2 copy.37
  132.6 23.3 %all_to_all.29 = bf16[128,3,2,128]{3,2,1,0:T(2,128)(2,1)S(1)} all-to-all(bf16[128,3,2,128]{3,2,1,0:T(2,128)(2,1)S(1)} %copy.37), channel_id=1, replica_groups=mesh['x'=4,'z'=16,'c'=2,'r'=4] {'z','x','c'}, dimensions={0} | all-to-all | bytes 393216 | tf_op jit(solution)/shard_map/all_to_all | solution.py:131
  155.9 0.8 reshape.53
  (23 shorter events, 0.3 us)
Async XLA Ops:
  0.0 13.8 %copy-start = (bf16[384,1024]{1,0:T(8,128)(2,1)S(1)}, bf16[384,1024]{1,0:T(8,128)(2,1)}, u32[]{:S(2)}) copy-start(bf16[384,1024]{1,0:T(8,128)(2,1)} %param.14) | copy-start | bytes 2359300
  0.0 1.1 copy-start.1
  1.1 12.3 %copy-start.2 = (bf16[512,384]{1,0:T(8,128)(2,1)S(1)}, bf16[512,384]{1,0:T(8,128)(2,1)}, u32[]{:S(2)}) copy-start(bf16[512,384]{1,0:T(8,128)(2,1)} %param.10) | copy-start | bytes 1179652
  13.5 0.7 copy-start.7
  13.5 0.7 copy-start.9
  15.9 1.7 %copy-start.3 = (s32[2,128]{1,0:T(2,128)S(1)}, s32[2,128]{1,0:T(2,128)}, u32[]{:S(2)}) copy-start(s32[2,128]{1,0:T(2,128)} %param.12) | copy-start | bytes 3076
  17.6 1.0 copy-start.4
  17.6 1.1 copy-start.5
  17.6 1.2 copy-start.6
  17.6 1.2 copy-start.8
